TPU v7x, 32 devices: a whole 2x2x4 slice. The times are simulated.
32 devices in a mesh: member: 4 (over x, core), slab: 8 (over z, y).
Axes of the slice: x: 2, y: 2, z: 4, core: 2. Of those that a mesh axis runs over, the one named last changes fastest.
Arguments:
- ocean_state: float32 [8, 4, 16, 256, 256], P('member', None, 'slab'), may hold values from -6 to 6
- diffusivity: float32 [8, 16, 256, 256], P('member', None, 'slab'), may hold values from 5 to 100
- bottom_drag: float32 [8, 256, 256], P('member', 'slab'), may hold values from 0.5 to 5
- surface_forcing: float32 [2, 3, 256, 256], P(None, None, 'slab', 'member'), may hold values from -6 to 6
- land_sea: int32 [8, 256, 256], P('member'), may hold values 0 or 1
- bottom_level: int32 [8, 256, 256], P('member'), may hold values from 1 to 16
Outputs:
- state_out: float32 [8, 4, 16, 256, 256], P('member', None, 'slab')
Inputs may be any that keep to these rules, and one draw needn't show every extreme that they name: `bottom_level`: levels at and below this count are rock.
All inputs are finite; a program needn't handle non-finite values. No bound on the sum of `land_sea` on one device may be relied on, other than what follows from the above.
Results may differ from a plain program's by a relative error of at most 0.0003.
Values sent between devices are 32-bit elements; how exact they have to be, the bound alone decides.
No kernel may reach another device: no remote copies, remote signals or barrier semaphores. Data moves between devices by JAX's collectives and lax.ppermute only.
A program may use at most 128 MiB of HBM per device.

v0:
```python
import jax
import jax.numpy as jnp
from jax import lax
from jax.sharding import PartitionSpec as P

STEPS = 2


COURANT = 0.2


def wrap_rows(values):
    return jnp.concatenate([values[..., -1:, :], values, values[..., :1, :]], axis=-2)


def wet_cells(land_rows, bottom_rows, level_ids):
    deeper = level_ids[None, :, None, None] < bottom_rows[:, None, :, :]
    ocean = land_rows[:, None, :, :] == 1
    return jnp.where(ocean & deeper, 1.0, 0.0).astype(jnp.float32)


def advect_tracers(tracer_pad, zonal_pad, merid_mid, wet_pad):
    wet_mid = wet_pad[..., 1:-1, :]
    tracer_mid = tracer_pad[..., 1:-1, :]
    face_zonal = (
        0.5
        * (zonal_pad[..., :-1, :] + zonal_pad[..., 1:, :])
        * (wet_pad[..., :-1, :] * wet_pad[..., 1:, :])
    )
    flux_zonal = face_zonal * (0.5 * (tracer_pad[..., :-1, :] + tracer_pad[..., 1:, :]))
    spread_zonal = flux_zonal[..., 1:, :] - flux_zonal[..., :-1, :]
    face_merid = (
        0.5 * (merid_mid[..., :-1] + merid_mid[..., 1:]) * (wet_mid[..., :-1] * wet_mid[..., 1:])
    )
    flux_merid = face_merid * (0.5 * (tracer_mid[..., :-1] + tracer_mid[..., 1:]))
    walls = jnp.zeros(flux_merid.shape[:-1] + (1,), jnp.float32)
    flux_merid = jnp.concatenate([walls, flux_merid, walls], axis=-1)
    spread_merid = flux_merid[..., 1:] - flux_merid[..., :-1]
    return (tracer_mid - COURANT * (spread_zonal + spread_merid)) * wet_mid


def advance(state_pad, wet_pad):
    wet_wide = wet_pad[:, None]
    tracers = advect_tracers(
        state_pad[:, 0:2], state_pad[:, 2:3], state_pad[:, 3:4, :, 1:-1, :], wet_wide
    )
    currents = state_pad[:, 2:4, :, 1:-1, :] * wet_wide[..., 1:-1, :]
    return jnp.concatenate([tracers, currents], axis=1)


def mix_columns(columns, diffusivity, bottom_drag, forcing_now, land_rows, bottom_rows, level_ids):
    wet_now = wet_cells(land_rows, bottom_rows, level_ids)
    coupling = diffusivity[:, :-1] * (wet_now[:, :-1] * wet_now[:, 1:])
    edge_zero = jnp.zeros_like(coupling[:, :1])
    rate_above = jnp.concatenate([edge_zero, coupling], axis=1)
    rate_below = jnp.concatenate([coupling, edge_zero], axis=1)
    floor_cells = jnp.where(
        (level_ids[None, :, None, None] == bottom_rows[:, None, :, :] - 1)
        & (land_rows[:, None, :, :] == 1),
        1.0,
        0.0,
    ).astype(jnp.float32)
    diagonal_base = 1.0 + rate_above + rate_below
    diagonal_drag = diagonal_base + bottom_drag[:, None] * floor_cells
    diagonal_all = jnp.stack([diagonal_base, diagonal_base, diagonal_drag, diagonal_drag], axis=1)
    surface_wet = wet_now[:, 0]
    forcing_terms = jnp.stack(
        [
            forcing_now[0] * surface_wet,
            jnp.zeros_like(surface_wet),
            forcing_now[1] * surface_wet,
            forcing_now[2] * surface_wet,
        ],
        axis=1,
    )
    right_side = columns.at[:, :, 0].add(forcing_terms)
    lower_band = jnp.moveaxis(-rate_above[:, None], 2, 0)
    upper_band = jnp.moveaxis(-rate_below[:, None], 2, 0)
    diagonal_lev = jnp.moveaxis(diagonal_all, 2, 0)
    right_lev = jnp.moveaxis(right_side, 2, 0)
    start_zero = jnp.zeros(right_lev.shape[1:], jnp.float32)

    def eliminate(previous, level_row):
        prior_upper, prior_right = previous
        lower_row, upper_row, diagonal_row, right_row = level_row
        denominator = diagonal_row - lower_row * prior_upper
        upper_new = upper_row / denominator
        right_new = (right_row - lower_row * prior_right) / denominator
        return ((upper_new, right_new), (upper_new, right_new))

    _, (upper_mod, right_mod) = lax.scan(
        eliminate, (start_zero, start_zero), (lower_band, upper_band, diagonal_lev, right_lev)
    )

    def substitute(next_value, level_row):
        upper_row, right_row = level_row
        value_now = right_row - upper_row * next_value
        return (value_now, value_now)

    _, solved = lax.scan(substitute, start_zero, (upper_mod, right_mod), reverse=True)
    return jnp.moveaxis(solved, 0, 2)


def per_device(ocean_state, diffusivity, bottom_drag, surface_forcing, land_sea, bottom_level):
    forcing_full = lax.all_gather(surface_forcing, "member", axis=3, tiled=True)
    rows_tile = diffusivity.shape[2]
    levels_all = diffusivity.shape[1]
    row_start = lax.axis_index("slab") * rows_tile
    level_ids = jnp.arange(levels_all, dtype=jnp.int32)
    land_tile = lax.dynamic_slice_in_dim(land_sea, row_start, rows_tile, 1)
    bottom_tile = lax.dynamic_slice_in_dim(bottom_level, row_start, rows_tile, 1)
    depth_local = ocean_state.shape[2]
    local_ids = lax.axis_index("slab") * depth_local + jnp.arange(depth_local, dtype=jnp.int32)
    wet_local = wrap_rows(wet_cells(land_sea, bottom_level, local_ids))
    current = ocean_state
    for step_index in range(STEPS):
        current = advance(wrap_rows(current), wet_local)
        columns = lax.all_to_all(current, "slab", split_axis=3, concat_axis=2, tiled=True)
        columns = mix_columns(
            columns,
            diffusivity,
            bottom_drag,
            forcing_full[step_index],
            land_tile,
            bottom_tile,
            level_ids,
        )
        current = lax.all_to_all(columns, "slab", split_axis=2, concat_axis=3, tiled=True)
    return current


def solution(mesh):
    placed = (
        P("member", None, "slab", None, None),
        P("member", None, "slab", None),
        P("member", "slab", None),
        P(None, None, "slab", "member"),
        P("member", None, None),
        P("member", None, None),
    )
    return jax.shard_map(
        per_device,
        mesh=mesh,
        in_specs=placed,
        out_specs=P("member", None, "slab", None, None),
        check_vma=False,
    )
```

profile of v0, /device:TPU:0, one launch (start us, length us, event | category | flops | bytes accessed | tf_op | source)
XLA Modules:
  0.0 596.4 jit_solution(2146394213938262272)
XLA Ops:
  7.9 4.7 copy.46
  12.7 7.4 %all-to-all-start = ((f32[2,4,2,256,256]{4,1,2,0,3:T(4,128)}), f32[2,4,2,256,256]{4,1,2,0,3:T(4,128)}, u32[]{:S(2)}, u32[]{:S(2)}) async-start(f32[2,4,2,256,256]{4,1,2,0,3:T(4,128)} %copy.46), calls=%async_computation | async-start | bytes 8388608 | tf_op jit(solution)/shard_map/all_to_all | solution.py:118
  20.3 8.8 %all_gather.3 = f32[2,3,32,256]{2,0,1,3:T(2,128)S(1)} all-gather(f32[2,3,32,64]{2,0,1,3:T(2,128)S(1)} %copy.48), channel_id=1, replica_groups=mesh['member'=4,'slab'=8] {'member'}, dimensions={3}, use_global_device_ids=true | all-gather | bytes 245760 | tf_op jit(solution)/shard_map/all_gather | solution.py:105
  37.0 2.3 copy.62
  41.5 71.8 %all-to-all-done = f32[2,4,2,256,256]{4,1,2,0,3:T(4,128)} async-done(((f32[2,4,2,256,256]{4,1,2,0,3:T(4,128)}), f32[2,4,2,256,256]{4,1,2,0,3:T(4,128)}, u32[]{:S(2)}, u32[]{:S(2)}) %all-to-all-start) | async-done | bytes 4194336 | tf_op jit(solution)/shard_map/all_to_all | solution.py:118
  113.4 4.6 copy.47
  118.0 2.8 broadcast.118.clone.3
  120.9 2.5 broadcast.118.clone.4
  123.4 46.8 %while.70 = (s32[]{:T(128)}, f32[2,4,32,256]{3,2,1,0:T(8,128)S(1)}, f32[2,4,32,256]{3,2,1,0:T(8,128)S(1)}, f32[16,2,4,32,256]{4,3,2,1,0:T(8,128)}, f32[16,2,4,32...) while((s32[]{:T(128)}, f32[2,4,32,256]{3,2,1,0:T(8,128)S(1)}, ...), condition=%wide.region_1.2_spmd.clone, body=%wide.region_0.1_spmd.clone.sunk | while | flops 524291 | bytes 2491003 | solution.py:91
  170.2 2.5 broadcast.118.clone.2
  172.7 31.4 %while.71 = (s32[]{:T(128)}, f32[2,4,32,256]{3,2,1,0:T(8,128)S(1)}, f32[16,2,4,32,256]{4,3,2,1,0:T(8,128)}, f32[16,2,4,32,256]{4,3,2,1,0:T(8,128)}, f32[16,2,4,3...) while((s32[]{:T(128)}, f32[2,4,32,256]{3,2,1,0:T(8,128)S(1)}, ...), condition=%wide.region_3.4_spmd.clone, body=%wide.region_2.3_spmd.clone.sunk | while | flops 196612 | bytes 1310831 | solution.py:100
  204.1 96.9 %all_to_all.72 = f32[2,4,16,32,256]{4,3,1,0,2:T(8,128)S(1)} all-to-all(f32[2,4,16,32,256]{4,3,1,0,2:T(8,128)} %bitcast.142), channel_id=1, replica_groups=mesh['member'=4,'slab'=8] {'slab'}, dimensions={2} | all-to-all | bytes 8388608 | tf_op jit(solution)/shard_map/all_to_all | solution.py:128
  304.6 4.7 copy.56
  309.3 4.6 all-to-all-start.2
  313.9 92.2 %all-to-all-done.2 = f32[2,4,2,256,256]{4,1,2,0,3:T(4,128)} async-done(((f32[2,4,2,256,256]{4,1,2,0,3:T(4,128)}), f32[2,4,2,256,256]{4,1,2,0,3:T(4,128)}, u32[]{:S(2)}, u32[]{:S(2)}) %all-to-all-start.2) | async-done | bytes 4194336 | tf_op jit(solution)/shard_map/all_to_all | solution.py:118
  406.0 4.6 copy.57
  410.7 2.9 broadcast.118.clone
  413.6 2.5 broadcast.118.clone.1
  416.1 47.2 %while.72 = (s32[]{:T(128)}, f32[2,4,32,256]{3,2,1,0:T(8,128)S(1)}, f32[2,4,32,256]{3,2,1,0:T(8,128)S(1)}, f32[16,2,4,32,256]{4,3,2,1,0:T(8,128)}, f32[16,2,4,32...) while((s32[]{:T(128)}, f32[2,4,32,256]{3,2,1,0:T(8,128)S(1)}, ...), condition=%wide.region_5.6_spmd.clone, body=%wide.region_4.5_spmd.clone.sunk | while | flops 524291 | bytes 2491003 | solution.py:91
  419.9 2.1 bitcast_dynamic-update-slice_fusion.12
  463.3 2.5 broadcast.118
  465.9 31.3 %while.73 = (s32[]{:T(128)}, f32[2,4,32,256]{3,2,1,0:T(8,128)S(1)}, f32[16,2,4,32,256]{4,3,2,1,0:T(8,128)}, f32[16,2,4,32,256]{4,3,2,1,0:T(8,128)}, f32[16,2,4,3...) while((s32[]{:T(128)}, f32[2,4,32,256]{3,2,1,0:T(8,128)S(1)}, ...), condition=%wide.region_7.8_spmd.clone, body=%wide.region_6.7_spmd.clone.sunk | while | flops 196612 | bytes 1310831 | solution.py:100
  497.2 96.9 %all_to_all.73 = f32[2,4,16,32,256]{4,3,1,0,2:T(8,128)S(1)} all-to-all(f32[2,4,16,32,256]{4,3,1,0,2:T(8,128)} %bitcast.141), channel_id=1, replica_groups=mesh['member'=4,'slab'=8] {'slab'}, dimensions={2} | all-to-all | bytes 8388608 | tf_op jit(solution)/shard_map/all_to_all | solution.py:128
  594.1 2.3 copy.64
  (152 shorter events, 176.2 us)
Async XLA Ops:
  2.4 2.3 copy-start
  12.7 7.4 %copy-start.3 = (f32[2,3,32,64]{3,2,1,0:T(8,128)S(1)}, f32[2,3,32,64]{3,2,1,0:T(8,128)}, u32[]{:S(2)}) copy-start(f32[2,3,32,64]{3,2,1,0:T(8,128)} %param.21) | copy-start | bytes 147460
  12.7 100.7 %all-to-all-start = ((f32[2,4,2,256,256]{4,1,2,0,3:T(4,128)}), f32[2,4,2,256,256]{4,1,2,0,3:T(4,128)}, u32[]{:S(2)}, u32[]{:S(2)}) async-start(f32[2,4,2,256,256]{4,1,2,0,3:T(4,128)} %copy.46), calls=%async_computation | async-start | bytes 8388608 | tf_op jit(solution)/shard_map/all_to_all | solution.py:118
  34.4 1.4 copy-start.4
  118.0 5.4 copy-start.2
  309.3 96.8 %all-to-all-start.2 = ((f32[2,4,2,256,256]{4,1,2,0,3:T(4,128)}), f32[2,4,2,256,256]{4,1,2,0,3:T(4,128)}, u32[]{:S(2)}, u32[]{:S(2)}) async-start(f32[2,4,2,256,256]{4,1,2,0,3:T(4,128)} %copy.56), calls=%async_computation.2 | async-start | bytes 8388608 | tf_op jit(solution)/shard_map/all_to_all | solution.py:118
  410.7 5.4 copy-start.1
where the time goes:
time: 600 us; the launch traced here: 596 us
  blocking collectives  203 us (34%)
  waiting for transfers between devices  164 us (27%)
  other arithmetic  142 us (24%)
  local copies, waits for them, and re-layouts  75.5 us (13%)
  starting transfers between devices  12 us (2%)
    all_to_all x2, blocking collectives, per_device(): lax.all_to_all(columns, 'slab', split_axis=2, concat_axis=3, tiled=True)  194 us
    all_to_all x2, waiting for transfers between devices, per_device(): lax.all_to_all(current, 'slab', split_axis=3, concat_axis=2, tiled=True)  164 us
    dynamic_update_slice x64, other arithmetic, mix_columns(): lax.scan(eliminate, (start_zero, start_zero), (lower_band, upper_band, di...  128 us
    mul x32, local copies, waits for them, and re-layouts, eliminate(): denominator = diagonal_row - lower_row * prior_upper  28.2 us
    another operation x6, local copies, waits for them, and re-layouts  15.8 us
  transfers between devices with their start and end apart: 2, of which 2 were waited for; matrix products, arithmetic and copies ran while one was open for 2% of the time, Pallas kernels for 0%

commit v1 on v0

v1 whole, which is shorter than its diff:
```python
import functools

import jax
import jax.numpy as jnp
from jax import lax
from jax.experimental import pallas as pl
from jax.experimental.pallas import tpu as pltpu
from jax.sharding import PartitionSpec as P

STEPS = 2
COURANT = 0.2
F32 = jnp.float32


def shift_next(block, after):
    rows = block.shape[0]
    row_ids = lax.broadcasted_iota(jnp.int32, block.shape, 0)
    return jnp.where(row_ids == rows - 1, after, pltpu.roll(block, rows - 1, 0))


def shift_prev(block, before):
    row_ids = lax.broadcasted_iota(jnp.int32, block.shape, 0)
    return jnp.where(row_ids == 0, before, pltpu.roll(block, 1, 0))


def lane_next(block):
    return pltpu.roll(block, block.shape[1] - 1, 1)


def lane_prev(block):
    return pltpu.roll(block, 1, 1)


def advect_tile(tracers, zonal, merid, counts, level):
    cell_n, zonal_n, zonal_first_n, merid_n = counts
    u, u_before, u_after = zonal
    face_u = jnp.where(level < zonal_n, 0.25 * (u + shift_next(u, u_after)), 0.0)
    first_u = jnp.where(level < zonal_first_n, 0.25 * (u_before + u[0:1]), 0.0)
    face_v = jnp.where(level < merid_n, 0.25 * (merid + lane_next(merid)), 0.0)
    out = []
    for c, c_before, c_after in tracers:
        flux_x = face_u * (c + shift_next(c, c_after))
        first_x = first_u * (c_before + c[0:1])
        flux_y = face_v * (c + lane_next(c))
        spread = (flux_x - shift_prev(flux_x, first_x)) + (flux_y - lane_prev(flux_y))
        out.append(jnp.where(level < cell_n, c - COURANT * spread, 0.0))
    return out


def advect_kernel(groups, rows, levels_own, scal, state, cell_n, zonal_n, merid_n, *outs):
    level_here = pl.program_id(0)
    nx = state.shape[3]
    group = scal[0]
    level = scal[2] + level_here
    for part in range(groups):
        for tile in range(2):
            row0 = (tile * groups + (group ^ part)) * rows
            before = pl.multiple_of(lax.rem(row0 + nx - 8, nx), 8)
            after = pl.multiple_of(lax.rem(row0 + rows, nx), 8)
            here = pl.multiple_of(row0, 8)

            def whole(field):
                return (
                    state[0, field, 0, pl.ds(here, rows), :],
                    state[0, field, 0, pl.ds(before, 8), :][7:8],
                    state[0, field, 0, pl.ds(after, 8), :][0:1],
                )

            counts = (
                cell_n[0, pl.ds(here, rows), :],
                zonal_n[0, pl.ds(here, rows), :],
                zonal_n[0, pl.ds(before, 8), :][7:8],
                merid_n[0, pl.ds(here, rows), :],
            )
            merid = state[0, 3, 0, pl.ds(here, rows), :]
            moved = advect_tile([whole(0), whole(1)], whole(2), merid, counts, level)
            for field in range(2):
                outs[part][0, field, 0, tile] = moved[field]


def factor_kernel(half_levels, scal, own, got, own_drag, cell_n, rate, inv_t, inv_v, mid):
    half = scal[1]
    tile = pl.program_id(1)
    top = half == 0
    start = half * (half_levels - 1)
    is_own = tile == half
    count = cell_n[0, 0]
    shape = count.shape
    drag = jnp.where(is_own, own_drag[0], got[0, half_levels])
    prev = jnp.zeros(shape, F32)
    c_t = prev
    c_v = prev
    for e in range(half_levels):
        spot = jnp.where(top, e, half_levels - 1 - e)
        deeper = jnp.where(top, e + 1, 2 * half_levels - 1 - e)
        level = jnp.where(top, e, 2 * half_levels - 1 - e)
        diff = jnp.where(is_own, own[0, start + spot], got[0, spot])
        r = jnp.where(deeper < count, diff, 0.0)
        base = 1.0 + r
        den_t = base + prev * (1.0 - c_t)
        den_v = base + prev * (1.0 - c_v) + jnp.where(level == count - 1, drag, 0.0)
        i_t = 1.0 / den_t
        i_v = 1.0 / den_v
        rate[0, 0, e] = r
        inv_t[0, 0, e] = i_t
        inv_v[0, 0, e] = i_v
        c_t = r * i_t
        c_v = r * i_v
        prev = r
    mid[0, 0, 0] = c_t
    mid[0, 0, 1] = c_v


def sweep(rhs, rate, inv, store):
    half_levels = rate.shape[2]
    carry = [None, None]
    before = None
    for e in range(half_levels):
        inverse = inv[0, 0, e]
        for f in range(2):
            value = rhs(e, f)
            if e > 0:
                value = value + before * carry[f]
            carry[f] = value * inverse
            store(e, f, carry[f])
        before = rate[0, 0, e]
    return carry


def back(d_ref, other, rate, inv, mid, mid_other, kind, store):
    half_levels = rate.shape[2]
    last = half_levels - 1
    c_own = mid[0, 0, kind]
    c_oth = mid_other[0, 0, kind]
    scale = 1.0 / (1.0 - c_own * c_oth)
    value = [(d_ref[0, 0, f, last] + c_own * other[0, 0, f]) * scale for f in range(2)]
    for f in range(2):
        store(last, f, value[f])
    for e in range(last - 1, -1, -1):
        c = rate[0, 0, e] * inv[0, 0, e]
        for f in range(2):
            value[f] = d_ref[0, 0, f, e] + c * value[f]
            store(e, f, value[f])


def forced(forcing, count, force_ids, f):
    if force_ids[f] is None:
        return 0.0
    return jnp.where(count > 0, forcing[0, force_ids[f], 0], 0.0)


def first_kernel(groups, levels_own, force_ids, masked, scal, *refs):
    chunks = refs[:groups]
    rate, inv, cell_n, forcing, d_ref, mid_ref, buf = refs[groups:]
    count = cell_n[0, 0]
    for part in range(groups):
        for lev in range(levels_own):
            at = 3 + part * levels_own + lev
            slot = scal[at]
            level = scal[at + groups * levels_own]
            for f in range(2):
                value = chunks[part][0, f, lev, 0]
                buf[f, slot] = value if masked else jnp.where(level < count, value, 0.0)

    def rhs(e, f):
        value = buf[f, e]
        return value + forced(forcing, count, force_ids, f) if e == 0 else value

    def store(e, f, value):
        d_ref[0, 0, f, e] = value

    carry = sweep(rhs, rate, inv, store)
    for f in range(2):
        mid_ref[0, 0, f] = carry[f]


def middle_v_kernel(scal, d_ref, other, rate, inv, mid, mid_other, cell_n, forcing, x_ref, top_ref, end_ref, d2_ref, mid2_ref):
    rows = x_ref.shape[4]

    def keep(e, f, value):
        x_ref[0, 0, f, e] = value
        if f == 0:
            top_ref[0, 0, pl.ds(e, 1), :] = value[0:1]
            end_ref[0, 0, pl.ds(e, 1), :] = value[rows - 1 : rows]

    back(d_ref, other, rate, inv, mid, mid_other, 1, keep)
    count = cell_n[0, 0]

    def rhs(e, f):
        value = x_ref[0, 0, f, e]
        return value + forced(forcing, count, (1, 2), f) if e == 0 else value

    def store(e, f, value):
        d2_ref[0, 0, f, e] = value

    carry = sweep(rhs, rate, inv, store)
    for f in range(2):
        mid2_ref[0, 0, f] = carry[f]


def middle_t_kernel(scal, d_ref, other, rate, inv, mid, mid_other, x_ref, top_ref, end_ref):
    rows = x_ref.shape[4]

    def keep(e, f, value):
        x_ref[0, 0, f, e] = value
        top_ref[0, 0, f, pl.ds(e, 1), :] = value[0:1]
        end_ref[0, 0, f, pl.ds(e, 1), :] = value[rows - 1 : rows]

    back(d_ref, other, rate, inv, mid, mid_other, 0, keep)


def second_t_kernel(scal, x_ref, v_ref, t_before, t_after, u_before, u_after, rate, inv, cell_n, zonal_n, first_n, merid_n, forcing, d_ref, mid_ref, buf):
    half_levels = rate.shape[2]
    top = scal[1] == 0
    count = cell_n[0, 0]
    counts = (count, zonal_n[0, 0], first_n[0, 0], merid_n[0, 0])
    for e in range(half_levels):
        level = jnp.where(top, e, 2 * half_levels - 1 - e)
        tracers = [
            (x_ref[0, 0, f, e], t_before[0, 0, f, e : e + 1, :], t_after[0, 0, f, e : e + 1, :]) for f in range(2)
        ]
        zonal = (v_ref[0, 0, 0, e], u_before[0, 0, e : e + 1, :], u_after[0, 0, e : e + 1, :])
        moved = advect_tile(tracers, zonal, v_ref[0, 0, 1, e], counts, level)
        for f in range(2):
            buf[f, e] = moved[f]

    def rhs(e, f):
        value = buf[f, e]
        return value + forced(forcing, count, (0, None), f) if e == 0 else value

    def store(e, f, value):
        d_ref[0, 0, f, e] = value

    carry = sweep(rhs, rate, inv, store)
    for f in range(2):
        mid_ref[0, 0, f] = carry[f]


def last_kernel(groups, levels_own, kind, scal, d_ref, other, rate, inv, mid, mid_other, *refs):
    outs = refs[:groups]
    buf = refs[groups]

    def keep(e, f, value):
        buf[f, e] = value

    back(d_ref, other, rate, inv, mid, mid_other, kind, keep)
    for part in range(groups):
        for lev in range(levels_own):
            slot = scal[3 + part * levels_own + lev]
            for f in range(2):
                outs[part][0, f, lev, 0] = buf[f, slot]


def place_kernel(groups, member, fields, aliased, scal, *refs):
    chunks = refs[:groups]
    out, sem = refs[groups + (1 if aliased else 0) :]
    copies = []
    for part in range(groups):
        place = scal[0] ^ part
        members = chunks[part].shape[0]
        copies.append(
            pltpu.make_async_copy(
                chunks[part],
                out.at[pl.ds(member, members), pl.ds(fields, 2), :, :, place],
                sem.at[part],
            )
        )
    for copy in copies:
        copy.start()
    for copy in copies:
        copy.wait()


VMEM_LIMIT = 40 * 1024 * 1024


def call(kernel, name, scal, grid, inputs, outputs, scratch=(), aliases=None, cost=None):
    def spec(block, index):
        if block is None:
            return pl.BlockSpec(memory_space=pl.ANY)
        return pl.BlockSpec(block, index)

    bytes_moved = sum(a.size * 4 for a, b, _ in inputs if b is not None)
    for s, b, _ in outputs:
        size = 4
        for dim in s:
            size *= dim
        bytes_moved += size
    return pl.pallas_call(
        kernel,
        grid_spec=pltpu.PrefetchScalarGridSpec(
            num_scalar_prefetch=1,
            grid=grid,
            in_specs=[spec(b, i) for _, b, i in inputs],
            out_specs=[spec(b, i) for _, b, i in outputs],
            scratch_shapes=list(scratch),
        ),
        out_shape=[jax.ShapeDtypeStruct(s, F32) for s, _, _ in outputs],
        input_output_aliases=aliases or {},
        compiler_params=pltpu.CompilerParams(vmem_limit_bytes=VMEM_LIMIT),
        cost_estimate=pl.CostEstimate(flops=bytes_moved * 4, bytes_accessed=bytes_moved, transcendentals=0),
        name=name,
    )(scal, *[a for a, _, _ in inputs])


def per_device(slabs, ocean_state, diffusivity, bottom_drag, surface_forcing, land_sea, bottom_level):
    members, _, own, nx, ny = ocean_state.shape
    groups = slabs // 2
    rows = nx // slabs
    levels = diffusivity.shape[1]
    half_levels = levels // 2
    slab = lax.axis_index("slab")
    half = slab // groups
    group = slab % groups
    partner = [(i, (i + groups) % slabs) for i in range(slabs)]

    def swap(values):
        return lax.ppermute(values, "slab", partner)

    def cross(values, part):
        return lax.ppermute(values, "slab", [(i, (i // groups) * groups + ((i % groups) ^ part)) for i in range(slabs)])

    to_next = [(i, (i // groups) * groups + (i % groups + 1) % groups) for i in range(slabs)]
    to_prev = [(b, a) for a, b in to_next]

    parts = jnp.arange(groups, dtype=jnp.int32)
    local = ((group ^ parts)[:, None] * own + jnp.arange(own, dtype=jnp.int32)[None, :]).reshape(-1)
    slots = jnp.where(half == 0, local, half_levels - 1 - local)
    scal = jnp.concatenate(
        [
            jnp.stack([group, half, slab * own, ]).astype(jnp.int32),
            slots,
            half * half_levels + local,
        ]
    ).astype(jnp.int32)

    view = ocean_state.reshape(members, 4, own, 2, groups, rows, ny)
    v_send = [
        lax.dynamic_index_in_dim(view[:, 2:4], group ^ part, 4, keepdims=False) for part in range(groups)
    ]
    v_got = [v_send[0]] + [cross(v_send[part], part) for part in range(1, groups)]

    give = jnp.concatenate(
        [
            lax.dynamic_slice_in_dim(diffusivity, (1 - half) * (half_levels - 1), half_levels, 1),
            bottom_drag[:, None],
        ],
        axis=1,
    )
    got = swap(give)

    f_got = swap(surface_forcing)
    f_tiles = jnp.where(half == 0, jnp.stack([surface_forcing, f_got], axis=2), 0.0)
    forcing = lax.all_gather(f_tiles, "member", axis=4, tiled=True)

    cell_n = jnp.where(land_sea == 1, bottom_level, 0)
    zonal_n = jnp.minimum(cell_n, jnp.roll(cell_n, -1, axis=1))
    merid_n = jnp.minimum(cell_n, jnp.concatenate([cell_n[:, :, 1:], jnp.zeros_like(cell_n[:, :, :1])], axis=2))

    def tiles(values):
        return lax.dynamic_index_in_dim(values.reshape(members, 2, groups, rows, ny), group, 2, keepdims=False)

    cell_t = tiles(cell_n)
    zonal_t = tiles(zonal_n)
    merid_t = tiles(merid_n)
    first_t = tiles(jnp.roll(zonal_n, 1, axis=1))[:, :, :1]

    chunk_shape = (1, 2, own, 2, rows, ny)

    def advected(m):
        return call(
            functools.partial(advect_kernel, groups, rows, own),
            "advect",
            scal,
            (own,),
            [
                (ocean_state, (1, 4, 1, nx, ny), lambda l, s: (m, 0, l, 0, 0)),
                (cell_n, (1, nx, ny), lambda l, s: (m, 0, 0)),
                (zonal_n, (1, nx, ny), lambda l, s: (m, 0, 0)),
                (merid_n, (1, nx, ny), lambda l, s: (m, 0, 0)),
            ],
            [(chunk_shape, (1, 2, 1, 2, rows, ny), lambda l, s: (0, 0, l, 0, 0, 0))] * groups,
        )

    t_send = [advected(m) for m in range(members)]
    t_got = [[t_send[m][0]] + [cross(t_send[m][part], part) for part in range(1, groups)] for m in range(members)]

    col_shape = (members, 2, half_levels, rows, ny)
    col_block = (1, 1, half_levels, rows, ny)
    rate, inv_t, inv_v, mid = call(
        functools.partial(factor_kernel, half_levels),
        "factor",
        scal,
        (members, 2),
        [
            (diffusivity, (1, levels, rows, ny), lambda m, t, s: (m, 0, 0, 0)),
            (got, (1, half_levels + 1, rows, ny), lambda m, t, s: (m, 0, 0, 0)),
            (bottom_drag, (1, rows, ny), lambda m, t, s: (m, 0, 0)),
            (cell_t, (1, 1, rows, ny), lambda m, t, s: (m, t, 0, 0)),
        ],
        [
            (col_shape, col_block, lambda m, t, s: (m, t, 0, 0, 0)),
            (col_shape, col_block, lambda m, t, s: (m, t, 0, 0, 0)),
            (col_shape, col_block, lambda m, t, s: (m, t, 0, 0, 0)),
            ((members, 2, 2, rows, ny), (1, 1, 2, rows, ny), lambda m, t, s: (m, t, 0, 0, 0)),
        ],
    )
    mid_other = swap(mid)

    state_block = (1, 1, 2, half_levels, rows, ny)
    pair_block = (1, 1, 2, rows, ny)

    def at(m0):
        def mine(extra):
            return lambda m, t, s: (m, t) + (0,) * extra

        def shared(extra):
            return lambda m, t, s: (m + m0, t) + (0,) * extra

        return mine, shared

    def first(chunks, m0, count, inv, force_ids, masked):
        mine, shared = at(m0)
        return call(
            functools.partial(first_kernel, groups, own, force_ids, masked),
            "first",
            scal,
            (count, 2),
            [(c, (1, 2, own, 1, rows, ny), lambda m, t, s: (m, 0, 0, t, 0, 0)) for c in chunks]
            + [
                (rate, col_block, shared(3)),
                (inv, col_block, shared(3)),
                (cell_t, (1, 1, rows, ny), shared(2)),
                (forcing, (1, 3, 1, rows, ny), lambda m, t, s: (0, 0, t, 0, 0)),
            ],
            [
                ((count, 2, 2, half_levels, rows, ny), state_block, mine(4)),
                ((count, 2, 2, rows, ny), pair_block, mine(3)),
            ],
            [pltpu.VMEM((2, half_levels, rows, ny), F32)],
        )

    def last(d, other, m0, count, inv, kind):
        mine, shared = at(m0)
        return call(
            functools.partial(last_kernel, groups, own, kind),
            "last",
            scal,
            (count, 2),
            [
                (d, state_block, mine(4)),
                (other, pair_block, mine(3)),
                (rate, col_block, shared(3)),
                (inv, col_block, shared(3)),
                (mid, pair_block, shared(3)),
                (mid_other, pair_block, shared(3)),
            ],
            [((count, 2, own, 2, rows, ny), (1, 2, own, 1, rows, ny), lambda m, t, s: (m, 0, 0, t, 0, 0))] * groups,
            [pltpu.VMEM((2, half_levels, rows, ny), F32)],
        )

    mine, shared = at(0)
    d_v, dm_v = first(v_got, 0, members, inv_v, (1, 2), False)
    dm_v_other = swap(dm_v)
    x_v, u_top, u_end, d2_v, dm2_v = call(
        middle_v_kernel,
        "middle_v",
        scal,
        (members, 2),
        [
            (d_v, state_block, mine(4)),
            (dm_v_other, pair_block, mine(3)),
            (rate, col_block, shared(3)),
            (inv_v, col_block, shared(3)),
            (mid, pair_block, shared(3)),
            (mid_other, pair_block, shared(3)),
            (cell_t, (1, 1, rows, ny), shared(2)),
            (forcing, (1, 3, 1, rows, ny), lambda m, t, s: (1, 0, t, 0, 0)),
        ],
        [
            ((members, 2, 2, half_levels, rows, ny), state_block, mine(4)),
            ((members, 2, half_levels, ny), (1, 1, half_levels, ny), mine(2)),
            ((members, 2, half_levels, ny), (1, 1, half_levels, ny), mine(2)),
            ((members, 2, 2, half_levels, rows, ny), state_block, mine(4)),
            ((members, 2, 2, rows, ny), pair_block, mine(3)),
        ],
    )
    dm2_v_other = swap(dm2_v)
    u_before = lax.ppermute(u_end, "slab", to_next)
    u_after = lax.ppermute(u_top, "slab", to_prev)
    out_v = last(d2_v, dm2_v_other, 0, members, inv_v, 1)
    back_v = [out_v[0]] + [cross(out_v[part], part) for part in range(1, groups)]

    back_t = []
    for m in range(members):
        mine, shared = at(m)
        d_t, dm_t = first(t_got[m], m, 1, inv_t, (0, None), True)
        dm_t_other = swap(dm_t)
        x_t, t_top, t_end = call(
            middle_t_kernel,
            "middle_t",
            scal,
            (1, 2),
            [
                (d_t, state_block, mine(4)),
                (dm_t_other, pair_block, mine(3)),
                (rate, col_block, shared(3)),
                (inv_t, col_block, shared(3)),
                (mid, pair_block, shared(3)),
                (mid_other, pair_block, shared(3)),
            ],
            [
                ((1, 2, 2, half_levels, rows, ny), state_block, mine(4)),
                ((1, 2, 2, half_levels, ny), (1, 1, 2, half_levels, ny), mine(3)),
                ((1, 2, 2, half_levels, ny), (1, 1, 2, half_levels, ny), mine(3)),
            ],
        )
        t_before = lax.ppermute(t_end, "slab", to_next)
        t_after = lax.ppermute(t_top, "slab", to_prev)

        def from_before(extra, m0):
            return lambda i, t, s: (i + m0, t ^ jnp.where(s[0] == 0, 1, 0)) + (0,) * extra

        def from_after(extra, m0):
            return lambda i, t, s: (i + m0, t ^ jnp.where(s[0] == groups - 1, 1, 0)) + (0,) * extra

        d2_t, dm2_t = call(
            second_t_kernel,
            "second_t",
            scal,
            (1, 2),
            [
                (x_t, state_block, mine(4)),
                (x_v, state_block, shared(4)),
                (t_before, (1, 1, 2, half_levels, ny), from_before(3, 0)),
                (t_after, (1, 1, 2, half_levels, ny), from_after(3, 0)),
                (u_before, (1, 1, half_levels, ny), from_before(2, m)),
                (u_after, (1, 1, half_levels, ny), from_after(2, m)),
                (rate, col_block, shared(3)),
                (inv_t, col_block, shared(3)),
                (cell_t, (1, 1, rows, ny), shared(2)),
                (zonal_t, (1, 1, rows, ny), shared(2)),
                (first_t, (1, 1, 1, ny), shared(2)),
                (merid_t, (1, 1, rows, ny), shared(2)),
                (forcing, (1, 3, 1, rows, ny), lambda i, t, s: (1, 0, t, 0, 0)),
            ],
            [
                ((1, 2, 2, half_levels, rows, ny), state_block, mine(4)),
                ((1, 2, 2, rows, ny), pair_block, mine(3)),
            ],
            [pltpu.VMEM((2, half_levels, rows, ny), F32)],
        )
        out_t = last(d2_t, swap(dm2_t), m, 1, inv_t, 0)
        back_t.append([out_t[0]] + [cross(out_t[part], part) for part in range(1, groups)])

    whole = view.shape
    sems = [pltpu.SemaphoreType.DMA((groups,))]
    (result,) = call(
        functools.partial(place_kernel, groups, 0, 2, False),
        "place_v",
        scal,
        (),
        [(c, None, None) for c in back_v],
        [(whole, None, None)],
        sems,
    )
    for m in range(members):
        (result,) = call(
            functools.partial(place_kernel, groups, m, 0, True),
            "place_t",
            scal,
            (),
            [(c, None, None) for c in back_t[m]] + [(result, None, None)],
            [(whole, None, None)],
            sems,
            {groups + 1: 0},
        )
    return result.reshape(ocean_state.shape)


def solution(mesh):
    placed = (
        P("member", None, "slab", None, None),
        P("member", None, "slab", None),
        P("member", "slab", None),
        P(None, None, "slab", "member"),
        P("member", None, None),
        P("member", None, None),
    )
    return jax.shard_map(
        functools.partial(per_device, mesh.shape["slab"]),
        mesh=mesh,
        in_specs=placed,
        out_specs=P("member", None, "slab", None, None),
        check_vma=False,
    )
```

time: 600 us -> 182 us (0.30)
  blocking collectives: 203 us -> 13.8 us
  other arithmetic: 142 us -> 3.22 us
  waiting for transfers between devices: 164 us -> 81.5 us
  local copies, waits for them, and re-layouts: 75.5 us -> 8.8 us
  starting transfers between devices: 12 us -> 45.2 us
  Pallas kernels: 0 us -> 28.6 us
    all_to_all x2 -> x0, blocking collectives: 194 us -> none  [per_device(): lax.all_to_all(columns, 'slab', split_axis=2, concat_axis=3, tiled=True)]
    all_to_all x2 -> x0, waiting for transfers between devices: 164 us -> none  [per_device(): lax.all_to_all(current, 'slab', split_axis=3, concat_axis=2, tiled=True)]
    dynamic_update_slice x64 -> x0, other arithmetic: 128 us -> none  [mix_columns(): lax.scan(eliminate, (start_zero, start_zero), (lower_band, upper_band, di...]
    ppermute x0 -> x33, waiting for transfers between devices: none -> 81.5 us  [the longest x9 40.4 us: swap(): return lax.ppermute(values, 'slab', partner)]
    ppermute x0 -> x33, starting transfers between devices: none -> 45.2 us  [the longest x18 25.7 us: cross(): lax.ppermute(values, 'slab', [(i, i // groups * groups + (i % groups ^ pa...]
    mul x39 -> x0, local copies, waits for them, and re-layouts: 30.5 us -> none  [the longest x32 28.2 us: eliminate(): denominator = diagonal_row - lower_row * prior_upper]
    pallas_call x0 -> x17, Pallas kernels: none -> 28.6 us  [call(): pl.pallas_call(kernel, grid_spec=pltpu.PrefetchScalarGridSpec(num_scalar_...]
    another operation x7 -> x0, local copies, waits for them, and re-layouts: 15.9 us -> none
  transfers between devices with their start and end apart: 2 -> 33, of which waited for: 2 -> 16; matrix products, arithmetic and copies ran while one was open for 2% -> 7% of each run, Pallas kernels for 0% -> 13%
where the time goes in v1:
time: 182 us; the launch traced here: 181 us
  waiting for transfers between devices  81.5 us (45%)
  starting transfers between devices  45.2 us (25%)
  Pallas kernels  28.6 us (16%)
  blocking collectives  13.8 us (8%)
  local copies, waits for them, and re-layouts  8.8 us (5%)
  other arithmetic  3.22 us (2%)
    ppermute x9, waiting for transfers between devices, swap(): return lax.ppermute(values, 'slab', partner)  40.4 us
    ppermute x18, waiting for transfers between devices, cross(): lax.ppermute(values, 'slab', [(i, i // groups * groups + (i % groups ^ pa...  33 us
    pallas_call x17, Pallas kernels, call(): pl.pallas_call(kernel, grid_spec=pltpu.PrefetchScalarGridSpec(num_scalar_...  28.6 us
    ppermute x18, starting transfers between devices, cross(): lax.ppermute(values, 'slab', [(i, i // groups * groups + (i % groups ^ pa...  25.7 us
    all_gather x1, blocking collectives, per_device(): forcing = lax.all_gather(f_tiles, 'member', axis=4, tiled=True)  13.8 us
    ppermute x9, starting transfers between devices, swap(): return lax.ppermute(values, 'slab', partner)  10.5 us
    ppermute x2, waiting for transfers between devices, per_device(): t_before = lax.ppermute(t_end, 'slab', to_next)  5.95 us
    ppermute x2, starting transfers between devices, per_device(): t_after = lax.ppermute(t_top, 'slab', to_prev)  5.02 us
  transfers between devices with their start and end apart: 33, of which 16 were waited for; matrix products, arithmetic and copies ran while one was open for 7% of the time, Pallas kernels for 13%

profile of v1, /device:TPU:0, one launch (start us, length us, event | category | flops | bytes accessed | tf_op | source)
XLA Modules:
  0.0 181.4 jit_solution(7279294891640618425)
XLA Ops:
  0.0 4.0 %collective-permute-start.4 = (f32[2,3,32,64]{3,2,1,0:T(8,128)}, f32[2,3,32,64]{3,2,1,0:T(8,128)S(1)}, u32[]{:S(2)}, u32[]{:S(2)}) collective-permute-start(f32[2,3,32,64]{3,2,1,0:T(8,128)} %param.9), channel_id=1, source_target_pairs={{0,4},{1,5},{2,6},{3,7},{4,0},{5,1},{6,2},{7,3},{8,12},{9,13},{10,... | collective-permute-start | bytes 147464 | tf_op jit(solution)/shard_map/ppermute | solution.py:318
  9.8 2.9 %collective-permute-start.9 = (f32[2,2,2,2,32,256]{5,4,3,2,1,0:T(8,128)}, f32[2,2,2,2,32,256]{5,4,3,2,1,0:T(8,128)}, u32[]{:S(2)}, u32[]{:S(2)}) collective-permute-start(f32[2,2,2,2,32,256]{5,4,3,2,1,0:T(8,128)} %get-tuple-element.95), channel_id=1, source_target_pairs={{0,3},{1,2},{2,1},{3,0},{4,7},{5,6},{6,5},{7,4},{8,11},{9,10},{10,... | collective-permute-start | bytes 1572872 | tf_op jit(solution)/shard_map/ppermute | solution.py:321
  17.0 13.8 %all_gather.3 = f32[2,3,2,32,256]{3,2,1,0,4:T(2,128)} all-gather(f32[2,3,2,32,64]{3,2,1,0,4:T(2,128)S(1)} %copy.33), channel_id=1, replica_groups=mesh['member'=4,'slab'=8] {'member'}, dimensions={4}, use_global_device_ids=true | all-gather | bytes 491520 | tf_op jit(solution)/shard_map/all_gather | solution.py:354
  37.4 9.9 %collective-permute-done.8.refs_2_ = f32[2,2,2,2,32,256]{5,4,3,2,1,0:T(8,128)} collective-permute-done((f32[2,2,2,2,32,256]{5,4,3,2,1,0:T(8,128)}, f32[2,2,2,2,32,256]{5,4,3,2,1,0:T(8,128)}, u32[]{:S(2)}, u32[]{:S(2)}) %collective-permute-start.8) | collective-permute-done | bytes 524320 | tf_op jit(solution)/shard_map/ppermute | solution.py:321
  47.3 3.4 %first.4 = (f32[2,2,2,8,32,256]{5,4,3,2,1,0:T(8,128)S(1)}, f32[2,2,2,32,256]{4,3,2,1,0:T(8,128)S(1)}) custom-call(s32[19]{0:T(128)S(1)} %concatenate.17.scal, f32[2,2,2,2,32,256]{5,4,3,2,1,0:T(8,128)S(1)} %get-tuple-element.98.refs_0_, f32[2,2,2,2,32,256]{5,4,3,2,1,0:T(8,128)} %collective-permute-done.7.refs_1_, ...), custom_call_target="tpu_custom_call" | custom-call | flops 28311552 | bytes 7077888 | tf_op jit(solution)/shard_map/first/pallas_call | solution.py:289
  50.7 4.2 %collective-permute-start.10 = (f32[2,2,2,32,256]{4,3,2,1,0:T(8,128)S(1)}, f32[2,2,2,32,256]{4,3,2,1,0:T(8,128)S(1)}, u32[]{:S(2)}, u32[]{:S(2)}) collective-permute-start(f32[2,2,2,32,256]{4,3,2,1,0:T(8,128)S(1)} %get-tuple-element.62), channel_id=1, source_target_pairs={{0,4},{1,5},{2,6},{3,7},{4,0},{5,1},{6,2},{7,3},{8,12},{9,13},{10,... | collective-permute-start | bytes 786440 | tf_op jit(solution)/shard_map/ppermute | solution.py:318
  55.1 3.0 %advect.3 = (f32[1,2,2,2,32,256]{5,4,3,2,1,0:T(8,128)S(1)}, f32[1,2,2,2,32,256]{5,4,3,2,1,0:T(8,128)S(1)}, f32[1,2,2,2,32,256]{5,4,3,2,1,0:T(8,128)S(1)}, f32[1,2,2,2,32,256]{5,4,3,2,1,0:T(8,128)S(1)}) custom-call(s32[19]{0:T(128)S(1)} %concatenate.17.scal, f32[2,4,2,256,256]{4,3,2,1,0:T(8,128)S(1)} %copy-done, ...), custom_call_target="tpu_custom_call" | custom-call | flops 27262976 | bytes 6815744 | tf_op jit(solution)/shard_map/advect/pallas_call | solution.py:289
  62.1 2.9 %advect.2 = (f32[1,2,2,2,32,256]{5,4,3,2,1,0:T(8,128)S(1)}, f32[1,2,2,2,32,256]{5,4,3,2,1,0:T(8,128)S(1)}, f32[1,2,2,2,32,256]{5,4,3,2,1,0:T(8,128)S(1)}, f32[1,2,2,2,32,256]{5,4,3,2,1,0:T(8,128)S(1)}) custom-call(s32[19]{0:T(128)S(1)} %concatenate.17.scal, f32[2,4,2,256,256]{4,3,2,1,0:T(8,128)S(1)} %copy-done, ...), custom_call_target="tpu_custom_call" | custom-call | flops 27262976 | bytes 6815744 | tf_op jit(solution)/shard_map/advect/pallas_call | solution.py:289
  65.1 8.1 %collective-permute-done.10.other = f32[2,2,2,32,256]{4,3,2,1,0:T(8,128)S(1)} collective-permute-done((f32[2,2,2,32,256]{4,3,2,1,0:T(8,128)S(1)}, f32[2,2,2,32,256]{4,3,2,1,0:T(8,128)S(1)}, u32[]{:S(2)}, u32[]{:S(2)}) %collective-permute-start.10) | collective-permute-done | bytes 262176 | tf_op jit(solution)/shard_map/ppermute | solution.py:318
  73.6 3.1 %collective-permute-done.6.mid_other = f32[2,2,2,32,256]{4,3,2,1,0:T(8,128)S(1)} collective-permute-done((f32[2,2,2,32,256]{4,3,2,1,0:T(8,128)S(1)}, f32[2,2,2,32,256]{4,3,2,1,0:T(8,128)S(1)}, u32[]{:S(2)}, u32[]{:S(2)}) %collective-permute-start.6) | collective-permute-done | bytes 262176 | tf_op jit(solution)/shard_map/ppermute | solution.py:318
  78.1 6.1 %collective-permute-done.21.refs_3_ = f32[1,2,2,2,32,256]{5,4,3,2,1,0:T(8,128)S(1)} collective-permute-done((f32[1,2,2,2,32,256]{5,4,3,2,1,0:T(8,128)S(1)}, f32[1,2,2,2,32,256]{5,4,3,2,1,0:T(8,128)S(1)}, u32[]{:S(2)}, u32[]{:S(2)}) %collective-permute-start.21) | collective-permute-done | bytes 262176 | tf_op jit(solution)/shard_map/ppermute | solution.py:321
  85.1 5.5 %collective-permute-start.1 = (f32[1,2,2,2,32,256]{5,4,3,2,1,0:T(8,128)S(1)}, f32[1,2,2,2,32,256]{5,4,3,2,1,0:T(8,128)S(1)}, u32[]{:S(2)}, u32[]{:S(2)}) collective-permute-start(f32[1,2,2,2,32,256]{5,4,3,2,1,0:T(8,128)S(1)} %get-tuple-element.52), channel_id=1, source_target_pairs={{0,2},{1,3},{2,0},{3,1},{4,6},{5,7},{6,4},{7,5},{8,10},{9,11},{10,... | collective-permute-start | bytes 786440 | tf_op jit(solution)/shard_map/ppermute | solution.py:321
  90.6 5.9 %collective-permute-done.22.other = f32[1,2,2,32,256]{4,3,2,1,0:T(8,128)S(1)} collective-permute-done((f32[1,2,2,32,256]{4,3,2,1,0:T(8,128)S(1)}, f32[1,2,2,32,256]{4,3,2,1,0:T(8,128)S(1)}, u32[]{:S(2)}, u32[]{:S(2)}) %collective-permute-start.22) | collective-permute-done | bytes 131104 | tf_op jit(solution)/shard_map/ppermute | solution.py:318
  100.3 2.9 %collective-permute-start.14 = (f32[2,2,8,256]{3,2,1,0:T(8,128)S(1)}, f32[2,2,8,256]{3,2,1,0:T(8,128)S(1)}, u32[]{:S(2)}, u32[]{:S(2)}) collective-permute-start(f32[2,2,8,256]{3,2,1,0:T(8,128)S(1)} %get-tuple-element.67), channel_id=1, source_target_pairs={{1,0},{2,1},{3,2},{0,3},{5,4},{6,5},{7,6},{4,7},{9,8},{10,9},{11,1... | collective-permute-start | bytes 98312 | tf_op jit(solution)/shard_map/ppermute | solution.py:490
  109.0 2.8 %second_t.3 = (f32[1,2,2,8,32,256]{5,4,3,2,1,0:T(8,128)S(1)}, f32[1,2,2,32,256]{4,3,2,1,0:T(8,128)S(1)}) custom-call(s32[19]{0:T(128)S(1)} %concatenate.17.scal, f32[1,2,2,8,32,256]{5,4,3,2,1,0:T(8,128)S(1)} %get-tuple-element.80.x_ref, f32[2,2,2,8,32,256]{5,4,3,2,1,0:T(8,128)S(1)} %get-tuple-element.63.v_ref, ...), custom_call_target="tpu_custom_call" | custom-call | flops 29376512 | bytes 7344128 | tf_op jit(solution)/shard_map/second_t/pallas_call | solution.py:289
  112.1 5.4 %collective-permute-done.2.refs_3_ = f32[1,2,2,2,32,256]{5,4,3,2,1,0:T(8,128)S(1)} collective-permute-done((f32[1,2,2,2,32,256]{5,4,3,2,1,0:T(8,128)S(1)}, f32[1,2,2,2,32,256]{5,4,3,2,1,0:T(8,128)S(1)}, u32[]{:S(2)}, u32[]{:S(2)}) %collective-permute-start.2) | collective-permute-done | bytes 262176 | tf_op jit(solution)/shard_map/ppermute | solution.py:321
  118.5 15.3 %collective-permute-done.25.other = f32[1,2,2,32,256]{4,3,2,1,0:T(8,128)S(1)} collective-permute-done((f32[1,2,2,32,256]{4,3,2,1,0:T(8,128)S(1)}, f32[1,2,2,32,256]{4,3,2,1,0:T(8,128)S(1)}, u32[]{:S(2)}, u32[]{:S(2)}) %collective-permute-start.25) | collective-permute-done | bytes 131104 | tf_op jit(solution)/shard_map/ppermute | solution.py:318
  137.8 5.9 %collective-permute-done.11.t_before = f32[1,2,2,8,256]{4,3,2,1,0:T(8,128)S(1)} collective-permute-done((f32[1,2,2,8,256]{4,3,2,1,0:T(8,128)S(1)}, f32[1,2,2,8,256]{4,3,2,1,0:T(8,128)S(1)}, u32[]{:S(2)}, u32[]{:S(2)}) %collective-permute-start.11) | collective-permute-done | bytes 32800 | tf_op jit(solution)/shard_map/ppermute | solution.py:518
  143.7 2.5 %collective-permute-start.12 = (f32[1,2,2,8,256]{4,3,2,1,0:T(8,128)S(1)}, f32[1,2,2,8,256]{4,3,2,1,0:T(8,128)S(1)}, u32[]{:S(2)}, u32[]{:S(2)}) collective-permute-start(f32[1,2,2,8,256]{4,3,2,1,0:T(8,128)S(1)} %get-tuple-element.65), channel_id=1, source_target_pairs={{1,0},{2,1},{3,2},{0,3},{5,4},{6,5},{7,6},{4,7},{9,8},{10,9},{11,1... | collective-permute-start | bytes 98312 | tf_op jit(solution)/shard_map/ppermute | solution.py:519
  147.9 2.8 %second_t.2 = (f32[1,2,2,8,32,256]{5,4,3,2,1,0:T(8,128)S(1)}, f32[1,2,2,32,256]{4,3,2,1,0:T(8,128)S(1)}) custom-call(s32[19]{0:T(128)S(1)} %concatenate.17.scal, f32[1,2,2,8,32,256]{5,4,3,2,1,0:T(8,128)S(1)} %get-tuple-element.59.x_ref, f32[2,2,2,8,32,256]{5,4,3,2,1,0:T(8,128)S(1)} %get-tuple-element.63.v_ref, ...), custom_call_target="tpu_custom_call" | custom-call | flops 29376512 | bytes 7344128 | tf_op jit(solution)/shard_map/second_t/pallas_call | solution.py:289
  152.3 5.8 %collective-permute-done.15.other = f32[1,2,2,32,256]{4,3,2,1,0:T(8,128)S(1)} collective-permute-done((f32[1,2,2,32,256]{4,3,2,1,0:T(8,128)S(1)}, f32[1,2,2,32,256]{4,3,2,1,0:T(8,128)S(1)}, u32[]{:S(2)}, u32[]{:S(2)}) %collective-permute-start.15) | collective-permute-done | bytes 131104 | tf_op jit(solution)/shard_map/ppermute | solution.py:318
  158.4 2.5 %collective-permute-start.28 = (f32[1,2,2,2,32,256]{5,4,3,2,1,0:T(8,128)S(1)}, f32[1,2,2,2,32,256]{5,4,3,2,1,0:T(8,128)S(1)}, u32[]{:S(2)}, u32[]{:S(2)}) collective-permute-start(f32[1,2,2,2,32,256]{5,4,3,2,1,0:T(8,128)S(1)} %get-tuple-element.88), channel_id=1, source_target_pairs={{0,3},{1,2},{2,1},{3,0},{4,7},{5,6},{6,5},{7,4},{8,11},{9,10},{10,... | collective-permute-start | bytes 786440 | tf_op jit(solution)/shard_map/ppermute | solution.py:321
  167.4 6.4 %collective-permute-done.28.refs_3_ = f32[1,2,2,2,32,256]{5,4,3,2,1,0:T(8,128)S(1)} collective-permute-done((f32[1,2,2,2,32,256]{5,4,3,2,1,0:T(8,128)S(1)}, f32[1,2,2,2,32,256]{5,4,3,2,1,0:T(8,128)S(1)}, u32[]{:S(2)}, u32[]{:S(2)}) %collective-permute-start.28) | collective-permute-done | bytes 262176 | tf_op jit(solution)/shard_map/ppermute | solution.py:321
  176.3 3.6 %collective-permute-done.18.refs_3_ = f32[1,2,2,2,32,256]{5,4,3,2,1,0:T(8,128)S(1)} collective-permute-done((f32[1,2,2,2,32,256]{5,4,3,2,1,0:T(8,128)S(1)}, f32[1,2,2,2,32,256]{5,4,3,2,1,0:T(8,128)S(1)}, u32[]{:S(2)}, u32[]{:S(2)}) %collective-permute-start.18) | collective-permute-done | bytes 262176 | tf_op jit(solution)/shard_map/ppermute | solution.py:321
  (95 shorter events, 52.3 us)
Async XLA Ops:
  0.0 16.7 %collective-permute-start.4 = (f32[2,3,32,64]{3,2,1,0:T(8,128)}, f32[2,3,32,64]{3,2,1,0:T(8,128)S(1)}, u32[]{:S(2)}, u32[]{:S(2)}) collective-permute-start(f32[2,3,32,64]{3,2,1,0:T(8,128)} %param.9), channel_id=1, source_target_pairs={{0,4},{1,5},{2,6},{3,7},{4,0},{5,1},{6,2},{7,3},{8,12},{9,13},{10,... | collective-permute-start | bytes 147464 | tf_op jit(solution)/shard_map/ppermute | solution.py:318
  6.8 28.6 %collective-permute-start.3 = (f32[2,9,32,256]{3,2,1,0:T(8,128)}, f32[2,9,32,256]{3,2,1,0:T(8,128)S(1)}, u32[]{:S(2)}, u32[]{:S(2)}) collective-permute-start(f32[2,9,32,256]{3,2,1,0:T(8,128)} %pad_maximum_fusion), channel_id=1, source_target_pairs={{0,4},{1,5},{2,6},{3,7},{4,0},{5,1},{6,2},{7,3},{8,12},{9,13},{10,... | collective-permute-start | bytes 1769480 | tf_op jit(solution)/shard_map/ppermute | solution.py:318
  9.8 27.6 %collective-permute-start.9 = (f32[2,2,2,2,32,256]{5,4,3,2,1,0:T(8,128)}, f32[2,2,2,2,32,256]{5,4,3,2,1,0:T(8,128)}, u32[]{:S(2)}, u32[]{:S(2)}) collective-permute-start(f32[2,2,2,2,32,256]{5,4,3,2,1,0:T(8,128)} %get-tuple-element.95), channel_id=1, source_target_pairs={{0,3},{1,2},{2,1},{3,0},{4,7},{5,6},{6,5},{7,4},{8,11},{9,10},{10,... | collective-permute-start | bytes 1572872 | tf_op jit(solution)/shard_map/ppermute | solution.py:321
  12.6 34.6 %collective-permute-start.8 = (f32[2,2,2,2,32,256]{5,4,3,2,1,0:T(8,128)}, f32[2,2,2,2,32,256]{5,4,3,2,1,0:T(8,128)}, u32[]{:S(2)}, u32[]{:S(2)}) collective-permute-start(f32[2,2,2,2,32,256]{5,4,3,2,1,0:T(8,128)} %get-tuple-element.96), channel_id=1, source_target_pairs={{0,2},{1,3},{2,0},{3,1},{4,6},{5,7},{6,4},{7,5},{8,10},{9,11},{10,... | collective-permute-start | bytes 1572872 | tf_op jit(solution)/shard_map/ppermute | solution.py:321
  13.1 34.2 %collective-permute-start.7 = (f32[2,2,2,2,32,256]{5,4,3,2,1,0:T(8,128)}, f32[2,2,2,2,32,256]{5,4,3,2,1,0:T(8,128)}, u32[]{:S(2)}, u32[]{:S(2)}) collective-permute-start(f32[2,2,2,2,32,256]{5,4,3,2,1,0:T(8,128)} %get-tuple-element.97), channel_id=1, source_target_pairs={{0,1},{1,0},{2,3},{3,2},{4,5},{5,4},{6,7},{7,6},{8,9},{9,8},{10,11... | collective-permute-start | bytes 1572872 | tf_op jit(solution)/shard_map/ppermute | solution.py:321
  50.7 22.4 %collective-permute-start.10 = (f32[2,2,2,32,256]{4,3,2,1,0:T(8,128)S(1)}, f32[2,2,2,32,256]{4,3,2,1,0:T(8,128)S(1)}, u32[]{:S(2)}, u32[]{:S(2)}) collective-permute-start(f32[2,2,2,32,256]{4,3,2,1,0:T(8,128)S(1)} %get-tuple-element.62), channel_id=1, source_target_pairs={{0,4},{1,5},{2,6},{3,7},{4,0},{5,1},{6,2},{7,3},{8,12},{9,13},{10,... | collective-permute-start | bytes 786440 | tf_op jit(solution)/shard_map/ppermute | solution.py:318
  54.9 21.8 %collective-permute-start.6 = (f32[2,2,2,32,256]{4,3,2,1,0:T(8,128)S(1)}, f32[2,2,2,32,256]{4,3,2,1,0:T(8,128)S(1)}, u32[]{:S(2)}, u32[]{:S(2)}) collective-permute-start(f32[2,2,2,32,256]{4,3,2,1,0:T(8,128)S(1)} %get-tuple-element.58.mid), channel_id=1, source_target_pairs={{0,4},{1,5},{2,6},{3,7},{4,0},{5,1},{6,2},{7,3},{8,12},{9,13},{10,... | collective-permute-start | bytes 786440 | tf_op jit(solution)/shard_map/ppermute | solution.py:318
  58.1 20.0 %collective-permute-start.19 = (f32[1,2,2,2,32,256]{5,4,3,2,1,0:T(8,128)S(1)}, f32[1,2,2,2,32,256]{5,4,3,2,1,0:T(8,128)S(1)}, u32[]{:S(2)}, u32[]{:S(2)}) collective-permute-start(f32[1,2,2,2,32,256]{5,4,3,2,1,0:T(8,128)S(1)} %get-tuple-element.75), channel_id=1, source_target_pairs={{0,1},{1,0},{2,3},{3,2},{4,5},{5,4},{6,7},{7,6},{8,9},{9,8},{10,11... | collective-permute-start | bytes 786440 | tf_op jit(solution)/shard_map/ppermute | solution.py:321
  58.6 19.4 %collective-permute-start.20 = (f32[1,2,2,2,32,256]{5,4,3,2,1,0:T(8,128)S(1)}, f32[1,2,2,2,32,256]{5,4,3,2,1,0:T(8,128)S(1)}, u32[]{:S(2)}, u32[]{:S(2)}) collective-permute-start(f32[1,2,2,2,32,256]{5,4,3,2,1,0:T(8,128)S(1)} %get-tuple-element.76), channel_id=1, source_target_pairs={{0,2},{1,3},{2,0},{3,1},{4,6},{5,7},{6,4},{7,5},{8,10},{9,11},{10,... | collective-permute-start | bytes 786440 | tf_op jit(solution)/shard_map/ppermute | solution.py:321
  61.1 23.0 %collective-permute-start.21 = (f32[1,2,2,2,32,256]{5,4,3,2,1,0:T(8,128)S(1)}, f32[1,2,2,2,32,256]{5,4,3,2,1,0:T(8,128)S(1)}, u32[]{:S(2)}, u32[]{:S(2)}) collective-permute-start(f32[1,2,2,2,32,256]{5,4,3,2,1,0:T(8,128)S(1)} %get-tuple-element.77), channel_id=1, source_target_pairs={{0,3},{1,2},{2,1},{3,0},{4,7},{5,6},{6,5},{7,4},{8,11},{9,10},{10,... | collective-permute-start | bytes 786440 | tf_op jit(solution)/shard_map/ppermute | solution.py:321
  73.2 27.1 %collective-permute-start = (f32[1,2,2,2,32,256]{5,4,3,2,1,0:T(8,128)S(1)}, f32[1,2,2,2,32,256]{5,4,3,2,1,0:T(8,128)S(1)}, u32[]{:S(2)}, u32[]{:S(2)}) collective-permute-start(f32[1,2,2,2,32,256]{5,4,3,2,1,0:T(8,128)S(1)} %get-tuple-element.51), channel_id=1, source_target_pairs={{0,1},{1,0},{2,3},{3,2},{4,5},{5,4},{6,7},{7,6},{8,9},{9,8},{10,11... | collective-permute-start | bytes 786440 | tf_op jit(solution)/shard_map/ppermute | solution.py:321
  78.0 22.3 %collective-permute-start.29 = (f32[2,2,2,32,256]{4,3,2,1,0:T(8,128)S(1)}, f32[2,2,2,32,256]{4,3,2,1,0:T(8,128)S(1)}, u32[]{:S(2)}, u32[]{:S(2)}) collective-permute-start(f32[2,2,2,32,256]{4,3,2,1,0:T(8,128)S(1)} %get-tuple-element.90), channel_id=1, source_target_pairs={{0,4},{1,5},{2,6},{3,7},{4,0},{5,1},{6,2},{7,3},{8,12},{9,13},{10,... | collective-permute-start | bytes 786440 | tf_op jit(solution)/shard_map/ppermute | solution.py:318
  85.1 26.6 %collective-permute-start.1 = (f32[1,2,2,2,32,256]{5,4,3,2,1,0:T(8,128)S(1)}, f32[1,2,2,2,32,256]{5,4,3,2,1,0:T(8,128)S(1)}, u32[]{:S(2)}, u32[]{:S(2)}) collective-permute-start(f32[1,2,2,2,32,256]{5,4,3,2,1,0:T(8,128)S(1)} %get-tuple-element.52), channel_id=1, source_target_pairs={{0,2},{1,3},{2,0},{3,1},{4,6},{5,7},{6,4},{7,5},{8,10},{9,11},{10,... | collective-permute-start | bytes 786440 | tf_op jit(solution)/shard_map/ppermute | solution.py:321
  104.5 13.0 %collective-permute-start.2 = (f32[1,2,2,2,32,256]{5,4,3,2,1,0:T(8,128)S(1)}, f32[1,2,2,2,32,256]{5,4,3,2,1,0:T(8,128)S(1)}, u32[]{:S(2)}, u32[]{:S(2)}) collective-permute-start(f32[1,2,2,2,32,256]{5,4,3,2,1,0:T(8,128)S(1)} %get-tuple-element.53), channel_id=1, source_target_pairs={{0,3},{1,2},{2,1},{3,0},{4,7},{5,6},{6,5},{7,4},{8,11},{9,10},{10,... | collective-permute-start | bytes 786440 | tf_op jit(solution)/shard_map/ppermute | solution.py:321
  104.5 57.3 %collective-permute-start.30 = (f32[2,2,2,2,32,256]{5,4,3,2,1,0:T(8,128)S(1)}, f32[2,2,2,2,32,256]{5,4,3,2,1,0:T(8,128)S(1)}, u32[]{:S(2)}, u32[]{:S(2)}) collective-permute-start(f32[2,2,2,2,32,256]{5,4,3,2,1,0:T(8,128)S(1)} %get-tuple-element.92), channel_id=1, source_target_pairs={{0,1},{1,0},{2,3},{3,2},{4,5},{5,4},{6,7},{7,6},{8,9},{9,8},{10,11... | collective-permute-start | bytes 1572872 | tf_op jit(solution)/shard_map/ppermute | solution.py:321
  105.6 56.9 %collective-permute-start.31 = (f32[2,2,2,2,32,256]{5,4,3,2,1,0:T(8,128)S(1)}, f32[2,2,2,2,32,256]{5,4,3,2,1,0:T(8,128)S(1)}, u32[]{:S(2)}, u32[]{:S(2)}) collective-permute-start(f32[2,2,2,2,32,256]{5,4,3,2,1,0:T(8,128)S(1)} %get-tuple-element.93), channel_id=1, source_target_pairs={{0,2},{1,3},{2,0},{3,1},{4,6},{5,7},{6,4},{7,5},{8,10},{9,11},{10,... | collective-permute-start | bytes 1572872 | tf_op jit(solution)/shard_map/ppermute | solution.py:321
  108.0 56.0 %collective-permute-start.32 = (f32[2,2,2,2,32,256]{5,4,3,2,1,0:T(8,128)S(1)}, f32[2,2,2,2,32,256]{5,4,3,2,1,0:T(8,128)S(1)}, u32[]{:S(2)}, u32[]{:S(2)}) collective-permute-start(f32[2,2,2,2,32,256]{5,4,3,2,1,0:T(8,128)S(1)} %get-tuple-element.94), channel_id=1, source_target_pairs={{0,3},{1,2},{2,1},{3,0},{4,7},{5,6},{6,5},{7,4},{8,11},{9,10},{10,... | collective-permute-start | bytes 1572872 | tf_op jit(solution)/shard_map/ppermute | solution.py:321
  111.8 22.0 %collective-permute-start.25 = (f32[1,2,2,32,256]{4,3,2,1,0:T(8,128)S(1)}, f32[1,2,2,32,256]{4,3,2,1,0:T(8,128)S(1)}, u32[]{:S(2)}, u32[]{:S(2)}) collective-permute-start(f32[1,2,2,32,256]{4,3,2,1,0:T(8,128)S(1)} %get-tuple-element.84), channel_id=1, source_target_pairs={{0,4},{1,5},{2,6},{3,7},{4,0},{5,1},{6,2},{7,3},{8,12},{9,13},{10,... | collective-permute-start | bytes 393224 | tf_op jit(solution)/shard_map/ppermute | solution.py:318
  118.4 18.1 %collective-permute-start.5 = (f32[1,2,2,32,256]{4,3,2,1,0:T(8,128)S(1)}, f32[1,2,2,32,256]{4,3,2,1,0:T(8,128)S(1)}, u32[]{:S(2)}, u32[]{:S(2)}) collective-permute-start(f32[1,2,2,32,256]{4,3,2,1,0:T(8,128)S(1)} %get-tuple-element.57), channel_id=1, source_target_pairs={{0,4},{1,5},{2,6},{3,7},{4,0},{5,1},{6,2},{7,3},{8,12},{9,13},{10,... | collective-permute-start | bytes 393224 | tf_op jit(solution)/shard_map/ppermute | solution.py:318
  134.6 23.9 %collective-permute-start.26 = (f32[1,2,2,2,32,256]{5,4,3,2,1,0:T(8,128)S(1)}, f32[1,2,2,2,32,256]{5,4,3,2,1,0:T(8,128)S(1)}, u32[]{:S(2)}, u32[]{:S(2)}) collective-permute-start(f32[1,2,2,2,32,256]{5,4,3,2,1,0:T(8,128)S(1)} %get-tuple-element.86), channel_id=1, source_target_pairs={{0,1},{1,0},{2,3},{3,2},{4,5},{5,4},{6,7},{7,6},{8,9},{9,8},{10,11... | collective-permute-start | bytes 786440 | tf_op jit(solution)/shard_map/ppermute | solution.py:321
  158.4 15.3 %collective-permute-start.28 = (f32[1,2,2,2,32,256]{5,4,3,2,1,0:T(8,128)S(1)}, f32[1,2,2,2,32,256]{5,4,3,2,1,0:T(8,128)S(1)}, u32[]{:S(2)}, u32[]{:S(2)}) collective-permute-start(f32[1,2,2,2,32,256]{5,4,3,2,1,0:T(8,128)S(1)} %get-tuple-element.88), channel_id=1, source_target_pairs={{0,3},{1,2},{2,1},{3,0},{4,7},{5,6},{6,5},{7,4},{8,11},{9,10},{10,... | collective-permute-start | bytes 786440 | tf_op jit(solution)/shard_map/ppermute | solution.py:321
  161.8 13.5 %collective-permute-start.16 = (f32[1,2,2,2,32,256]{5,4,3,2,1,0:T(8,128)S(1)}, f32[1,2,2,2,32,256]{5,4,3,2,1,0:T(8,128)S(1)}, u32[]{:S(2)}, u32[]{:S(2)}) collective-permute-start(f32[1,2,2,2,32,256]{5,4,3,2,1,0:T(8,128)S(1)} %get-tuple-element.71), channel_id=1, source_target_pairs={{0,1},{1,0},{2,3},{3,2},{4,5},{5,4},{6,7},{7,6},{8,9},{9,8},{10,11... | collective-permute-start | bytes 786440 | tf_op jit(solution)/shard_map/ppermute | solution.py:321
  162.5 13.8 %collective-permute-start.17 = (f32[1,2,2,2,32,256]{5,4,3,2,1,0:T(8,128)S(1)}, f32[1,2,2,2,32,256]{5,4,3,2,1,0:T(8,128)S(1)}, u32[]{:S(2)}, u32[]{:S(2)}) collective-permute-start(f32[1,2,2,2,32,256]{5,4,3,2,1,0:T(8,128)S(1)} %get-tuple-element.72), channel_id=1, source_target_pairs={{0,2},{1,3},{2,0},{3,1},{4,6},{5,7},{6,4},{7,5},{8,10},{9,11},{10,... | collective-permute-start | bytes 786440 | tf_op jit(solution)/shard_map/ppermute | solution.py:321
  164.0 15.9 %collective-permute-start.18 = (f32[1,2,2,2,32,256]{5,4,3,2,1,0:T(8,128)S(1)}, f32[1,2,2,2,32,256]{5,4,3,2,1,0:T(8,128)S(1)}, u32[]{:S(2)}, u32[]{:S(2)}) collective-permute-start(f32[1,2,2,2,32,256]{5,4,3,2,1,0:T(8,128)S(1)} %get-tuple-element.73), channel_id=1, source_target_pairs={{0,3},{1,2},{2,1},{3,0},{4,7},{5,6},{6,5},{7,4},{8,11},{9,10},{10,... | collective-permute-start | bytes 786440 | tf_op jit(solution)/shard_map/ppermute | solution.py:321
  (15 other events, 144.7 us)

commit v2 on v1

--- a/solution.py
+++ b/solution.py
@@ -47,14 +47,12 @@
     return out
 
 
-def advect_kernel(groups, rows, levels_own, scal, state, cell_n, zonal_n, merid_n, *outs):
-    level_here = pl.program_id(0)
+def advect_kernel(groups, rows, scal, state, cell_n, zonal_n, merid_n, *outs):
     nx = state.shape[3]
-    group = scal[0]
-    level = scal[2] + level_here
+    level = scal[2] + pl.program_id(1)
     for part in range(groups):
         for tile in range(2):
-            row0 = (tile * groups + (group ^ part)) * rows
+            row0 = (tile * groups + (scal[0] ^ part)) * rows
             before = pl.multiple_of(lax.rem(row0 + nx - 8, nx), 8)
             after = pl.multiple_of(lax.rem(row0 + rows, nx), 8)
             here = pl.multiple_of(row0, 8)
@@ -78,7 +76,45 @@
                 outs[part][0, field, 0, tile] = moved[field]
 
 
-def factor_kernel(half_levels, scal, own, got, own_drag, cell_n, rate, inv_t, inv_v, mid):
+def split_kernel(groups, rows, scal, state, *outs):
+    for part in range(groups):
+        for tile in range(2):
+            here = pl.multiple_of((tile * groups + (scal[0] ^ part)) * rows, 8)
+            for field in range(2):
+                outs[part][0, field, 0, tile] = state[0, field, 0, pl.ds(here, rows), :]
+
+
+def give_kernel(half_levels, scal, own, drag, land, bottom, out, mid_other):
+    half = scal[1]
+    count = jnp.where(land[0] == 1, bottom[0], 0)
+    shape = count.shape
+    for e in range(half_levels):
+        out[0, e] = own[0, (1 - half) * (half_levels - 1) + e]
+    out[0, half_levels] = drag[0]
+
+    def ends(which):
+        top = which == 0
+        prev = jnp.zeros(shape, F32)
+        c_t = prev
+        c_v = prev
+        for e in range(half_levels):
+            upper = jnp.where(top, e, 2 * half_levels - 2 - e)
+            level = jnp.where(top, e, 2 * half_levels - 1 - e)
+            r = jnp.where(upper + 1 < count, own[0, upper], 0.0)
+            base = 1.0 + r
+            c_v = r / (base + prev * (1.0 - c_v) + jnp.where(level == count - 1, drag[0], 0.0))
+            c_t = r / (base + prev * (1.0 - c_t))
+            prev = r
+        return c_t, c_v
+
+    mine = ends(half)
+    others = ends(1 - half)
+    for kind in range(2):
+        out[0, half_levels + 1 + kind] = mine[kind]
+        mid_other[0, kind] = others[kind]
+
+
+def factor_kernel(half_levels, scal, own, got, own_drag, own_other, cell_n, rate, inv_t, inv_v, mid, mid_other):
     half = scal[1]
     tile = pl.program_id(1)
     top = half == 0
@@ -109,6 +145,8 @@
         prev = r
     mid[0, 0, 0] = c_t
     mid[0, 0, 1] = c_v
+    for kind in range(2):
+        mid_other[0, 0, kind] = jnp.where(is_own, own_other[0, kind], got[0, half_levels + 1 + kind])
 
 
 def sweep(rhs, rate, inv, store):
@@ -149,15 +187,20 @@
     return jnp.where(count > 0, forcing[0, force_ids[f], 0], 0.0)
 
 
+def slot_of(scal, part, lev, levels_own, half_levels):
+    spot = (scal[0] ^ part) * levels_own + lev
+    return jnp.where(scal[1] == 0, spot, half_levels - 1 - spot)
+
+
 def first_kernel(groups, levels_own, force_ids, masked, scal, *refs):
     chunks = refs[:groups]
     rate, inv, cell_n, forcing, d_ref, mid_ref, buf = refs[groups:]
+    half_levels = rate.shape[2]
     count = cell_n[0, 0]
     for part in range(groups):
         for lev in range(levels_own):
-            at = 3 + part * levels_own + lev
-            slot = scal[at]
-            level = scal[at + groups * levels_own]
+            slot = slot_of(scal, part, lev, levels_own, half_levels)
+            level = scal[1] * half_levels + (scal[0] ^ part) * levels_own + lev
             for f in range(2):
                 value = chunks[part][0, f, lev, 0]
                 buf[f, slot] = value if masked else jnp.where(level < count, value, 0.0)
@@ -237,8 +280,8 @@
 
 
 def last_kernel(groups, levels_own, kind, scal, d_ref, other, rate, inv, mid, mid_other, *refs):
-    outs = refs[:groups]
-    buf = refs[groups]
+    outs, buf = refs[:groups], refs[groups]
+    half_levels = rate.shape[2]
 
     def keep(e, f, value):
         buf[f, e] = value
@@ -246,7 +289,7 @@
     back(d_ref, other, rate, inv, mid, mid_other, kind, keep)
     for part in range(groups):
         for lev in range(levels_own):
-            slot = scal[3 + part * levels_own + lev]
+            slot = slot_of(scal, part, lev, levels_own, half_levels)
             for f in range(2):
                 outs[part][0, f, lev, 0] = buf[f, slot]
 
@@ -256,12 +299,11 @@
     out, sem = refs[groups + (1 if aliased else 0) :]
     copies = []
     for part in range(groups):
-        place = scal[0] ^ part
         members = chunks[part].shape[0]
         copies.append(
             pltpu.make_async_copy(
                 chunks[part],
-                out.at[pl.ds(member, members), pl.ds(fields, 2), :, :, place],
+                out.at[pl.ds(member, members), pl.ds(fields, 2), :, :, scal[0] ^ part],
                 sem.at[part],
             )
         )
@@ -271,13 +313,19 @@
         copy.wait()
 
 
-VMEM_LIMIT = 40 * 1024 * 1024
-
-
-def call(kernel, name, scal, grid, inputs, outputs, scratch=(), aliases=None, cost=None):
+def pick(values, which):
+    out = values[0]
+    for index in range(1, len(values)):
+        out = jnp.where(which == index, values[index], out)
+    return out
+
+
+def call(kernel, name, scal, grid, inputs, outputs, scratch=(), aliases=None, limit=40):
     def spec(block, index):
         if block is None:
             return pl.BlockSpec(memory_space=pl.ANY)
+        if block == "VMEM":
+            return pl.BlockSpec(memory_space=pltpu.VMEM)
         return pl.BlockSpec(block, index)
 
     bytes_moved = sum(a.size * 4 for a, b, _ in inputs if b is not None)
@@ -297,8 +345,8 @@
         ),
         out_shape=[jax.ShapeDtypeStruct(s, F32) for s, _, _ in outputs],
         input_output_aliases=aliases or {},
-        compiler_params=pltpu.CompilerParams(vmem_limit_bytes=VMEM_LIMIT),
-        cost_estimate=pl.CostEstimate(flops=bytes_moved * 4, bytes_accessed=bytes_moved, transcendentals=0),
+        compiler_params=pltpu.CompilerParams(vmem_limit_bytes=limit * 1024 * 1024),
+        cost_estimate=pl.CostEstimate(flops=0, bytes_accessed=bytes_moved // 1024, transcendentals=0),
         name=name,
     )(scal, *[a for a, _, _ in inputs])
 
@@ -317,41 +365,61 @@
     def swap(values):
         return lax.ppermute(values, "slab", partner)
 
-    def cross(values, part):
-        return lax.ppermute(values, "slab", [(i, (i // groups) * groups + ((i % groups) ^ part)) for i in range(slabs)])
+    def cross(values):
+        def moved(part):
+            return [(i, (i // groups) * groups + ((i % groups) ^ part)) for i in range(slabs)]
+
+        return [values[0]] + [lax.ppermute(values[part], "slab", moved(part)) for part in range(1, groups)]
 
     to_next = [(i, (i // groups) * groups + (i % groups + 1) % groups) for i in range(slabs)]
     to_prev = [(b, a) for a, b in to_next]
 
-    parts = jnp.arange(groups, dtype=jnp.int32)
-    local = ((group ^ parts)[:, None] * own + jnp.arange(own, dtype=jnp.int32)[None, :]).reshape(-1)
-    slots = jnp.where(half == 0, local, half_levels - 1 - local)
-    scal = jnp.concatenate(
+    scal = jnp.stack([group, half, slab * own]).astype(jnp.int32)
+
+    view = ocean_state.reshape(members, 4, own, 2, groups, rows, ny)
+    chunk_all = (members, 2, own, 2, rows, ny)
+    chunk_level = (1, 2, 1, 2, rows, ny)
+    v_send = call(
+        functools.partial(split_kernel, groups, rows),
+        "split",
+        scal,
+        (members, own),
+        [(ocean_state, (1, 2, 1, nx, ny), lambda m, l, s: (m, 1, l, 0, 0))],
+        [(chunk_all, chunk_level, lambda m, l, s: (m, 0, l, 0, 0, 0))] * groups,
+        limit=60,
+    )
+    v_send, (diffusivity, bottom_drag, land_sea, bottom_level, ocean_late) = lax.optimization_barrier(
+        (v_send, (diffusivity, bottom_drag, land_sea, bottom_level, ocean_state))
+    )
+    v_got = cross(v_send)
+
+    f_got = swap(surface_forcing)
+    give, own_other = call(
+        functools.partial(give_kernel, half_levels),
+        "give",
+        scal,
+        (members,),
         [
-            jnp.stack([group, half, slab * own, ]).astype(jnp.int32),
-            slots,
-            half * half_levels + local,
-        ]
-    ).astype(jnp.int32)
-
-    view = ocean_state.reshape(members, 4, own, 2, groups, rows, ny)
-    v_send = [
-        lax.dynamic_index_in_dim(view[:, 2:4], group ^ part, 4, keepdims=False) for part in range(groups)
+            (diffusivity, (1, levels, rows, ny), lambda m, s: (m, 0, 0, 0)),
+            (bottom_drag, (1, rows, ny), lambda m, s: (m, 0, 0)),
+            (land_sea, (1, rows, ny), lambda m, s: (m, s[1] * groups + s[0], 0)),
+            (bottom_level, (1, rows, ny), lambda m, s: (m, s[1] * groups + s[0], 0)),
+        ],
+        [
+            ((members, half_levels + 3, rows, ny), (1, half_levels + 3, rows, ny), lambda m, s: (m, 0, 0, 0)),
+            ((members, 2, rows, ny), (1, 2, rows, ny), lambda m, s: (m, 0, 0, 0)),
+        ],
+    )
+    give, land_sea, bottom_level, ocean_late = lax.optimization_barrier((give, land_sea, bottom_level, ocean_late))
+    got = swap(give)
+
+    f_tiles = jnp.where(half == 0, jnp.stack([surface_forcing, f_got], axis=2), 0.0)
+    places = lax.axis_size("member")
+    place = lax.axis_index("member")
+    f_parts = [f_tiles] + [
+        lax.ppermute(f_tiles, "member", [(i, (i + step) % places) for i in range(places)]) for step in range(1, places)
     ]
-    v_got = [v_send[0]] + [cross(v_send[part], part) for part in range(1, groups)]
-
-    give = jnp.concatenate(
-        [
-            lax.dynamic_slice_in_dim(diffusivity, (1 - half) * (half_levels - 1), half_levels, 1),
-            bottom_drag[:, None],
-        ],
-        axis=1,
-    )
-    got = swap(give)
-
-    f_got = swap(surface_forcing)
-    f_tiles = jnp.where(half == 0, jnp.stack([surface_forcing, f_got], axis=2), 0.0)
-    forcing = lax.all_gather(f_tiles, "member", axis=4, tiled=True)
+    forcing = jnp.concatenate([pick(f_parts, lax.rem(place - q + places, places)) for q in range(places)], axis=4)
 
     cell_n = jnp.where(land_sea == 1, bottom_level, 0)
     zonal_n = jnp.minimum(cell_n, jnp.roll(cell_n, -1, axis=1))
@@ -365,47 +433,44 @@
     merid_t = tiles(merid_n)
     first_t = tiles(jnp.roll(zonal_n, 1, axis=1))[:, :, :1]
 
-    chunk_shape = (1, 2, own, 2, rows, ny)
-
-    def advected(m):
-        return call(
-            functools.partial(advect_kernel, groups, rows, own),
-            "advect",
-            scal,
-            (own,),
-            [
-                (ocean_state, (1, 4, 1, nx, ny), lambda l, s: (m, 0, l, 0, 0)),
-                (cell_n, (1, nx, ny), lambda l, s: (m, 0, 0)),
-                (zonal_n, (1, nx, ny), lambda l, s: (m, 0, 0)),
-                (merid_n, (1, nx, ny), lambda l, s: (m, 0, 0)),
-            ],
-            [(chunk_shape, (1, 2, 1, 2, rows, ny), lambda l, s: (0, 0, l, 0, 0, 0))] * groups,
-        )
-
-    t_send = [advected(m) for m in range(members)]
-    t_got = [[t_send[m][0]] + [cross(t_send[m][part], part) for part in range(1, groups)] for m in range(members)]
+    t_send = call(
+        functools.partial(advect_kernel, groups, rows),
+        "advect",
+        scal,
+        (members, own),
+        [
+            (ocean_late, (1, 4, 1, nx, ny), lambda m, l, s: (m, 0, l, 0, 0)),
+            (cell_n, (1, nx, ny), lambda m, l, s: (m, 0, 0)),
+            (zonal_n, (1, nx, ny), lambda m, l, s: (m, 0, 0)),
+            (merid_n, (1, nx, ny), lambda m, l, s: (m, 0, 0)),
+        ],
+        [(chunk_all, chunk_level, lambda m, l, s: (m, 0, l, 0, 0, 0))] * groups,
+    )
 
     col_shape = (members, 2, half_levels, rows, ny)
     col_block = (1, 1, half_levels, rows, ny)
-    rate, inv_t, inv_v, mid = call(
+    mid_shape = (members, 2, 2, rows, ny)
+    mid_block = (1, 1, 2, rows, ny)
+    rate, inv_t, inv_v, mid, mid_other = call(
         functools.partial(factor_kernel, half_levels),
         "factor",
         scal,
         (members, 2),
         [
             (diffusivity, (1, levels, rows, ny), lambda m, t, s: (m, 0, 0, 0)),
-            (got, (1, half_levels + 1, rows, ny), lambda m, t, s: (m, 0, 0, 0)),
+            (got, (1, half_levels + 3, rows, ny), lambda m, t, s: (m, 0, 0, 0)),
             (bottom_drag, (1, rows, ny), lambda m, t, s: (m, 0, 0)),
+            (own_other, (1, 2, rows, ny), lambda m, t, s: (m, 0, 0, 0)),
             (cell_t, (1, 1, rows, ny), lambda m, t, s: (m, t, 0, 0)),
         ],
         [
             (col_shape, col_block, lambda m, t, s: (m, t, 0, 0, 0)),
             (col_shape, col_block, lambda m, t, s: (m, t, 0, 0, 0)),
             (col_shape, col_block, lambda m, t, s: (m, t, 0, 0, 0)),
-            ((members, 2, 2, rows, ny), (1, 1, 2, rows, ny), lambda m, t, s: (m, t, 0, 0, 0)),
+            (mid_shape, mid_block, lambda m, t, s: (m, t, 0, 0, 0)),
+            (mid_shape, mid_block, lambda m, t, s: (m, t, 0, 0, 0)),
         ],
     )
-    mid_other = swap(mid)
 
     state_block = (1, 1, 2, half_levels, rows, ny)
     pair_block = (1, 1, 2, rows, ny)
@@ -426,7 +491,7 @@
             "first",
             scal,
             (count, 2),
-            [(c, (1, 2, own, 1, rows, ny), lambda m, t, s: (m, 0, 0, t, 0, 0)) for c in chunks]
+            [(c, (1, 2, own, 1, rows, ny), lambda m, t, s: (m + m0, 0, 0, t, 0, 0)) for c in chunks]
             + [
                 (rate, col_block, shared(3)),
                 (inv, col_block, shared(3)),
@@ -461,6 +526,8 @@
 
     mine, shared = at(0)
     d_v, dm_v = first(v_got, 0, members, inv_v, (1, 2), False)
+    t_send, dm_v = lax.optimization_barrier((t_send, dm_v))
+    t_got = cross(t_send)
     dm_v_other = swap(dm_v)
     x_v, u_top, u_end, d2_v, dm2_v = call(
         middle_v_kernel,
@@ -488,19 +555,20 @@
     dm2_v_other = swap(dm2_v)
     u_before = lax.ppermute(u_end, "slab", to_next)
     u_after = lax.ppermute(u_top, "slab", to_prev)
+    d2_v, u_before, u_after = lax.optimization_barrier((d2_v, u_before, u_after))
     out_v = last(d2_v, dm2_v_other, 0, members, inv_v, 1)
-    back_v = [out_v[0]] + [cross(out_v[part], part) for part in range(1, groups)]
+    back_v = cross(out_v)
 
     back_t = []
-    for m in range(members):
+    for m in range(1):
         mine, shared = at(m)
-        d_t, dm_t = first(t_got[m], m, 1, inv_t, (0, None), True)
+        d_t, dm_t = first(t_got, m, members, inv_t, (0, None), True)
         dm_t_other = swap(dm_t)
         x_t, t_top, t_end = call(
             middle_t_kernel,
             "middle_t",
             scal,
-            (1, 2),
+            (members, 2),
             [
                 (d_t, state_block, mine(4)),
                 (dm_t_other, pair_block, mine(3)),
@@ -510,9 +578,9 @@
                 (mid_other, pair_block, shared(3)),
             ],
             [
-                ((1, 2, 2, half_levels, rows, ny), state_block, mine(4)),
-                ((1, 2, 2, half_levels, ny), (1, 1, 2, half_levels, ny), mine(3)),
-                ((1, 2, 2, half_levels, ny), (1, 1, 2, half_levels, ny), mine(3)),
+                ((members, 2, 2, half_levels, rows, ny), state_block, mine(4)),
+                ((members, 2, 2, half_levels, ny), (1, 1, 2, half_levels, ny), mine(3)),
+                ((members, 2, 2, half_levels, ny), (1, 1, 2, half_levels, ny), mine(3)),
             ],
         )
         t_before = lax.ppermute(t_end, "slab", to_next)
@@ -524,11 +592,12 @@
         def from_after(extra, m0):
             return lambda i, t, s: (i + m0, t ^ jnp.where(s[0] == groups - 1, 1, 0)) + (0,) * extra
 
+        x_t, back_v[1:-1] = lax.optimization_barrier((x_t, back_v[1:-1]))
         d2_t, dm2_t = call(
             second_t_kernel,
             "second_t",
             scal,
-            (1, 2),
+            (members, 2),
             [
                 (x_t, state_block, mine(4)),
                 (x_v, state_block, shared(4)),
@@ -545,13 +614,13 @@
                 (forcing, (1, 3, 1, rows, ny), lambda i, t, s: (1, 0, t, 0, 0)),
             ],
             [
-                ((1, 2, 2, half_levels, rows, ny), state_block, mine(4)),
-                ((1, 2, 2, rows, ny), pair_block, mine(3)),
+                ((members, 2, 2, half_levels, rows, ny), state_block, mine(4)),
+                ((members, 2, 2, rows, ny), pair_block, mine(3)),
             ],
             [pltpu.VMEM((2, half_levels, rows, ny), F32)],
         )
-        out_t = last(d2_t, swap(dm2_t), m, 1, inv_t, 0)
-        back_t.append([out_t[0]] + [cross(out_t[part], part) for part in range(1, groups)])
+        d2_t, back_v[-1] = lax.optimization_barrier((d2_t, back_v[-1]))
+        back_t.append(cross(last(d2_t, swap(dm2_t), m, members, inv_t, 0)))
 
     whole = view.shape
     sems = [pltpu.SemaphoreType.DMA((groups,))]
@@ -560,17 +629,17 @@
         "place_v",
         scal,
         (),
-        [(c, None, None) for c in back_v],
+        [(c, "VMEM", None) for c in back_v],
         [(whole, None, None)],
         sems,
     )
-    for m in range(members):
+    for m in range(1):
         (result,) = call(
             functools.partial(place_kernel, groups, m, 0, True),
             "place_t",
             scal,
             (),
-            [(c, None, None) for c in back_t[m]] + [(result, None, None)],
+            [(c, "VMEM", None) for c in back_t[m]] + [(result, None, None)],
             [(whole, None, None)],
             sems,
             {groups + 1: 0},

time: 182 us -> 171 us (0.940)
  waiting for transfers between devices: 81.5 us -> 105 us
  starting transfers between devices: 45.2 us -> 27.2 us
  blocking collectives: 13.8 us -> 0 us
  local copies, waits for them, and re-layouts: 8.8 us -> 3.2 us
  Pallas kernels: 28.6 us -> 31 us
    ppermute x1, waiting for transfers between devices: 0.55 us -> 23.5 us  [per_device(): u_before = lax.ppermute(u_end, 'slab', to_next)]
    all_gather x1 -> x0, blocking collectives: 13.8 us -> none  [per_device(): forcing = lax.all_gather(f_tiles, 'member', axis=4, tiled=True)]
    ppermute x18 -> x15, starting transfers between devices: 25.7 us -> 16 us  [the longest x12 14.1 us: cross(): lax.ppermute(values[part], 'slab', moved(part))]
    ppermute x18 -> x15, waiting for transfers between devices: 33 us -> 24.8 us  [the longest x12 16.4 us: cross(): lax.ppermute(values[part], 'slab', moved(part))]
    ppermute x9 -> x6, waiting for transfers between devices: 40.4 us -> 45.4 us  [swap(): return lax.ppermute(values, 'slab', partner)]
    ppermute x1, waiting for transfers between devices: 0.01 us -> 3.91 us  [per_device(): u_after = lax.ppermute(u_top, 'slab', to_prev)]
    ppermute x1, starting transfers between devices: 2.92 us -> 0.01 us  [per_device(): u_after = lax.ppermute(u_top, 'slab', to_prev)]
    ppermute x9 -> x6, starting transfers between devices: 10.5 us -> 7.59 us  [swap(): return lax.ppermute(values, 'slab', partner)]
  transfers between devices with their start and end apart: 33 -> 25, of which waited for: 16 -> 13; matrix products, arithmetic and copies ran while one was open for 7% -> 2% of each run, Pallas kernels for 13% -> 15%
where the time goes in v2:
time: 171 us; the launch traced here: 170 us
  waiting for transfers between devices  105 us (61%)
  Pallas kernels  31 us (18%)
  starting transfers between devices  27.2 us (16%)
  local copies, waits for them, and re-layouts  3.2 us (2%)
  other arithmetic  2.86 us (2%)
    ppermute x6, waiting for transfers between devices, swap(): return lax.ppermute(values, 'slab', partner)  45.4 us
    pallas_call x13, Pallas kernels, call(): pl.pallas_call(kernel, grid_spec=pltpu.PrefetchScalarGridSpec(num_scalar_...  31 us
    ppermute x1, waiting for transfers between devices, per_device(): u_before = lax.ppermute(u_end, 'slab', to_next)  23.5 us
    ppermute x12, waiting for transfers between devices, cross(): lax.ppermute(values[part], 'slab', moved(part))  16.4 us
    ppermute x12, starting transfers between devices, cross(): lax.ppermute(values[part], 'slab', moved(part))  14.1 us
    ppermute x3, waiting for transfers between devices, per_device(): lax.ppermute(f_tiles, 'member', [(i, (i + step) % places) for i in range(...  8.44 us
    ppermute x6, starting transfers between devices, swap(): return lax.ppermute(values, 'slab', partner)  7.59 us
    ppermute x1, waiting for transfers between devices, per_device(): t_before = lax.ppermute(t_end, 'slab', to_next)  6.8 us
  transfers between devices with their start and end apart: 25, of which 13 were waited for; matrix products, arithmetic and copies ran while one was open for 2% of the time, Pallas kernels for 15%

profile of v2, /device:TPU:0, one launch (start us, length us, event | category | flops | bytes accessed | tf_op | source)
XLA Modules:
  0.0 169.7 jit_solution(14383738367191996465)
XLA Ops:
  0.0 4.0 %collective-permute-start.4 = (f32[2,3,32,64]{3,2,1,0:T(8,128)}, f32[2,3,32,64]{3,2,1,0:T(8,128)S(1)}, u32[]{:S(2)}, u32[]{:S(2)}) collective-permute-start(f32[2,3,32,64]{3,2,1,0:T(8,128)} %param.9), channel_id=1, source_target_pairs={{0,4},{1,5},{2,6},{3,7},{4,0},{5,1},{6,2},{7,3},{8,12},{9,13},{10,... | collective-permute-start | bytes 147464 | tf_op jit(solution)/shard_map/ppermute | solution.py:366
  4.7 4.6 %split.1 = (f32[2,2,2,2,32,256]{5,4,3,2,1,0:T(8,128)}, f32[2,2,2,2,32,256]{5,4,3,2,1,0:T(8,128)}, f32[2,2,2,2,32,256]{5,4,3,2,1,0:T(8,128)}, f32[2,2,2,2,32,256]{5,4,3,2,1,0:T(8,128)}) custom-call(s32[3]{0:T(128)} %pad_add_fusion.1.scal, f32[2,4,2,256,256]{4,3,2,1,0:T(8,128)} %state.2), custom_call_target="tpu_custom_call" | custom-call | bytes 6144 | tf_op jit(solution)/shard_map/split/pallas_call | solution.py:337
  12.9 1.9 %give.1 = (f32[2,11,32,256]{3,2,1,0:T(8,128)}, f32[2,2,32,256]{3,2,1,0:T(8,128)S(1)}) custom-call(s32[3]{0:T(128)S(1)} %copy-done.6, f32[2,16,32,256]{3,2,1,0:T(8,128)S(1)} %copy-done.1, f32[2,32,256]{2,1,0:T(8,128)S(1)} %copy-done.5, s32[2,256,256]{2,1,0:T(8,128)S(1)} %copy-done.3, s32[2,256,256]{2,1,0:T(8,128)S(1)} %copy-done.2), custom_call_target="tpu_custom_call" | custom-call | bytes 2944 | tf_op jit(solution)/shard_map/give/pallas_call | solution.py:337
  15.9 5.0 %collective-permute-done.7 = f32[2,3,2,32,64]{4,3,2,1,0:T(8,128)S(1)} collective-permute-done((f32[2,3,2,32,64]{4,3,2,1,0:T(8,128)}, f32[2,3,2,32,64]{4,3,2,1,0:T(8,128)S(1)}, u32[]{:S(2)}, u32[]{:S(2)}) %collective-permute-start.7) | collective-permute-done | bytes 98336 | tf_op jit(solution)/shard_map/ppermute | solution.py:420
  23.5 2.2 %copy-done = f32[2,4,2,256,256]{4,3,2,1,0:T(8,128)S(1)} copy-done((f32[2,4,2,256,256]{4,3,2,1,0:T(8,128)S(1)}, f32[2,4,2,256,256]{4,3,2,1,0:T(8,128)}, u32[]{:S(2)}) %copy-start) | copy-done | bytes 4194328
  25.7 5.3 %advect.1 = (f32[2,2,2,2,32,256]{5,4,3,2,1,0:T(8,128)S(1)}, f32[2,2,2,2,32,256]{5,4,3,2,1,0:T(8,128)S(1)}, f32[2,2,2,2,32,256]{5,4,3,2,1,0:T(8,128)S(1)}, f32[2,2,2,2,32,256]{5,4,3,2,1,0:T(8,128)S(1)}) custom-call(s32[3]{0:T(128)S(1)} %copy-done.6, f32[2,4,2,256,256]{4,3,2,1,0:T(8,128)S(1)} %copy-done, s32[2,256,256]{2,1,0:T(8,128)S(1)} %compare_select_fusion.cell_n, ...), custom_call_target="tpu_custom_call" | custom-call | bytes 7680 | tf_op jit(solution)/shard_map/advect/pallas_call | solution.py:337
  31.1 3.5 %collective-permute-done.5 = f32[2,3,2,32,64]{4,3,2,1,0:T(8,128)S(1)} collective-permute-done((f32[2,3,2,32,64]{4,3,2,1,0:T(8,128)}, f32[2,3,2,32,64]{4,3,2,1,0:T(8,128)S(1)}, u32[]{:S(2)}, u32[]{:S(2)}) %collective-permute-start.5) | collective-permute-done | bytes 98336 | tf_op jit(solution)/shard_map/ppermute | solution.py:420
  35.8 14.2 %collective-permute-done.3.got = f32[2,11,32,256]{3,2,1,0:T(8,128)S(1)} collective-permute-done((f32[2,11,32,256]{3,2,1,0:T(8,128)}, f32[2,11,32,256]{3,2,1,0:T(8,128)S(1)}, u32[]{:S(2)}, u32[]{:S(2)}) %collective-permute-start.3) | collective-permute-done | bytes 720928 | tf_op jit(solution)/shard_map/ppermute | solution.py:366
  51.4 3.2 %first.2 = (f32[2,2,2,8,32,256]{5,4,3,2,1,0:T(8,128)S(1)}, f32[2,2,2,32,256]{4,3,2,1,0:T(8,128)S(1)}) custom-call(s32[3]{0:T(128)S(1)} %copy-done.6, f32[2,2,2,2,32,256]{5,4,3,2,1,0:T(8,128)S(1)} %copy-done.4, f32[2,2,2,2,32,256]{5,4,3,2,1,0:T(8,128)} %collective-permute-done.refs_1_, f32[2,2,2,2,32,256]{5,4,3,2,1,0:T(8,128)} %collective-permute-done.1.refs_2_, ...), custom_call_target="tpu_custom_call" | custom-call | bytes 6912 | tf_op jit(solution)/shard_map/first/pallas_call | solution.py:337
  54.6 3.3 %collective-permute-start.12 = (f32[2,2,2,32,256]{4,3,2,1,0:T(8,128)S(1)}, f32[2,2,2,32,256]{4,3,2,1,0:T(8,128)S(1)}, u32[]{:S(2)}, u32[]{:S(2)}) collective-permute-start(f32[2,2,2,32,256]{4,3,2,1,0:T(8,128)S(1)} %get-tuple-element.105), channel_id=1, source_target_pairs={{0,4},{1,5},{2,6},{3,7},{4,0},{5,1},{6,2},{7,3},{8,12},{9,13},{10,... | collective-permute-start | bytes 786440 | tf_op jit(solution)/shard_map/ppermute | solution.py:366
  58.4 3.0 %collective-permute-start.10 = (f32[2,2,2,2,32,256]{5,4,3,2,1,0:T(8,128)S(1)}, f32[2,2,2,2,32,256]{5,4,3,2,1,0:T(8,128)S(1)}, u32[]{:S(2)}, u32[]{:S(2)}) collective-permute-start(f32[2,2,2,2,32,256]{5,4,3,2,1,0:T(8,128)S(1)} %get-tuple-element.97), channel_id=1, source_target_pairs={{0,3},{1,2},{2,1},{3,0},{4,7},{5,6},{6,5},{7,4},{8,11},{9,10},{10,... | collective-permute-start | bytes 1572872 | tf_op jit(solution)/shard_map/ppermute | solution.py:372
  61.4 7.0 %collective-permute-done.12.other = f32[2,2,2,32,256]{4,3,2,1,0:T(8,128)S(1)} collective-permute-done((f32[2,2,2,32,256]{4,3,2,1,0:T(8,128)S(1)}, f32[2,2,2,32,256]{4,3,2,1,0:T(8,128)S(1)}, u32[]{:S(2)}, u32[]{:S(2)}) %collective-permute-start.12) | collective-permute-done | bytes 262176 | tf_op jit(solution)/shard_map/ppermute | solution.py:366
  70.3 23.5 %collective-permute-done.13.u_before = f32[2,2,8,256]{3,2,1,0:T(8,128)S(1)} collective-permute-done((f32[2,2,8,256]{3,2,1,0:T(8,128)S(1)}, f32[2,2,8,256]{3,2,1,0:T(8,128)S(1)}, u32[]{:S(2)}, u32[]{:S(2)}) %collective-permute-start.13) | collective-permute-done | bytes 32800 | tf_op jit(solution)/shard_map/ppermute | solution.py:556
  93.9 3.9 %collective-permute-done.14.u_after = f32[2,2,8,256]{3,2,1,0:T(8,128)S(1)} collective-permute-done((f32[2,2,8,256]{3,2,1,0:T(8,128)S(1)}, f32[2,2,8,256]{3,2,1,0:T(8,128)S(1)}, u32[]{:S(2)}, u32[]{:S(2)}) %collective-permute-start.14) | collective-permute-done | bytes 32800 | tf_op jit(solution)/shard_map/ppermute | solution.py:557
  102.0 2.1 %collective-permute-start.20 = (f32[2,2,2,2,32,256]{5,4,3,2,1,0:T(8,128)S(1)}, f32[2,2,2,2,32,256]{5,4,3,2,1,0:T(8,128)S(1)}, u32[]{:S(2)}, u32[]{:S(2)}) collective-permute-start(f32[2,2,2,2,32,256]{5,4,3,2,1,0:T(8,128)S(1)} %get-tuple-element.120), channel_id=1, source_target_pairs={{0,3},{1,2},{2,1},{3,0},{4,7},{5,6},{6,5},{7,4},{8,11},{9,10},{10,... | collective-permute-start | bytes 1572872 | tf_op jit(solution)/shard_map/ppermute | solution.py:372
  104.2 14.4 %collective-permute-done.11.other = f32[2,2,2,32,256]{4,3,2,1,0:T(8,128)S(1)} collective-permute-done((f32[2,2,2,32,256]{4,3,2,1,0:T(8,128)S(1)}, f32[2,2,2,32,256]{4,3,2,1,0:T(8,128)S(1)}, u32[]{:S(2)}, u32[]{:S(2)}) %collective-permute-start.11) | collective-permute-done | bytes 262176 | tf_op jit(solution)/shard_map/ppermute | solution.py:366
  120.1 2.4 %collective-permute-start.19 = (f32[2,2,2,8,256]{4,3,2,1,0:T(8,128)S(1)}, f32[2,2,2,8,256]{4,3,2,1,0:T(8,128)S(1)}, u32[]{:S(2)}, u32[]{:S(2)}) collective-permute-start(f32[2,2,2,8,256]{4,3,2,1,0:T(8,128)S(1)} %get-tuple-element.116), channel_id=1, source_target_pairs={{1,0},{2,1},{3,2},{0,3},{5,4},{6,5},{7,6},{4,7},{9,8},{10,9},{11,1... | collective-permute-start | bytes 196616 | tf_op jit(solution)/shard_map/ppermute | solution.py:587
  122.5 6.8 %collective-permute-done.18.t_before = f32[2,2,2,8,256]{4,3,2,1,0:T(8,128)S(1)} collective-permute-done((f32[2,2,2,8,256]{4,3,2,1,0:T(8,128)S(1)}, f32[2,2,2,8,256]{4,3,2,1,0:T(8,128)S(1)}, u32[]{:S(2)}, u32[]{:S(2)}) %collective-permute-start.18) | collective-permute-done | bytes 65568 | tf_op jit(solution)/shard_map/ppermute | solution.py:586
  129.9 5.0 %second_t.1 = (f32[2,2,2,8,32,256]{5,4,3,2,1,0:T(8,128)S(1)}, f32[2,2,2,32,256]{4,3,2,1,0:T(8,128)S(1)}) custom-call(s32[3]{0:T(128)S(1)} %copy-done.6, f32[2,2,2,8,32,256]{5,4,3,2,1,0:T(8,128)S(1)} %get-tuple-element.113.x_ref, f32[2,2,2,8,32,256]{5,4,3,2,1,0:T(8,128)S(1)} %get-tuple-element.114.v_ref, ...), custom_call_target="tpu_custom_call" | custom-call | bytes 9412 | tf_op jit(solution)/shard_map/second_t/pallas_call | solution.py:337
  135.0 9.8 %collective-permute-done.21.other = f32[2,2,2,32,256]{4,3,2,1,0:T(8,128)S(1)} collective-permute-done((f32[2,2,2,32,256]{4,3,2,1,0:T(8,128)S(1)}, f32[2,2,2,32,256]{4,3,2,1,0:T(8,128)S(1)}, u32[]{:S(2)}, u32[]{:S(2)}) %collective-permute-start.21) | collective-permute-done | bytes 262176 | tf_op jit(solution)/shard_map/ppermute | solution.py:366
  147.3 2.3 %collective-permute-start.24 = (f32[2,2,2,2,32,256]{5,4,3,2,1,0:T(8,128)S(1)}, f32[2,2,2,2,32,256]{5,4,3,2,1,0:T(8,128)S(1)}, u32[]{:S(2)}, u32[]{:S(2)}) collective-permute-start(f32[2,2,2,2,32,256]{5,4,3,2,1,0:T(8,128)S(1)} %get-tuple-element.126), channel_id=1, source_target_pairs={{0,3},{1,2},{2,1},{3,0},{4,7},{5,6},{6,5},{7,4},{8,11},{9,10},{10,... | collective-permute-start | bytes 1572872 | tf_op jit(solution)/shard_map/ppermute | solution.py:372
  149.6 1.9 %place_v.1.refs_4_ = f32[2,4,2,2,4,32,256]{6,5,4,3,2,1,0:T(8,128)} custom-call(s32[3]{0:T(128)S(1)} %copy-done.6, f32[2,2,2,2,32,256]{5,4,3,2,1,0:T(8,128)S(1)} %get-tuple-element.127.refs_0_, f32[2,2,2,2,32,256]{5,4,3,2,1,0:T(8,128)S(1)} %collective-permute-done.16.refs_1_, f32[2,2,2,2,32,256]{5,4,3,2,1,0:T(8,128)S(1)} %collective-permute-done.17.refs_2_, ...), custom_call_target="tpu_custom_call" | custom-call | bytes 6144 | tf_op jit(solution)/shard_map/place_v/pallas_call | solution.py:337
  151.5 8.3 %collective-permute-done.22.refs_1_ = f32[2,2,2,2,32,256]{5,4,3,2,1,0:T(8,128)S(1)} collective-permute-done((f32[2,2,2,2,32,256]{5,4,3,2,1,0:T(8,128)S(1)}, f32[2,2,2,2,32,256]{5,4,3,2,1,0:T(8,128)S(1)}, u32[]{:S(2)}, u32[]{:S(2)}) %collective-permute-start.22) | collective-permute-done | bytes 524320 | tf_op jit(solution)/shard_map/ppermute | solution.py:372
  161.7 6.2 %collective-permute-done.24.refs_3_ = f32[2,2,2,2,32,256]{5,4,3,2,1,0:T(8,128)S(1)} collective-permute-done((f32[2,2,2,2,32,256]{5,4,3,2,1,0:T(8,128)S(1)}, f32[2,2,2,2,32,256]{5,4,3,2,1,0:T(8,128)S(1)}, u32[]{:S(2)}, u32[]{:S(2)}) %collective-permute-start.24) | collective-permute-done | bytes 524320 | tf_op jit(solution)/shard_map/ppermute | solution.py:372
  (80 shorter events, 25.6 us)
Async XLA Ops:
  0.0 14.8 %collective-permute-start.4 = (f32[2,3,32,64]{3,2,1,0:T(8,128)}, f32[2,3,32,64]{3,2,1,0:T(8,128)S(1)}, u32[]{:S(2)}, u32[]{:S(2)}) collective-permute-start(f32[2,3,32,64]{3,2,1,0:T(8,128)} %param.9), channel_id=1, source_target_pairs={{0,4},{1,5},{2,6},{3,7},{4,0},{5,1},{6,2},{7,3},{8,12},{9,13},{10,... | collective-permute-start | bytes 147464 | tf_op jit(solution)/shard_map/ppermute | solution.py:366
  9.3 42.0 %collective-permute-start = (f32[2,2,2,2,32,256]{5,4,3,2,1,0:T(8,128)}, f32[2,2,2,2,32,256]{5,4,3,2,1,0:T(8,128)}, u32[]{:S(2)}, u32[]{:S(2)}) collective-permute-start(f32[2,2,2,2,32,256]{5,4,3,2,1,0:T(8,128)} %get-tuple-element.86), channel_id=1, source_target_pairs={{0,1},{1,0},{2,3},{3,2},{4,5},{5,4},{6,7},{7,6},{8,9},{9,8},{10,11... | collective-permute-start | bytes 1572872 | tf_op jit(solution)/shard_map/ppermute | solution.py:372
  10.9 40.5 %collective-permute-start.1 = (f32[2,2,2,2,32,256]{5,4,3,2,1,0:T(8,128)}, f32[2,2,2,2,32,256]{5,4,3,2,1,0:T(8,128)}, u32[]{:S(2)}, u32[]{:S(2)}) collective-permute-start(f32[2,2,2,2,32,256]{5,4,3,2,1,0:T(8,128)} %get-tuple-element.87), channel_id=1, source_target_pairs={{0,2},{1,3},{2,0},{3,1},{4,6},{5,7},{6,4},{7,5},{8,10},{9,11},{10,... | collective-permute-start | bytes 1572872 | tf_op jit(solution)/shard_map/ppermute | solution.py:372
  12.4 38.9 %collective-permute-start.2 = (f32[2,2,2,2,32,256]{5,4,3,2,1,0:T(8,128)}, f32[2,2,2,2,32,256]{5,4,3,2,1,0:T(8,128)}, u32[]{:S(2)}, u32[]{:S(2)}) collective-permute-start(f32[2,2,2,2,32,256]{5,4,3,2,1,0:T(8,128)} %get-tuple-element.88), channel_id=1, source_target_pairs={{0,3},{1,2},{2,1},{3,0},{4,7},{5,6},{6,5},{7,4},{8,11},{9,10},{10,... | collective-permute-start | bytes 1572872 | tf_op jit(solution)/shard_map/ppermute | solution.py:372
  14.8 35.3 %collective-permute-start.3 = (f32[2,11,32,256]{3,2,1,0:T(8,128)}, f32[2,11,32,256]{3,2,1,0:T(8,128)S(1)}, u32[]{:S(2)}, u32[]{:S(2)}) collective-permute-start(f32[2,11,32,256]{3,2,1,0:T(8,128)} %get-tuple-element.89), channel_id=1, source_target_pairs={{0,4},{1,5},{2,6},{3,7},{4,0},{5,1},{6,2},{7,3},{8,12},{9,13},{10,... | collective-permute-start | bytes 2162696 | tf_op jit(solution)/shard_map/ppermute | solution.py:366
  15.5 5.3 %collective-permute-start.7 = (f32[2,3,2,32,64]{4,3,2,1,0:T(8,128)}, f32[2,3,2,32,64]{4,3,2,1,0:T(8,128)S(1)}, u32[]{:S(2)}, u32[]{:S(2)}) collective-permute-start(f32[2,3,2,32,64]{4,3,2,1,0:T(8,128)} %maximum_select_fusion), channel_id=1, source_target_pairs={{0,8},{8,16},{16,24},{24,0},{1,9},{9,17},{17,25},{25,1},{2,10},{10... | collective-permute-start | bytes 294920 | tf_op jit(solution)/shard_map/ppermute | solution.py:420
  21.5 9.5 %collective-permute-start.6 = (f32[2,3,2,32,64]{4,3,2,1,0:T(8,128)}, f32[2,3,2,32,64]{4,3,2,1,0:T(8,128)}, u32[]{:S(2)}, u32[]{:S(2)}) collective-permute-start(f32[2,3,2,32,64]{4,3,2,1,0:T(8,128)} %maximum_select_fusion), channel_id=1, source_target_pairs={{0,16},{8,24},{16,0},{24,8},{1,17},{9,25},{17,1},{25,9},{2,18},{10... | collective-permute-start | bytes 294920 | tf_op jit(solution)/shard_map/ppermute | solution.py:420
  54.6 13.8 %collective-permute-start.12 = (f32[2,2,2,32,256]{4,3,2,1,0:T(8,128)S(1)}, f32[2,2,2,32,256]{4,3,2,1,0:T(8,128)S(1)}, u32[]{:S(2)}, u32[]{:S(2)}) collective-permute-start(f32[2,2,2,32,256]{4,3,2,1,0:T(8,128)S(1)} %get-tuple-element.105), channel_id=1, source_target_pairs={{0,4},{1,5},{2,6},{3,7},{4,0},{5,1},{6,2},{7,3},{8,12},{9,13},{10,... | collective-permute-start | bytes 786440 | tf_op jit(solution)/shard_map/ppermute | solution.py:366
  57.9 42.6 %collective-permute-start.8 = (f32[2,2,2,2,32,256]{5,4,3,2,1,0:T(8,128)S(1)}, f32[2,2,2,2,32,256]{5,4,3,2,1,0:T(8,128)S(1)}, u32[]{:S(2)}, u32[]{:S(2)}) collective-permute-start(f32[2,2,2,2,32,256]{5,4,3,2,1,0:T(8,128)S(1)} %get-tuple-element.95), channel_id=1, source_target_pairs={{0,1},{1,0},{2,3},{3,2},{4,5},{5,4},{6,7},{7,6},{8,9},{9,8},{10,11... | collective-permute-start | bytes 1572872 | tf_op jit(solution)/shard_map/ppermute | solution.py:372
  58.4 42.1 %collective-permute-start.9 = (f32[2,2,2,2,32,256]{5,4,3,2,1,0:T(8,128)S(1)}, f32[2,2,2,2,32,256]{5,4,3,2,1,0:T(8,128)S(1)}, u32[]{:S(2)}, u32[]{:S(2)}) collective-permute-start(f32[2,2,2,2,32,256]{5,4,3,2,1,0:T(8,128)S(1)} %get-tuple-element.96), channel_id=1, source_target_pairs={{0,2},{1,3},{2,0},{3,1},{4,6},{5,7},{6,4},{7,5},{8,10},{9,11},{10,... | collective-permute-start | bytes 1572872 | tf_op jit(solution)/shard_map/ppermute | solution.py:372
  58.4 42.1 %collective-permute-start.10 = (f32[2,2,2,2,32,256]{5,4,3,2,1,0:T(8,128)S(1)}, f32[2,2,2,2,32,256]{5,4,3,2,1,0:T(8,128)S(1)}, u32[]{:S(2)}, u32[]{:S(2)}) collective-permute-start(f32[2,2,2,2,32,256]{5,4,3,2,1,0:T(8,128)S(1)} %get-tuple-element.97), channel_id=1, source_target_pairs={{0,3},{1,2},{2,1},{3,0},{4,7},{5,6},{6,5},{7,4},{8,11},{9,10},{10,... | collective-permute-start | bytes 1572872 | tf_op jit(solution)/shard_map/ppermute | solution.py:372
  69.6 28.2 %collective-permute-start.15 = (f32[2,2,2,32,256]{4,3,2,1,0:T(8,128)S(1)}, f32[2,2,2,32,256]{4,3,2,1,0:T(8,128)S(1)}, u32[]{:S(2)}, u32[]{:S(2)}) collective-permute-start(f32[2,2,2,32,256]{4,3,2,1,0:T(8,128)S(1)} %get-tuple-element.110), channel_id=1, source_target_pairs={{0,4},{1,5},{2,6},{3,7},{4,0},{5,1},{6,2},{7,3},{8,12},{9,13},{10,... | collective-permute-start | bytes 786440 | tf_op jit(solution)/shard_map/ppermute | solution.py:366
  69.7 24.2 %collective-permute-start.13 = (f32[2,2,8,256]{3,2,1,0:T(8,128)S(1)}, f32[2,2,8,256]{3,2,1,0:T(8,128)S(1)}, u32[]{:S(2)}, u32[]{:S(2)}) collective-permute-start(f32[2,2,8,256]{3,2,1,0:T(8,128)S(1)} %get-tuple-element.107), channel_id=1, source_target_pairs={{0,1},{1,2},{2,3},{3,0},{4,5},{5,6},{6,7},{7,4},{8,9},{9,10},{10,1... | collective-permute-start | bytes 98312 | tf_op jit(solution)/shard_map/ppermute | solution.py:556
  93.9 3.9 %collective-permute-start.14 = (f32[2,2,8,256]{3,2,1,0:T(8,128)S(1)}, f32[2,2,8,256]{3,2,1,0:T(8,128)S(1)}, u32[]{:S(2)}, u32[]{:S(2)}) collective-permute-start(f32[2,2,8,256]{3,2,1,0:T(8,128)S(1)} %get-tuple-element.108), channel_id=1, source_target_pairs={{1,0},{2,1},{3,2},{0,3},{5,4},{6,5},{7,6},{4,7},{9,8},{10,9},{11,1... | collective-permute-start | bytes 98312 | tf_op jit(solution)/shard_map/ppermute | solution.py:557
  99.0 23.5 %collective-permute-start.16 = (f32[2,2,2,2,32,256]{5,4,3,2,1,0:T(8,128)S(1)}, f32[2,2,2,2,32,256]{5,4,3,2,1,0:T(8,128)S(1)}, u32[]{:S(2)}, u32[]{:S(2)}) collective-permute-start(f32[2,2,2,2,32,256]{5,4,3,2,1,0:T(8,128)S(1)} %get-tuple-element.111), channel_id=1, source_target_pairs={{0,1},{1,0},{2,3},{3,2},{4,5},{5,4},{6,7},{7,6},{8,9},{9,8},{10,11... | collective-permute-start | bytes 1572872 | tf_op jit(solution)/shard_map/ppermute | solution.py:372
  99.1 23.4 %collective-permute-start.17 = (f32[2,2,2,2,32,256]{5,4,3,2,1,0:T(8,128)S(1)}, f32[2,2,2,2,32,256]{5,4,3,2,1,0:T(8,128)S(1)}, u32[]{:S(2)}, u32[]{:S(2)}) collective-permute-start(f32[2,2,2,2,32,256]{5,4,3,2,1,0:T(8,128)S(1)} %get-tuple-element.112), channel_id=1, source_target_pairs={{0,2},{1,3},{2,0},{3,1},{4,6},{5,7},{6,4},{7,5},{8,10},{9,11},{10,... | collective-permute-start | bytes 1572872 | tf_op jit(solution)/shard_map/ppermute | solution.py:372
  101.9 16.6 %collective-permute-start.11 = (f32[2,2,2,32,256]{4,3,2,1,0:T(8,128)S(1)}, f32[2,2,2,32,256]{4,3,2,1,0:T(8,128)S(1)}, u32[]{:S(2)}, u32[]{:S(2)}) collective-permute-start(f32[2,2,2,32,256]{4,3,2,1,0:T(8,128)S(1)} %get-tuple-element.100), channel_id=1, source_target_pairs={{0,4},{1,5},{2,6},{3,7},{4,0},{5,1},{6,2},{7,3},{8,12},{9,13},{10,... | collective-permute-start | bytes 786440 | tf_op jit(solution)/shard_map/ppermute | solution.py:366
  102.0 33.0 %collective-permute-start.20 = (f32[2,2,2,2,32,256]{5,4,3,2,1,0:T(8,128)S(1)}, f32[2,2,2,2,32,256]{5,4,3,2,1,0:T(8,128)S(1)}, u32[]{:S(2)}, u32[]{:S(2)}) collective-permute-start(f32[2,2,2,2,32,256]{5,4,3,2,1,0:T(8,128)S(1)} %get-tuple-element.120), channel_id=1, source_target_pairs={{0,3},{1,2},{2,1},{3,0},{4,7},{5,6},{6,5},{7,4},{8,11},{9,10},{10,... | collective-permute-start | bytes 1572872 | tf_op jit(solution)/shard_map/ppermute | solution.py:372
  119.5 9.8 %collective-permute-start.18 = (f32[2,2,2,8,256]{4,3,2,1,0:T(8,128)S(1)}, f32[2,2,2,8,256]{4,3,2,1,0:T(8,128)S(1)}, u32[]{:S(2)}, u32[]{:S(2)}) collective-permute-start(f32[2,2,2,8,256]{4,3,2,1,0:T(8,128)S(1)} %get-tuple-element.115), channel_id=1, source_target_pairs={{0,1},{1,2},{2,3},{3,0},{4,5},{5,6},{6,7},{7,4},{8,9},{9,10},{10,1... | collective-permute-start | bytes 196616 | tf_op jit(solution)/shard_map/ppermute | solution.py:586
  120.1 9.8 %collective-permute-start.19 = (f32[2,2,2,8,256]{4,3,2,1,0:T(8,128)S(1)}, f32[2,2,2,8,256]{4,3,2,1,0:T(8,128)S(1)}, u32[]{:S(2)}, u32[]{:S(2)}) collective-permute-start(f32[2,2,2,8,256]{4,3,2,1,0:T(8,128)S(1)} %get-tuple-element.116), channel_id=1, source_target_pairs={{1,0},{2,1},{3,2},{0,3},{5,4},{6,5},{7,6},{4,7},{9,8},{10,9},{11,1... | collective-permute-start | bytes 196616 | tf_op jit(solution)/shard_map/ppermute | solution.py:587
  134.9 9.9 %collective-permute-start.21 = (f32[2,2,2,32,256]{4,3,2,1,0:T(8,128)S(1)}, f32[2,2,2,32,256]{4,3,2,1,0:T(8,128)S(1)}, u32[]{:S(2)}, u32[]{:S(2)}) collective-permute-start(f32[2,2,2,32,256]{4,3,2,1,0:T(8,128)S(1)} %get-tuple-element.122), channel_id=1, source_target_pairs={{0,4},{1,5},{2,6},{3,7},{4,0},{5,1},{6,2},{7,3},{8,12},{9,13},{10,... | collective-permute-start | bytes 786440 | tf_op jit(solution)/shard_map/ppermute | solution.py:366
  146.1 13.8 %collective-permute-start.22 = (f32[2,2,2,2,32,256]{5,4,3,2,1,0:T(8,128)S(1)}, f32[2,2,2,2,32,256]{5,4,3,2,1,0:T(8,128)S(1)}, u32[]{:S(2)}, u32[]{:S(2)}) collective-permute-start(f32[2,2,2,2,32,256]{5,4,3,2,1,0:T(8,128)S(1)} %get-tuple-element.124), channel_id=1, source_target_pairs={{0,1},{1,0},{2,3},{3,2},{4,5},{5,4},{6,7},{7,6},{8,9},{9,8},{10,11... | collective-permute-start | bytes 1572872 | tf_op jit(solution)/shard_map/ppermute | solution.py:372
  147.3 14.3 %collective-permute-start.23 = (f32[2,2,2,2,32,256]{5,4,3,2,1,0:T(8,128)S(1)}, f32[2,2,2,2,32,256]{5,4,3,2,1,0:T(8,128)S(1)}, u32[]{:S(2)}, u32[]{:S(2)}) collective-permute-start(f32[2,2,2,2,32,256]{5,4,3,2,1,0:T(8,128)S(1)} %get-tuple-element.125), channel_id=1, source_target_pairs={{0,2},{1,3},{2,0},{3,1},{4,6},{5,7},{6,4},{7,5},{8,10},{9,11},{10,... | collective-permute-start | bytes 1572872 | tf_op jit(solution)/shard_map/ppermute | solution.py:372
  147.3 20.5 %collective-permute-start.24 = (f32[2,2,2,2,32,256]{5,4,3,2,1,0:T(8,128)S(1)}, f32[2,2,2,2,32,256]{5,4,3,2,1,0:T(8,128)S(1)}, u32[]{:S(2)}, u32[]{:S(2)}) collective-permute-start(f32[2,2,2,2,32,256]{5,4,3,2,1,0:T(8,128)S(1)} %get-tuple-element.126), channel_id=1, source_target_pairs={{0,3},{1,2},{2,1},{3,0},{4,7},{5,6},{6,5},{7,4},{8,11},{9,10},{10,... | collective-permute-start | bytes 1572872 | tf_op jit(solution)/shard_map/ppermute | solution.py:372
  (14 other events, 100.3 us)

commit v3 on v2

--- a/solution.py
+++ b/solution.py
@@ -76,12 +76,16 @@
                 outs[part][0, field, 0, tile] = moved[field]
 
 
-def split_kernel(groups, rows, scal, state, *outs):
-    for part in range(groups):
-        for tile in range(2):
-            here = pl.multiple_of((tile * groups + (scal[0] ^ part)) * rows, 8)
-            for field in range(2):
-                outs[part][0, field, 0, tile] = state[0, field, 0, pl.ds(here, rows), :]
+def split_kernel(groups, scal, state, *refs):
+    outs, sem = refs[:groups], refs[groups]
+    copies = [
+        pltpu.make_async_copy(state.at[:, pl.ds(2, 2), :, :, scal[0] ^ part], outs[part], sem.at[part])
+        for part in range(groups)
+    ]
+    for copy in copies:
+        copy.start()
+    for copy in copies:
+        copy.wait()
 
 
 def give_kernel(half_levels, scal, own, drag, land, bottom, out, mid_other):
@@ -241,8 +245,10 @@
         mid2_ref[0, 0, f] = carry[f]
 
 
-def middle_t_kernel(scal, d_ref, other, rate, inv, mid, mid_other, x_ref, top_ref, end_ref):
+def middle_t_kernel(scal, d_ref, other, rate, inv, mid, mid_other, u_top, u_end, x_ref, top_ref, end_ref):
     rows = x_ref.shape[4]
+    top_ref[0, 0, 2] = u_top[0, 0]
+    end_ref[0, 0, 2] = u_end[0, 0]
 
     def keep(e, f, value):
         x_ref[0, 0, f, e] = value
@@ -252,17 +258,19 @@
     back(d_ref, other, rate, inv, mid, mid_other, 0, keep)
 
 
-def second_t_kernel(scal, x_ref, v_ref, t_before, t_after, u_before, u_after, rate, inv, cell_n, zonal_n, first_n, merid_n, forcing, d_ref, mid_ref, buf):
+def second_t_kernel(scal, x_ref, v_ref, before, after, rate, inv, cell_n, zonal_n, first_n, merid_n, forcing, d_ref, mid_ref, buf):
     half_levels = rate.shape[2]
     top = scal[1] == 0
     count = cell_n[0, 0]
     counts = (count, zonal_n[0, 0], first_n[0, 0], merid_n[0, 0])
     for e in range(half_levels):
         level = jnp.where(top, e, 2 * half_levels - 1 - e)
-        tracers = [
-            (x_ref[0, 0, f, e], t_before[0, 0, f, e : e + 1, :], t_after[0, 0, f, e : e + 1, :]) for f in range(2)
-        ]
-        zonal = (v_ref[0, 0, 0, e], u_before[0, 0, e : e + 1, :], u_after[0, 0, e : e + 1, :])
+
+        def edges(f):
+            return before[0, 0, f, e : e + 1, :], after[0, 0, f, e : e + 1, :]
+
+        tracers = [(x_ref[0, 0, f, e],) + edges(f) for f in range(2)]
+        zonal = (v_ref[0, 0, 0, e],) + edges(2)
         moved = advect_tile(tracers, zonal, v_ref[0, 0, 1, e], counts, level)
         for f in range(2):
             buf[f, e] = moved[f]
@@ -294,17 +302,14 @@
                 outs[part][0, f, lev, 0] = buf[f, slot]
 
 
-def place_kernel(groups, member, fields, aliased, scal, *refs):
-    chunks = refs[:groups]
-    out, sem = refs[groups + (1 if aliased else 0) :]
+def place_kernel(pieces, scal, *refs):
+    chunks = refs[: len(pieces)]
+    out, sem = refs[-2:]
     copies = []
-    for part in range(groups):
-        members = chunks[part].shape[0]
+    for index, (field, part) in enumerate(pieces):
         copies.append(
             pltpu.make_async_copy(
-                chunks[part],
-                out.at[pl.ds(member, members), pl.ds(fields, 2), :, :, scal[0] ^ part],
-                sem.at[part],
+                chunks[index], out.at[:, pl.ds(field, 2), :, :, scal[0] ^ part], sem.at[index]
             )
         )
     for copy in copies:
@@ -320,7 +325,10 @@
     return out
 
 
-def call(kernel, name, scal, grid, inputs, outputs, scratch=(), aliases=None, limit=40):
+SPLIT_LIMIT = 40
+
+
+def call(kernel, name, scal, grid, inputs, outputs, scratch=(), aliases=None, limit=40, weight=1 / 1024):
     def spec(block, index):
         if block is None:
             return pl.BlockSpec(memory_space=pl.ANY)
@@ -346,7 +354,7 @@
         out_shape=[jax.ShapeDtypeStruct(s, F32) for s, _, _ in outputs],
         input_output_aliases=aliases or {},
         compiler_params=pltpu.CompilerParams(vmem_limit_bytes=limit * 1024 * 1024),
-        cost_estimate=pl.CostEstimate(flops=0, bytes_accessed=bytes_moved // 1024, transcendentals=0),
+        cost_estimate=pl.CostEstimate(flops=0, bytes_accessed=int(bytes_moved * weight), transcendentals=0),
         name=name,
     )(scal, *[a for a, _, _ in inputs])
 
@@ -365,11 +373,13 @@
     def swap(values):
         return lax.ppermute(values, "slab", partner)
 
-    def cross(values):
+    def cross(values, parts=range(1, groups)):
         def moved(part):
             return [(i, (i // groups) * groups + ((i % groups) ^ part)) for i in range(slabs)]
 
-        return [values[0]] + [lax.ppermute(values[part], "slab", moved(part)) for part in range(1, groups)]
+        return [values[0]] + [
+            lax.ppermute(values[part], "slab", moved(part)) if part in parts else None for part in range(1, groups)
+        ]
 
     to_next = [(i, (i // groups) * groups + (i % groups + 1) % groups) for i in range(slabs)]
     to_prev = [(b, a) for a, b in to_next]
@@ -380,20 +390,21 @@
     chunk_all = (members, 2, own, 2, rows, ny)
     chunk_level = (1, 2, 1, 2, rows, ny)
     v_send = call(
-        functools.partial(split_kernel, groups, rows),
+        functools.partial(split_kernel, groups),
         "split",
         scal,
-        (members, own),
-        [(ocean_state, (1, 2, 1, nx, ny), lambda m, l, s: (m, 1, l, 0, 0))],
-        [(chunk_all, chunk_level, lambda m, l, s: (m, 0, l, 0, 0, 0))] * groups,
-        limit=60,
-    )
+        (),
+        [(view, None, None)],
+        [(chunk_all, "VMEM", None)] * groups,
+        [pltpu.SemaphoreType.DMA((groups,))],
+        limit=SPLIT_LIMIT,
+    )
+    f_got = swap(surface_forcing)
     v_send, (diffusivity, bottom_drag, land_sea, bottom_level, ocean_late) = lax.optimization_barrier(
         (v_send, (diffusivity, bottom_drag, land_sea, bottom_level, ocean_state))
     )
     v_got = cross(v_send)
 
-    f_got = swap(surface_forcing)
     give, own_other = call(
         functools.partial(give_kernel, half_levels),
         "give",
@@ -526,9 +537,12 @@
 
     mine, shared = at(0)
     d_v, dm_v = first(v_got, 0, members, inv_v, (1, 2), False)
-    t_send, dm_v = lax.optimization_barrier((t_send, dm_v))
-    t_got = cross(t_send)
+    t_send, dm_v = lax.optimization_barrier((list(t_send), dm_v))
+    t_got = cross(t_send, range(1, groups - 1))
     dm_v_other = swap(dm_v)
+    t_send[-1], dm_v_other = lax.optimization_barrier((t_send[-1], dm_v_other))
+    t_got[-1] = cross(t_send, [groups - 1])[-1]
+    d_t, dm_t = first(t_got, 0, members, inv_t, (0, None), True)
     x_v, u_top, u_end, d2_v, dm2_v = call(
         middle_v_kernel,
         "middle_v",
@@ -551,19 +565,17 @@
             ((members, 2, 2, half_levels, rows, ny), state_block, mine(4)),
             ((members, 2, 2, rows, ny), pair_block, mine(3)),
         ],
+        weight=2,
     )
     dm2_v_other = swap(dm2_v)
-    u_before = lax.ppermute(u_end, "slab", to_next)
-    u_after = lax.ppermute(u_top, "slab", to_prev)
-    d2_v, u_before, u_after = lax.optimization_barrier((d2_v, u_before, u_after))
     out_v = last(d2_v, dm2_v_other, 0, members, inv_v, 1)
-    back_v = cross(out_v)
+    out_v, dm_t = lax.optimization_barrier((list(out_v), dm_t))
+    back_v = cross(out_v, range(1, groups - 1))
 
     back_t = []
     for m in range(1):
+        dm_t_other = swap(dm_t)
         mine, shared = at(m)
-        d_t, dm_t = first(t_got, m, members, inv_t, (0, None), True)
-        dm_t_other = swap(dm_t)
         x_t, t_top, t_end = call(
             middle_t_kernel,
             "middle_t",
@@ -576,15 +588,19 @@
                 (inv_t, col_block, shared(3)),
                 (mid, pair_block, shared(3)),
                 (mid_other, pair_block, shared(3)),
+                (u_top, (1, 1, half_levels, ny), mine(2)),
+                (u_end, (1, 1, half_levels, ny), mine(2)),
             ],
             [
                 ((members, 2, 2, half_levels, rows, ny), state_block, mine(4)),
-                ((members, 2, 2, half_levels, ny), (1, 1, 2, half_levels, ny), mine(3)),
-                ((members, 2, 2, half_levels, ny), (1, 1, 2, half_levels, ny), mine(3)),
+                ((members, 2, 3, half_levels, ny), (1, 1, 3, half_levels, ny), mine(3)),
+                ((members, 2, 3, half_levels, ny), (1, 1, 3, half_levels, ny), mine(3)),
             ],
         )
         t_before = lax.ppermute(t_end, "slab", to_next)
         t_after = lax.ppermute(t_top, "slab", to_prev)
+        out_v[-1], t_before, t_after = lax.optimization_barrier((out_v[-1], t_before, t_after))
+        back_v[-1] = cross(out_v, [groups - 1])[-1]
 
         def from_before(extra, m0):
             return lambda i, t, s: (i + m0, t ^ jnp.where(s[0] == 0, 1, 0)) + (0,) * extra
@@ -601,10 +617,8 @@
             [
                 (x_t, state_block, mine(4)),
                 (x_v, state_block, shared(4)),
-                (t_before, (1, 1, 2, half_levels, ny), from_before(3, 0)),
-                (t_after, (1, 1, 2, half_levels, ny), from_after(3, 0)),
-                (u_before, (1, 1, half_levels, ny), from_before(2, m)),
-                (u_after, (1, 1, half_levels, ny), from_after(2, m)),
+                (t_before, (1, 1, 3, half_levels, ny), from_before(3, 0)),
+                (t_after, (1, 1, 3, half_levels, ny), from_after(3, 0)),
                 (rate, col_block, shared(3)),
                 (inv_t, col_block, shared(3)),
                 (cell_t, (1, 1, rows, ny), shared(2)),
@@ -623,26 +637,21 @@
         back_t.append(cross(last(d2_t, swap(dm2_t), m, members, inv_t, 0)))
 
     whole = view.shape
-    sems = [pltpu.SemaphoreType.DMA((groups,))]
-    (result,) = call(
-        functools.partial(place_kernel, groups, 0, 2, False),
-        "place_v",
-        scal,
-        (),
-        [(c, "VMEM", None) for c in back_v],
-        [(whole, None, None)],
-        sems,
-    )
-    for m in range(1):
+    chunks = {(2, part): back_v[part] for part in range(groups)}
+    chunks.update({(0, part): back_t[0][part] for part in range(groups)})
+    pieces = list(chunks)
+    result = None
+    for some in (pieces[: groups + 1], pieces[groups + 1 : -1], pieces[-1:]):
+        held = [] if result is None else [(result, None, None)]
         (result,) = call(
-            functools.partial(place_kernel, groups, m, 0, True),
-            "place_t",
+            functools.partial(place_kernel, some),
+            "place",
             scal,
             (),
-            [(c, "VMEM", None) for c in back_t[m]] + [(result, None, None)],
+            [(chunks[piece], "VMEM", None) for piece in some] + held,
             [(whole, None, None)],
-            sems,
-            {groups + 1: 0},
+            [pltpu.SemaphoreType.DMA((len(some),))],
+            {len(some) + 1: 0} if held else None,
         )
     return result.reshape(ocean_state.shape)
 

time: 171 us -> 157 us (0.918)
  waiting for transfers between devices: 105 us -> 94.7 us
  starting transfers between devices: 27.2 us -> 24.1 us
  local copies, waits for them, and re-layouts: 3.2 us -> 5.41 us
    ppermute x2 -> x0, waiting for transfers between devices: 27.5 us -> none  [the longest x1 23.5 us: per_device(): u_before = lax.ppermute(u_end, 'slab', to_next)]
    ppermute x12, waiting for transfers between devices: 16.4 us -> 26.8 us  [cross(): lax.ppermute(values[part], 'slab', moved(part))]
    ppermute x6, waiting for transfers between devices: 45.4 us -> 53.2 us  [swap(): return lax.ppermute(values, 'slab', partner)]
    ppermute x12, starting transfers between devices: 14.1 us -> 8.26 us  [cross(): lax.ppermute(values[part], 'slab', moved(part))]
    ppermute x6, starting transfers between devices: 7.59 us -> 11 us  [swap(): return lax.ppermute(values, 'slab', partner)]
    unnamed x26 -> x28, local copies, waits for them, and re-layouts: 2.9 us -> 5.1 us
    pallas_call x13 -> x14, Pallas kernels: 31 us -> 29.4 us  [call(): pl.pallas_call(kernel, grid_spec=pltpu.PrefetchScalarGridSpec(num_scalar_...]
  transfers between devices with their start and end apart: 25 -> 23, of which waited for: 13 -> 13; matrix products, arithmetic and copies ran while one was open for 2% -> 2% of each run, Pallas kernels for 15% -> 14%
where the time goes in v3:
time: 157 us; the launch traced here: 156 us
  waiting for transfers between devices  94.7 us (60%)
  Pallas kernels  29.4 us (19%)
  starting transfers between devices  24.1 us (15%)
  local copies, waits for them, and re-layouts  5.41 us (3%)
  other arithmetic  2.3 us (1%)
    ppermute x6, waiting for transfers between devices, swap(): return lax.ppermute(values, 'slab', partner)  53.2 us
    pallas_call x14, Pallas kernels, call(): pl.pallas_call(kernel, grid_spec=pltpu.PrefetchScalarGridSpec(num_scalar_...  29.4 us
    ppermute x12, waiting for transfers between devices, cross(): lax.ppermute(values[part], 'slab', moved(part))  26.8 us
    ppermute x6, starting transfers between devices, swap(): return lax.ppermute(values, 'slab', partner)  11 us
    ppermute x3, waiting for transfers between devices, per_device(): lax.ppermute(f_tiles, 'member', [(i, (i + step) % places) for i in range(...  8.44 us
    ppermute x12, starting transfers between devices, cross(): lax.ppermute(values[part], 'slab', moved(part))  8.26 us
    ppermute x1, waiting for transfers between devices, per_device(): t_before = lax.ppermute(t_end, 'slab', to_next)  6.32 us
    unnamed x28, local copies, waits for them, and re-layouts  5.1 us
  transfers between devices with their start and end apart: 23, of which 13 were waited for; matrix products, arithmetic and copies ran while one was open for 2% of the time, Pallas kernels for 14%

profile of v3, /device:TPU:0, one launch (start us, length us, event | category | flops | bytes accessed | tf_op | source)
XLA Modules:
  0.0 156.3 jit_solution(8502311879708266626)
XLA Ops:
  0.0 4.0 %collective-permute-start.4 = (f32[2,3,32,64]{3,2,1,0:T(8,128)}, f32[2,3,32,64]{3,2,1,0:T(8,128)S(1)}, u32[]{:S(2)}, u32[]{:S(2)}) collective-permute-start(f32[2,3,32,64]{3,2,1,0:T(8,128)} %param.9), channel_id=1, source_target_pairs={{0,4},{1,5},{2,6},{3,7},{4,0},{5,1},{6,2},{7,3},{8,12},{9,13},{10,... | collective-permute-start | bytes 147464 | tf_op jit(solution)/shard_map/ppermute | solution.py:374
  4.1 2.2 %copy-done = f32[2,4,2,256,256]{4,3,2,1,0:T(8,128)S(1)} copy-done((f32[2,4,2,256,256]{4,3,2,1,0:T(8,128)S(1)}, f32[2,4,2,256,256]{4,3,2,1,0:T(8,128)}, u32[]{:S(2)}) %copy-start) | copy-done | bytes 4194328
  6.3 1.9 %split.1 = (f32[2,2,2,2,32,256]{5,4,3,2,1,0:T(8,128)S(1)}, f32[2,2,2,2,32,256]{5,4,3,2,1,0:T(8,128)}, f32[2,2,2,2,32,256]{5,4,3,2,1,0:T(8,128)}, f32[2,2,2,2,32,256]{5,4,3,2,1,0:T(8,128)}) custom-call(s32[3]{0:T(128)S(1)} %pad_add_fusion.1.scal, f32[2,4,2,2,4,32,256]{6,5,4,3,2,1,0:T(8,128)S(1)} %bitcast.28), custom_call_target="tpu_custom_call" | custom-call | bytes 2048 | tf_op jit(solution)/shard_map/split/pallas_call | solution.py:345
  11.8 1.9 %give.1 = (f32[2,11,32,256]{3,2,1,0:T(8,128)}, f32[2,2,32,256]{3,2,1,0:T(8,128)S(1)}) custom-call(s32[3]{0:T(128)S(1)} %pad_add_fusion.1.scal, f32[2,16,32,256]{3,2,1,0:T(8,128)S(1)} %copy-done.2, f32[2,32,256]{2,1,0:T(8,128)S(1)} %copy-done.7, s32[2,256,256]{2,1,0:T(8,128)S(1)} %copy-done.4, s32[2,256,256]{2,1,0:T(8,128)S(1)} %copy-done.3), custom_call_target="tpu_custom_call" | custom-call | bytes 2944 | tf_op jit(solution)/shard_map/give/pallas_call | solution.py:345
  14.8 5.0 %collective-permute-done.7 = f32[2,3,2,32,64]{4,3,2,1,0:T(8,128)S(1)} collective-permute-done((f32[2,3,2,32,64]{4,3,2,1,0:T(8,128)}, f32[2,3,2,32,64]{4,3,2,1,0:T(8,128)S(1)}, u32[]{:S(2)}, u32[]{:S(2)}) %collective-permute-start.7) | collective-permute-done | bytes 98336 | tf_op jit(solution)/shard_map/ppermute | solution.py:431
  20.5 1.8 %collective-permute-start.6 = (f32[2,3,2,32,64]{4,3,2,1,0:T(8,128)}, f32[2,3,2,32,64]{4,3,2,1,0:T(8,128)}, u32[]{:S(2)}, u32[]{:S(2)}) collective-permute-start(f32[2,3,2,32,64]{4,3,2,1,0:T(8,128)} %maximum_select_fusion), channel_id=1, source_target_pairs={{0,16},{8,24},{16,0},{24,8},{1,17},{9,25},{17,1},{25,9},{2,18},{10... | collective-permute-start | bytes 294920 | tf_op jit(solution)/shard_map/ppermute | solution.py:431
  22.5 2.2 %copy-done.1 = f32[2,4,2,256,256]{4,3,2,1,0:T(8,128)S(1)} copy-done((f32[2,4,2,256,256]{4,3,2,1,0:T(8,128)S(1)}, f32[2,4,2,256,256]{4,3,2,1,0:T(8,128)}, u32[]{:S(2)}) %copy-start.1) | copy-done | bytes 4194328
  24.6 5.3 %advect.1 = (f32[2,2,2,2,32,256]{5,4,3,2,1,0:T(8,128)S(1)}, f32[2,2,2,2,32,256]{5,4,3,2,1,0:T(8,128)S(1)}, f32[2,2,2,2,32,256]{5,4,3,2,1,0:T(8,128)S(1)}, f32[2,2,2,2,32,256]{5,4,3,2,1,0:T(8,128)S(1)}) custom-call(s32[3]{0:T(128)S(1)} %pad_add_fusion.1.scal, f32[2,4,2,256,256]{4,3,2,1,0:T(8,128)S(1)} %copy-done.1, ...), custom_call_target="tpu_custom_call" | custom-call | bytes 7680 | tf_op jit(solution)/shard_map/advect/pallas_call | solution.py:345
  30.0 3.5 %collective-permute-done.5 = f32[2,3,2,32,64]{4,3,2,1,0:T(8,128)S(1)} collective-permute-done((f32[2,3,2,32,64]{4,3,2,1,0:T(8,128)}, f32[2,3,2,32,64]{4,3,2,1,0:T(8,128)S(1)}, u32[]{:S(2)}, u32[]{:S(2)}) %collective-permute-start.5) | collective-permute-done | bytes 98336 | tf_op jit(solution)/shard_map/ppermute | solution.py:431
  34.8 14.2 %collective-permute-done.3.got = f32[2,11,32,256]{3,2,1,0:T(8,128)S(1)} collective-permute-done((f32[2,11,32,256]{3,2,1,0:T(8,128)}, f32[2,11,32,256]{3,2,1,0:T(8,128)S(1)}, u32[]{:S(2)}, u32[]{:S(2)}) %collective-permute-start.3) | collective-permute-done | bytes 720928 | tf_op jit(solution)/shard_map/ppermute | solution.py:374
  50.3 3.2 %first.2 = (f32[2,2,2,8,32,256]{5,4,3,2,1,0:T(8,128)S(1)}, f32[2,2,2,32,256]{4,3,2,1,0:T(8,128)S(1)}) custom-call(s32[3]{0:T(128)S(1)} %pad_add_fusion.1.scal, f32[2,2,2,2,32,256]{5,4,3,2,1,0:T(8,128)S(1)} %copy-done.6, f32[2,2,2,2,32,256]{5,4,3,2,1,0:T(8,128)} %collective-permute-done.refs_1_, f32[2,2,2,2,32,256]{5,4,3,2,1,0:T(8,128)} %collective-permute-done.1.refs_2_, ...), custom_call_target="tpu_custom_call" | custom-call | bytes 6912 | tf_op jit(solution)/shard_map/first/pallas_call | solution.py:345
  53.5 3.3 %collective-permute-start.10 = (f32[2,2,2,32,256]{4,3,2,1,0:T(8,128)S(1)}, f32[2,2,2,32,256]{4,3,2,1,0:T(8,128)S(1)}, u32[]{:S(2)}, u32[]{:S(2)}) collective-permute-start(f32[2,2,2,32,256]{4,3,2,1,0:T(8,128)S(1)} %get-tuple-element.105), channel_id=1, source_target_pairs={{0,4},{1,5},{2,6},{3,7},{4,0},{5,1},{6,2},{7,3},{8,12},{9,13},{10,... | collective-permute-start | bytes 786440 | tf_op jit(solution)/shard_map/ppermute | solution.py:374
  57.4 10.0 %collective-permute-done.10.other = f32[2,2,2,32,256]{4,3,2,1,0:T(8,128)S(1)} collective-permute-done((f32[2,2,2,32,256]{4,3,2,1,0:T(8,128)S(1)}, f32[2,2,2,32,256]{4,3,2,1,0:T(8,128)S(1)}, u32[]{:S(2)}, u32[]{:S(2)}) %collective-permute-start.10) | collective-permute-done | bytes 262176 | tf_op jit(solution)/shard_map/ppermute | solution.py:374
  68.6 1.9 %collective-permute-start.12 = (f32[2,2,2,32,256]{4,3,2,1,0:T(8,128)S(1)}, f32[2,2,2,32,256]{4,3,2,1,0:T(8,128)S(1)}, u32[]{:S(2)}, u32[]{:S(2)}) collective-permute-start(f32[2,2,2,32,256]{4,3,2,1,0:T(8,128)S(1)} %get-tuple-element.114), channel_id=1, source_target_pairs={{0,4},{1,5},{2,6},{3,7},{4,0},{5,1},{6,2},{7,3},{8,12},{9,13},{10,... | collective-permute-start | bytes 786440 | tf_op jit(solution)/shard_map/ppermute | solution.py:374
  70.4 18.6 %collective-permute-done.12.other = f32[2,2,2,32,256]{4,3,2,1,0:T(8,128)S(1)} collective-permute-done((f32[2,2,2,32,256]{4,3,2,1,0:T(8,128)S(1)}, f32[2,2,2,32,256]{4,3,2,1,0:T(8,128)S(1)}, u32[]{:S(2)}, u32[]{:S(2)}) %collective-permute-start.12) | collective-permute-done | bytes 262176 | tf_op jit(solution)/shard_map/ppermute | solution.py:374
  90.3 1.8 %collective-permute-done.11.refs_3_ = f32[2,2,2,2,32,256]{5,4,3,2,1,0:T(8,128)S(1)} collective-permute-done((f32[2,2,2,2,32,256]{5,4,3,2,1,0:T(8,128)S(1)}, f32[2,2,2,2,32,256]{5,4,3,2,1,0:T(8,128)S(1)}, u32[]{:S(2)}, u32[]{:S(2)}) %collective-permute-start.11) | collective-permute-done | bytes 524320 | tf_op jit(solution)/shard_map/ppermute | solution.py:381
  95.6 9.0 %collective-permute-done.13.other = f32[2,2,2,32,256]{4,3,2,1,0:T(8,128)S(1)} collective-permute-done((f32[2,2,2,32,256]{4,3,2,1,0:T(8,128)S(1)}, f32[2,2,2,32,256]{4,3,2,1,0:T(8,128)S(1)}, u32[]{:S(2)}, u32[]{:S(2)}) %collective-permute-start.13) | collective-permute-done | bytes 262176 | tf_op jit(solution)/shard_map/ppermute | solution.py:374
  108.6 6.3 %collective-permute-done.16.before = f32[2,2,3,8,256]{4,3,2,1,0:T(8,128)S(1)} collective-permute-done((f32[2,2,3,8,256]{4,3,2,1,0:T(8,128)S(1)}, f32[2,2,3,8,256]{4,3,2,1,0:T(8,128)S(1)}, u32[]{:S(2)}, u32[]{:S(2)}) %collective-permute-start.16) | collective-permute-done | bytes 98336 | tf_op jit(solution)/shard_map/ppermute | solution.py:600
  115.2 5.0 %second_t.1 = (f32[2,2,2,8,32,256]{5,4,3,2,1,0:T(8,128)S(1)}, f32[2,2,2,32,256]{4,3,2,1,0:T(8,128)S(1)}) custom-call(s32[3]{0:T(128)S(1)} %pad_add_fusion.1.scal, f32[2,2,2,8,32,256]{5,4,3,2,1,0:T(8,128)S(1)} %get-tuple-element.126.x_ref, f32[2,2,2,8,32,256]{5,4,3,2,1,0:T(8,128)S(1)} %get-tuple-element.127.v_ref, ...), custom_call_target="tpu_custom_call" | custom-call | bytes 9412 | tf_op jit(solution)/shard_map/second_t/pallas_call | solution.py:345
  120.3 10.7 %collective-permute-done.18.refs_3_ = f32[2,2,2,2,32,256]{5,4,3,2,1,0:T(8,128)S(1)} collective-permute-done((f32[2,2,2,2,32,256]{5,4,3,2,1,0:T(8,128)S(1)}, f32[2,2,2,2,32,256]{5,4,3,2,1,0:T(8,128)S(1)}, u32[]{:S(2)}, u32[]{:S(2)}) %collective-permute-start.18) | collective-permute-done | bytes 524320 | tf_op jit(solution)/shard_map/ppermute | solution.py:381
  134.4 2.7 %collective-permute-start.20 = (f32[2,2,2,2,32,256]{5,4,3,2,1,0:T(8,128)S(1)}, f32[2,2,2,2,32,256]{5,4,3,2,1,0:T(8,128)S(1)}, u32[]{:S(2)}, u32[]{:S(2)}) collective-permute-start(f32[2,2,2,2,32,256]{5,4,3,2,1,0:T(8,128)S(1)} %get-tuple-element.137), channel_id=1, source_target_pairs={{0,3},{1,2},{2,1},{3,0},{4,7},{5,6},{6,5},{7,4},{8,11},{9,10},{10,... | collective-permute-start | bytes 1572872 | tf_op jit(solution)/shard_map/ppermute | solution.py:381
  137.1 2.1 %place.3.refs_2_ = f32[2,4,2,2,4,32,256]{6,5,4,3,2,1,0:T(8,128)} custom-call(s32[3]{0:T(128)S(1)} %pad_add_fusion.1.scal, f32[2,2,2,2,32,256]{5,4,3,2,1,0:T(8,128)S(1)} %get-tuple-element.140.refs_0_, f32[2,2,2,2,32,256]{5,4,3,2,1,0:T(8,128)S(1)} %collective-permute-done.14.refs_1_, f32[2,2,2,2,32,256]{5,4,3,2,1,0:T(8,128)S(1)} %collective-permute-done.15.refs_2_, ...), custom_call_target="tpu_custom_call" | custom-call | bytes 6656 | tf_op jit(solution)/shard_map/place/pallas_call | solution.py:345
  139.2 8.9 %collective-permute-done.21.refs_0_ = f32[2,2,2,2,32,256]{5,4,3,2,1,0:T(8,128)S(1)} collective-permute-done((f32[2,2,2,2,32,256]{5,4,3,2,1,0:T(8,128)S(1)}, f32[2,2,2,2,32,256]{5,4,3,2,1,0:T(8,128)S(1)}, u32[]{:S(2)}, u32[]{:S(2)}) %collective-permute-start.21) | collective-permute-done | bytes 524320 | tf_op jit(solution)/shard_map/ppermute | solution.py:381
  150.7 4.3 %collective-permute-done.20.refs_0_ = f32[2,2,2,2,32,256]{5,4,3,2,1,0:T(8,128)S(1)} collective-permute-done((f32[2,2,2,2,32,256]{5,4,3,2,1,0:T(8,128)S(1)}, f32[2,2,2,2,32,256]{5,4,3,2,1,0:T(8,128)S(1)}, u32[]{:S(2)}, u32[]{:S(2)}) %collective-permute-start.20) | collective-permute-done | bytes 524320 | tf_op jit(solution)/shard_map/ppermute | solution.py:381
  (79 shorter events, 26.3 us)
Async XLA Ops:
  0.0 13.7 %collective-permute-start.4 = (f32[2,3,32,64]{3,2,1,0:T(8,128)}, f32[2,3,32,64]{3,2,1,0:T(8,128)S(1)}, u32[]{:S(2)}, u32[]{:S(2)}) collective-permute-start(f32[2,3,32,64]{3,2,1,0:T(8,128)} %param.9), channel_id=1, source_target_pairs={{0,4},{1,5},{2,6},{3,7},{4,0},{5,1},{6,2},{7,3},{8,12},{9,13},{10,... | collective-permute-start | bytes 147464 | tf_op jit(solution)/shard_map/ppermute | solution.py:374
  8.2 42.1 %collective-permute-start = (f32[2,2,2,2,32,256]{5,4,3,2,1,0:T(8,128)}, f32[2,2,2,2,32,256]{5,4,3,2,1,0:T(8,128)}, u32[]{:S(2)}, u32[]{:S(2)}) collective-permute-start(f32[2,2,2,2,32,256]{5,4,3,2,1,0:T(8,128)} %get-tuple-element.93), channel_id=1, source_target_pairs={{0,1},{1,0},{2,3},{3,2},{4,5},{5,4},{6,7},{7,6},{8,9},{9,8},{10,11... | collective-permute-start | bytes 1572872 | tf_op jit(solution)/shard_map/ppermute | solution.py:381
  9.8 40.5 %collective-permute-start.1 = (f32[2,2,2,2,32,256]{5,4,3,2,1,0:T(8,128)}, f32[2,2,2,2,32,256]{5,4,3,2,1,0:T(8,128)}, u32[]{:S(2)}, u32[]{:S(2)}) collective-permute-start(f32[2,2,2,2,32,256]{5,4,3,2,1,0:T(8,128)} %get-tuple-element.94), channel_id=1, source_target_pairs={{0,2},{1,3},{2,0},{3,1},{4,6},{5,7},{6,4},{7,5},{8,10},{9,11},{10,... | collective-permute-start | bytes 1572872 | tf_op jit(solution)/shard_map/ppermute | solution.py:381
  11.4 38.9 %collective-permute-start.2 = (f32[2,2,2,2,32,256]{5,4,3,2,1,0:T(8,128)}, f32[2,2,2,2,32,256]{5,4,3,2,1,0:T(8,128)}, u32[]{:S(2)}, u32[]{:S(2)}) collective-permute-start(f32[2,2,2,2,32,256]{5,4,3,2,1,0:T(8,128)} %get-tuple-element.95), channel_id=1, source_target_pairs={{0,3},{1,2},{2,1},{3,0},{4,7},{5,6},{6,5},{7,4},{8,11},{9,10},{10,... | collective-permute-start | bytes 1572872 | tf_op jit(solution)/shard_map/ppermute | solution.py:381
  13.7 35.3 %collective-permute-start.3 = (f32[2,11,32,256]{3,2,1,0:T(8,128)}, f32[2,11,32,256]{3,2,1,0:T(8,128)S(1)}, u32[]{:S(2)}, u32[]{:S(2)}) collective-permute-start(f32[2,11,32,256]{3,2,1,0:T(8,128)} %get-tuple-element.96), channel_id=1, source_target_pairs={{0,4},{1,5},{2,6},{3,7},{4,0},{5,1},{6,2},{7,3},{8,12},{9,13},{10,... | collective-permute-start | bytes 2162696 | tf_op jit(solution)/shard_map/ppermute | solution.py:374
  14.5 5.3 %collective-permute-start.7 = (f32[2,3,2,32,64]{4,3,2,1,0:T(8,128)}, f32[2,3,2,32,64]{4,3,2,1,0:T(8,128)S(1)}, u32[]{:S(2)}, u32[]{:S(2)}) collective-permute-start(f32[2,3,2,32,64]{4,3,2,1,0:T(8,128)} %maximum_select_fusion), channel_id=1, source_target_pairs={{0,8},{8,16},{16,24},{24,0},{1,9},{9,17},{17,25},{25,1},{2,10},{10... | collective-permute-start | bytes 294920 | tf_op jit(solution)/shard_map/ppermute | solution.py:431
  20.5 9.5 %collective-permute-start.6 = (f32[2,3,2,32,64]{4,3,2,1,0:T(8,128)}, f32[2,3,2,32,64]{4,3,2,1,0:T(8,128)}, u32[]{:S(2)}, u32[]{:S(2)}) collective-permute-start(f32[2,3,2,32,64]{4,3,2,1,0:T(8,128)} %maximum_select_fusion), channel_id=1, source_target_pairs={{0,16},{8,24},{16,0},{24,8},{1,17},{9,25},{17,1},{25,9},{2,18},{10... | collective-permute-start | bytes 294920 | tf_op jit(solution)/shard_map/ppermute | solution.py:431
  29.9 3.6 %collective-permute-start.5 = (f32[2,3,2,32,64]{4,3,2,1,0:T(8,128)}, f32[2,3,2,32,64]{4,3,2,1,0:T(8,128)S(1)}, u32[]{:S(2)}, u32[]{:S(2)}) collective-permute-start(f32[2,3,2,32,64]{4,3,2,1,0:T(8,128)} %maximum_select_fusion), channel_id=1, source_target_pairs={{0,24},{8,0},{16,8},{24,16},{1,25},{9,1},{17,9},{25,17},{2,26},{10... | collective-permute-start | bytes 294920 | tf_op jit(solution)/shard_map/ppermute | solution.py:431
  30.0 20.3 %copy-start.6 = (f32[2,2,2,2,32,256]{5,4,3,2,1,0:T(8,128)S(1)}, f32[2,2,2,2,32,256]{5,4,3,2,1,0:T(8,128)}, u32[]{:S(2)}) copy-start(f32[2,2,2,2,32,256]{5,4,3,2,1,0:T(8,128)} %copy-done.5) | copy-start | bytes 1572868
  53.5 13.8 %collective-permute-start.10 = (f32[2,2,2,32,256]{4,3,2,1,0:T(8,128)S(1)}, f32[2,2,2,32,256]{4,3,2,1,0:T(8,128)S(1)}, u32[]{:S(2)}, u32[]{:S(2)}) collective-permute-start(f32[2,2,2,32,256]{4,3,2,1,0:T(8,128)S(1)} %get-tuple-element.105), channel_id=1, source_target_pairs={{0,4},{1,5},{2,6},{3,7},{4,0},{5,1},{6,2},{7,3},{8,12},{9,13},{10,... | collective-permute-start | bytes 786440 | tf_op jit(solution)/shard_map/ppermute | solution.py:374
  56.8 33.4 %collective-permute-start.8 = (f32[2,2,2,2,32,256]{5,4,3,2,1,0:T(8,128)S(1)}, f32[2,2,2,2,32,256]{5,4,3,2,1,0:T(8,128)S(1)}, u32[]{:S(2)}, u32[]{:S(2)}) collective-permute-start(f32[2,2,2,2,32,256]{5,4,3,2,1,0:T(8,128)S(1)} %get-tuple-element.102), channel_id=1, source_target_pairs={{0,1},{1,0},{2,3},{3,2},{4,5},{5,4},{6,7},{7,6},{8,9},{9,8},{10,11... | collective-permute-start | bytes 1572872 | tf_op jit(solution)/shard_map/ppermute | solution.py:381
  57.4 32.9 %collective-permute-start.9 = (f32[2,2,2,2,32,256]{5,4,3,2,1,0:T(8,128)S(1)}, f32[2,2,2,2,32,256]{5,4,3,2,1,0:T(8,128)S(1)}, u32[]{:S(2)}, u32[]{:S(2)}) collective-permute-start(f32[2,2,2,2,32,256]{5,4,3,2,1,0:T(8,128)S(1)} %get-tuple-element.103), channel_id=1, source_target_pairs={{0,2},{1,3},{2,0},{3,1},{4,6},{5,7},{6,4},{7,5},{8,10},{9,11},{10,... | collective-permute-start | bytes 1572872 | tf_op jit(solution)/shard_map/ppermute | solution.py:381
  67.3 24.8 %collective-permute-start.11 = (f32[2,2,2,2,32,256]{5,4,3,2,1,0:T(8,128)S(1)}, f32[2,2,2,2,32,256]{5,4,3,2,1,0:T(8,128)S(1)}, u32[]{:S(2)}, u32[]{:S(2)}) collective-permute-start(f32[2,2,2,2,32,256]{5,4,3,2,1,0:T(8,128)S(1)} %get-tuple-element.106), channel_id=1, source_target_pairs={{0,3},{1,2},{2,1},{3,0},{4,7},{5,6},{6,5},{7,4},{8,11},{9,10},{10,... | collective-permute-start | bytes 1572872 | tf_op jit(solution)/shard_map/ppermute | solution.py:381
  68.6 20.5 %collective-permute-start.12 = (f32[2,2,2,32,256]{4,3,2,1,0:T(8,128)S(1)}, f32[2,2,2,32,256]{4,3,2,1,0:T(8,128)S(1)}, u32[]{:S(2)}, u32[]{:S(2)}) collective-permute-start(f32[2,2,2,32,256]{4,3,2,1,0:T(8,128)S(1)} %get-tuple-element.114), channel_id=1, source_target_pairs={{0,4},{1,5},{2,6},{3,7},{4,0},{5,1},{6,2},{7,3},{8,12},{9,13},{10,... | collective-permute-start | bytes 786440 | tf_op jit(solution)/shard_map/ppermute | solution.py:374
  93.5 11.2 %collective-permute-start.13 = (f32[2,2,2,32,256]{4,3,2,1,0:T(8,128)S(1)}, f32[2,2,2,32,256]{4,3,2,1,0:T(8,128)S(1)}, u32[]{:S(2)}, u32[]{:S(2)}) collective-permute-start(f32[2,2,2,32,256]{4,3,2,1,0:T(8,128)S(1)} %get-tuple-element.120), channel_id=1, source_target_pairs={{0,4},{1,5},{2,6},{3,7},{4,0},{5,1},{6,2},{7,3},{8,12},{9,13},{10,... | collective-permute-start | bytes 786440 | tf_op jit(solution)/shard_map/ppermute | solution.py:374
  95.1 20.1 %collective-permute-start.14 = (f32[2,2,2,2,32,256]{5,4,3,2,1,0:T(8,128)S(1)}, f32[2,2,2,2,32,256]{5,4,3,2,1,0:T(8,128)S(1)}, u32[]{:S(2)}, u32[]{:S(2)}) collective-permute-start(f32[2,2,2,2,32,256]{5,4,3,2,1,0:T(8,128)S(1)} %get-tuple-element.124), channel_id=1, source_target_pairs={{0,1},{1,0},{2,3},{3,2},{4,5},{5,4},{6,7},{7,6},{8,9},{9,8},{10,11... | collective-permute-start | bytes 1572872 | tf_op jit(solution)/shard_map/ppermute | solution.py:381
  95.6 19.6 %collective-permute-start.15 = (f32[2,2,2,2,32,256]{5,4,3,2,1,0:T(8,128)S(1)}, f32[2,2,2,2,32,256]{5,4,3,2,1,0:T(8,128)S(1)}, u32[]{:S(2)}, u32[]{:S(2)}) collective-permute-start(f32[2,2,2,2,32,256]{5,4,3,2,1,0:T(8,128)S(1)} %get-tuple-element.125), channel_id=1, source_target_pairs={{0,2},{1,3},{2,0},{3,1},{4,6},{5,7},{6,4},{7,5},{8,10},{9,11},{10,... | collective-permute-start | bytes 1572872 | tf_op jit(solution)/shard_map/ppermute | solution.py:381
  105.6 9.3 %collective-permute-start.16 = (f32[2,2,3,8,256]{4,3,2,1,0:T(8,128)S(1)}, f32[2,2,3,8,256]{4,3,2,1,0:T(8,128)S(1)}, u32[]{:S(2)}, u32[]{:S(2)}) collective-permute-start(f32[2,2,3,8,256]{4,3,2,1,0:T(8,128)S(1)} %get-tuple-element.129), channel_id=1, source_target_pairs={{0,1},{1,2},{2,3},{3,0},{4,5},{5,6},{6,7},{7,4},{8,9},{9,10},{10,1... | collective-permute-start | bytes 294920 | tf_op jit(solution)/shard_map/ppermute | solution.py:600
  106.9 8.0 %collective-permute-start.17 = (f32[2,2,3,8,256]{4,3,2,1,0:T(8,128)S(1)}, f32[2,2,3,8,256]{4,3,2,1,0:T(8,128)S(1)}, u32[]{:S(2)}, u32[]{:S(2)}) collective-permute-start(f32[2,2,3,8,256]{4,3,2,1,0:T(8,128)S(1)} %get-tuple-element.130), channel_id=1, source_target_pairs={{1,0},{2,1},{3,2},{0,3},{5,4},{6,5},{7,6},{4,7},{9,8},{10,9},{11,1... | collective-permute-start | bytes 294920 | tf_op jit(solution)/shard_map/ppermute | solution.py:601
  114.9 16.0 %collective-permute-start.18 = (f32[2,2,2,2,32,256]{5,4,3,2,1,0:T(8,128)S(1)}, f32[2,2,2,2,32,256]{5,4,3,2,1,0:T(8,128)S(1)}, u32[]{:S(2)}, u32[]{:S(2)}) collective-permute-start(f32[2,2,2,2,32,256]{5,4,3,2,1,0:T(8,128)S(1)} %get-tuple-element.134), channel_id=1, source_target_pairs={{0,3},{1,2},{2,1},{3,0},{4,7},{5,6},{6,5},{7,4},{8,11},{9,10},{10,... | collective-permute-start | bytes 1572872 | tf_op jit(solution)/shard_map/ppermute | solution.py:381
  120.2 12.1 %collective-permute-start.19 = (f32[2,2,2,32,256]{4,3,2,1,0:T(8,128)S(1)}, f32[2,2,2,32,256]{4,3,2,1,0:T(8,128)S(1)}, u32[]{:S(2)}, u32[]{:S(2)}) collective-permute-start(f32[2,2,2,32,256]{4,3,2,1,0:T(8,128)S(1)} %get-tuple-element.136), channel_id=1, source_target_pairs={{0,4},{1,5},{2,6},{3,7},{4,0},{5,1},{6,2},{7,3},{8,12},{9,13},{10,... | collective-permute-start | bytes 786440 | tf_op jit(solution)/shard_map/ppermute | solution.py:374
  133.6 14.5 %collective-permute-start.21 = (f32[2,2,2,2,32,256]{5,4,3,2,1,0:T(8,128)S(1)}, f32[2,2,2,2,32,256]{5,4,3,2,1,0:T(8,128)S(1)}, u32[]{:S(2)}, u32[]{:S(2)}) collective-permute-start(f32[2,2,2,2,32,256]{5,4,3,2,1,0:T(8,128)S(1)} %get-tuple-element.138), channel_id=1, source_target_pairs={{0,1},{1,0},{2,3},{3,2},{4,5},{5,4},{6,7},{7,6},{8,9},{9,8},{10,11... | collective-permute-start | bytes 1572872 | tf_op jit(solution)/shard_map/ppermute | solution.py:381
  134.4 14.7 %collective-permute-start.22 = (f32[2,2,2,2,32,256]{5,4,3,2,1,0:T(8,128)S(1)}, f32[2,2,2,2,32,256]{5,4,3,2,1,0:T(8,128)S(1)}, u32[]{:S(2)}, u32[]{:S(2)}) collective-permute-start(f32[2,2,2,2,32,256]{5,4,3,2,1,0:T(8,128)S(1)} %get-tuple-element.139), channel_id=1, source_target_pairs={{0,2},{1,3},{2,0},{3,1},{4,6},{5,7},{6,4},{7,5},{8,10},{9,11},{10,... | collective-permute-start | bytes 1572872 | tf_op jit(solution)/shard_map/ppermute | solution.py:381
  134.4 20.6 %collective-permute-start.20 = (f32[2,2,2,2,32,256]{5,4,3,2,1,0:T(8,128)S(1)}, f32[2,2,2,2,32,256]{5,4,3,2,1,0:T(8,128)S(1)}, u32[]{:S(2)}, u32[]{:S(2)}) collective-permute-start(f32[2,2,2,2,32,256]{5,4,3,2,1,0:T(8,128)S(1)} %get-tuple-element.137), channel_id=1, source_target_pairs={{0,3},{1,2},{2,1},{3,0},{4,7},{5,6},{6,5},{7,4},{8,11},{9,10},{10,... | collective-permute-start | bytes 1572872 | tf_op jit(solution)/shard_map/ppermute | solution.py:381
  (13 other events, 65.4 us)

commit v4 on v3

--- a/solution.py
+++ b/solution.py
@@ -196,17 +196,18 @@
     return jnp.where(scal[1] == 0, spot, half_levels - 1 - spot)
 
 
-def first_kernel(groups, levels_own, force_ids, masked, scal, *refs):
+def first_kernel(parts, levels_own, force_ids, masked, scal, *refs):
+    groups = len(parts)
     chunks = refs[:groups]
     rate, inv, cell_n, forcing, d_ref, mid_ref, buf = refs[groups:]
     half_levels = rate.shape[2]
     count = cell_n[0, 0]
-    for part in range(groups):
+    for chunk, part in zip(chunks, parts):
         for lev in range(levels_own):
             slot = slot_of(scal, part, lev, levels_own, half_levels)
             level = scal[1] * half_levels + (scal[0] ^ part) * levels_own + lev
             for f in range(2):
-                value = chunks[part][0, f, lev, 0]
+                value = chunk[0, f, lev, 0]
                 buf[f, slot] = value if masked else jnp.where(level < count, value, 0.0)
 
     def rhs(e, f):
@@ -394,7 +395,7 @@
         "split",
         scal,
         (),
-        [(view, None, None)],
+        [(pltpu.with_memory_space_constraint(view, pltpu.HBM), None, None)],
         [(chunk_all, "VMEM", None)] * groups,
         [pltpu.SemaphoreType.DMA((groups,))],
         limit=SPLIT_LIMIT,
@@ -458,6 +459,10 @@
         [(chunk_all, chunk_level, lambda m, l, s: (m, 0, l, 0, 0, 0))] * groups,
     )
 
+    t_send = list(t_send)
+    t_send[:-1], got, forcing = lax.optimization_barrier((t_send[:-1], got, forcing))
+    t_got = cross(t_send, range(1, groups - 1))
+
     col_shape = (members, 2, half_levels, rows, ny)
     col_block = (1, 1, half_levels, rows, ny)
     mid_shape = (members, 2, 2, rows, ny)
@@ -470,8 +475,8 @@
         [
             (diffusivity, (1, levels, rows, ny), lambda m, t, s: (m, 0, 0, 0)),
             (got, (1, half_levels + 3, rows, ny), lambda m, t, s: (m, 0, 0, 0)),
-            (bottom_drag, (1, rows, ny), lambda m, t, s: (m, 0, 0)),
-            (own_other, (1, 2, rows, ny), lambda m, t, s: (m, 0, 0, 0)),
+            (pltpu.with_memory_space_constraint(bottom_drag, pltpu.HBM), (1, rows, ny), lambda m, t, s: (m, 0, 0)),
+            (pltpu.with_memory_space_constraint(own_other, pltpu.HBM), (1, 2, rows, ny), lambda m, t, s: (m, 0, 0, 0)),
             (cell_t, (1, 1, rows, ny), lambda m, t, s: (m, t, 0, 0)),
         ],
         [
@@ -495,14 +500,14 @@
 
         return mine, shared
 
-    def first(chunks, m0, count, inv, force_ids, masked):
+    def first(chunks, m0, count, inv, force_ids, masked, parts):
         mine, shared = at(m0)
         return call(
-            functools.partial(first_kernel, groups, own, force_ids, masked),
+            functools.partial(first_kernel, tuple(parts), own, force_ids, masked),
             "first",
             scal,
             (count, 2),
-            [(c, (1, 2, own, 1, rows, ny), lambda m, t, s: (m + m0, 0, 0, t, 0, 0)) for c in chunks]
+            [(c, (1, 2, own, 1, rows, ny), lambda m, t, s: (m + m0, 0, 0, t, 0, 0)) for c in (chunks[p] for p in parts)]
             + [
                 (rate, col_block, shared(3)),
                 (inv, col_block, shared(3)),
@@ -514,6 +519,7 @@
                 ((count, 2, 2, rows, ny), pair_block, mine(3)),
             ],
             [pltpu.VMEM((2, half_levels, rows, ny), F32)],
+            weight=4,
         )
 
     def last(d, other, m0, count, inv, kind):
@@ -536,13 +542,12 @@
         )
 
     mine, shared = at(0)
-    d_v, dm_v = first(v_got, 0, members, inv_v, (1, 2), False)
-    t_send, dm_v = lax.optimization_barrier((list(t_send), dm_v))
-    t_got = cross(t_send, range(1, groups - 1))
+    d_v, dm_v = first(v_got, 0, members, inv_v, (1, 2), False, [0, groups - 1] + list(range(1, groups - 1)))
     dm_v_other = swap(dm_v)
-    t_send[-1], dm_v_other = lax.optimization_barrier((t_send[-1], dm_v_other))
+    t_send[-1], dm_v = lax.optimization_barrier((t_send[-1], dm_v))
+    dm_v_other, t_got[1:-1] = lax.optimization_barrier((dm_v_other, t_got[1:-1]))
     t_got[-1] = cross(t_send, [groups - 1])[-1]
-    d_t, dm_t = first(t_got, 0, members, inv_t, (0, None), True)
+    d_t, dm_t = first(t_got, 0, members, inv_t, (0, None), True, range(groups))
     x_v, u_top, u_end, d2_v, dm2_v = call(
         middle_v_kernel,
         "middle_v",

time: 157 us -> 155 us (0.987)
  waiting for transfers between devices: 94.7 us -> 82.9 us
  starting transfers between devices: 24.1 us -> 30.9 us
  Pallas kernels: 29.4 us -> 35.1 us
  local copies, waits for them, and re-layouts: 5.41 us -> 3.36 us
    ppermute x6, waiting for transfers between devices: 53.2 us -> 36.4 us  [swap(): return lax.ppermute(values, 'slab', partner)]
    ppermute x12, waiting for transfers between devices: 26.8 us -> 38.9 us  [cross(): lax.ppermute(values[part], 'slab', moved(part))]
    ppermute x3, waiting for transfers between devices: 8.44 us -> 0.01 us  [per_device(): lax.ppermute(f_tiles, 'member', [(i, (i + step) % places) for i in range(...]
    ppermute x12, starting transfers between devices: 8.26 us -> 14 us  [cross(): lax.ppermute(values[part], 'slab', moved(part))]
    pallas_call x14, Pallas kernels: 29.4 us -> 35.1 us  [call(): pl.pallas_call(kernel, grid_spec=pltpu.PrefetchScalarGridSpec(num_scalar_...]
    unnamed x28, local copies, waits for them, and re-layouts: 5.1 us -> 3.06 us
    ppermute x1, starting transfers between devices: 1.26 us -> 2.89 us  [per_device(): t_before = lax.ppermute(t_end, 'slab', to_next)]
    ppermute x1, starting transfers between devices: 1.72 us -> 0.08 us  [per_device(): t_after = lax.ppermute(t_top, 'slab', to_prev)]
  transfers between devices with their start and end apart: 23 -> 23, of which waited for: 13 -> 10; matrix products, arithmetic and copies ran while one was open for 2% -> 1% of each run, Pallas kernels for 14% -> 20%
where the time goes in v4:
time: 155 us; the launch traced here: 154 us
  waiting for transfers between devices  82.9 us (53%)
  Pallas kernels  35.1 us (23%)
  starting transfers between devices  30.9 us (20%)
  local copies, waits for them, and re-layouts  3.36 us (2%)
  other arithmetic  1.68 us (1%)
    ppermute x12, waiting for transfers between devices, cross(): lax.ppermute(values[part], 'slab', moved(part))  38.9 us
    ppermute x6, waiting for transfers between devices, swap(): return lax.ppermute(values, 'slab', partner)  36.4 us
    pallas_call x14, Pallas kernels, call(): pl.pallas_call(kernel, grid_spec=pltpu.PrefetchScalarGridSpec(num_scalar_...  35.1 us
    ppermute x12, starting transfers between devices, cross(): lax.ppermute(values[part], 'slab', moved(part))  14 us
    ppermute x6, starting transfers between devices, swap(): return lax.ppermute(values, 'slab', partner)  11 us
    ppermute x1, waiting for transfers between devices, per_device(): t_before = lax.ppermute(t_end, 'slab', to_next)  7.63 us
  transfers between devices with their start and end apart: 23, of which 10 were waited for; matrix products, arithmetic and copies ran while one was open for 1% of the time, Pallas kernels for 20%

profile of v4, /device:TPU:0, one launch (start us, length us, event | category | flops | bytes accessed | tf_op | source)
XLA Modules:
  0.0 154.3 jit_solution(3466167329058813466)
XLA Ops:
  0.0 4.0 %collective-permute-start.1 = (f32[2,3,32,64]{3,2,1,0:T(8,128)}, f32[2,3,32,64]{3,2,1,0:T(8,128)S(1)}, u32[]{:S(2)}, u32[]{:S(2)}) collective-permute-start(f32[2,3,32,64]{3,2,1,0:T(8,128)} %param.9), channel_id=1, source_target_pairs={{0,4},{1,5},{2,6},{3,7},{4,0},{5,1},{6,2},{7,3},{8,12},{9,13},{10,... | collective-permute-start | bytes 147464 | tf_op jit(solution)/shard_map/ppermute | solution.py:375
  4.1 3.4 %split.1 = (f32[2,2,2,2,32,256]{5,4,3,2,1,0:T(8,128)S(1)}, f32[2,2,2,2,32,256]{5,4,3,2,1,0:T(8,128)}, f32[2,2,2,2,32,256]{5,4,3,2,1,0:T(8,128)}, f32[2,2,2,2,32,256]{5,4,3,2,1,0:T(8,128)}) custom-call(s32[3]{0:T(128)S(1)} %pad_add_fusion.1.scal, f32[2,4,2,2,4,32,256]{6,5,4,3,2,1,0:T(8,128)} %bitcast.28), custom_call_target="tpu_custom_call" | custom-call | bytes 2048 | tf_op jit(solution)/shard_map/split/pallas_call | solution.py:346
  7.5 2.6 %collective-permute-start.5 = (f32[2,2,2,2,32,256]{5,4,3,2,1,0:T(8,128)}, f32[2,2,2,2,32,256]{5,4,3,2,1,0:T(8,128)}, u32[]{:S(2)}, u32[]{:S(2)}) collective-permute-start(f32[2,2,2,2,32,256]{5,4,3,2,1,0:T(8,128)} %get-tuple-element.96), channel_id=1, source_target_pairs={{0,3},{1,2},{2,1},{3,0},{4,7},{5,6},{6,5},{7,4},{8,11},{9,10},{10,... | collective-permute-start | bytes 1572872 | tf_op jit(solution)/shard_map/ppermute | solution.py:382
  10.2 1.9 %give.1 = (f32[2,11,32,256]{3,2,1,0:T(8,128)}, f32[2,2,32,256]{3,2,1,0:T(8,128)S(1)}) custom-call(s32[3]{0:T(128)S(1)} %pad_add_fusion.1.scal, f32[2,16,32,256]{3,2,1,0:T(8,128)S(1)} %copy-done.1, f32[2,32,256]{2,1,0:T(8,128)S(1)} %copy-done.6, s32[2,256,256]{2,1,0:T(8,128)S(1)} %copy-done.3, s32[2,256,256]{2,1,0:T(8,128)S(1)} %copy-done.2), custom_call_target="tpu_custom_call" | custom-call | bytes 2944 | tf_op jit(solution)/shard_map/give/pallas_call | solution.py:346
  16.8 2.2 %copy-done = f32[2,4,2,256,256]{4,3,2,1,0:T(8,128)S(1)} copy-done((f32[2,4,2,256,256]{4,3,2,1,0:T(8,128)S(1)}, f32[2,4,2,256,256]{4,3,2,1,0:T(8,128)}, u32[]{:S(2)}) %copy-start) | copy-done | bytes 4194328
  19.0 5.9 %advect.1 = (f32[2,2,2,2,32,256]{5,4,3,2,1,0:T(8,128)S(1)}, f32[2,2,2,2,32,256]{5,4,3,2,1,0:T(8,128)}, f32[2,2,2,2,32,256]{5,4,3,2,1,0:T(8,128)}, f32[2,2,2,2,32,256]{5,4,3,2,1,0:T(8,128)S(1)}) custom-call(s32[3]{0:T(128)S(1)} %pad_add_fusion.1.scal, f32[2,4,2,256,256]{4,3,2,1,0:T(8,128)S(1)} %copy-done, s32[2,256,256]{2,1,0:T(8,128)S(1)} %compare_select_fusion.cell_n, ...), custom_call_target="tpu_custom_call" | custom-call | bytes 7680 | tf_op jit(solution)/shard_map/advect/pallas_call | solution.py:346
  27.4 19.5 %collective-permute-done.got = f32[2,11,32,256]{3,2,1,0:T(8,128)} collective-permute-done((f32[2,11,32,256]{3,2,1,0:T(8,128)}, f32[2,11,32,256]{3,2,1,0:T(8,128)}, u32[]{:S(2)}, u32[]{:S(2)}) %collective-permute-start) | collective-permute-done | bytes 720928 | tf_op jit(solution)/shard_map/ppermute | solution.py:375
  47.4 3.1 %factor.1 = (f32[2,2,8,32,256]{4,3,2,1,0:T(8,128)S(1)}, f32[2,2,8,32,256]{4,3,2,1,0:T(8,128)S(1)}, f32[2,2,8,32,256]{4,3,2,1,0:T(8,128)S(1)}, f32[2,2,2,32,256]{4,3,2,1,0:T(8,128)S(1)}, f32[2,2,2,32,256]{4,3,2,1,0:T(8,128)S(1)}) custom-call(s32[3]{0:T(128)S(1)} %pad_add_fusion.1.scal, f32[2,16,32,256]{3,2,1,0:T(8,128)S(1)} %copy-done.1, ...), custom_call_target="tpu_custom_call" | custom-call | bytes 5632 | tf_op jit(solution)/shard_map/factor/pallas_call | solution.py:346
  50.5 3.2 %first.2 = (f32[2,2,2,8,32,256]{5,4,3,2,1,0:T(8,128)S(1)}, f32[2,2,2,32,256]{4,3,2,1,0:T(8,128)S(1)}) custom-call(s32[3]{0:T(128)S(1)} %pad_add_fusion.1.scal, f32[2,2,2,2,32,256]{5,4,3,2,1,0:T(8,128)S(1)} %get-tuple-element.95.refs_0_, f32[2,2,2,2,32,256]{5,4,3,2,1,0:T(8,128)} %collective-permute-done.5.refs_1_, ...), custom_call_target="tpu_custom_call" | custom-call | bytes 28311552 | tf_op jit(solution)/shard_map/first/pallas_call | solution.py:346
  54.5 2.3 %collective-permute-start.11 = (f32[2,2,2,2,32,256]{5,4,3,2,1,0:T(8,128)S(1)}, f32[2,2,2,2,32,256]{5,4,3,2,1,0:T(8,128)S(1)}, u32[]{:S(2)}, u32[]{:S(2)}) collective-permute-start(f32[2,2,2,2,32,256]{5,4,3,2,1,0:T(8,128)S(1)} %copy-done.9), channel_id=1, source_target_pairs={{0,3},{1,2},{2,1},{3,0},{4,7},{5,6},{6,5},{7,4},{8,11},{9,10},{10,... | collective-permute-start | bytes 1572872 | tf_op jit(solution)/shard_map/ppermute | solution.py:382
  56.8 9.5 %collective-permute-done.8.other = f32[2,2,2,32,256]{4,3,2,1,0:T(8,128)S(1)} collective-permute-done((f32[2,2,2,32,256]{4,3,2,1,0:T(8,128)S(1)}, f32[2,2,2,32,256]{4,3,2,1,0:T(8,128)S(1)}, u32[]{:S(2)}, u32[]{:S(2)}) %collective-permute-start.8) | collective-permute-done | bytes 262176 | tf_op jit(solution)/shard_map/ppermute | solution.py:375
  71.0 9.8 %collective-permute-done.11.refs_3_ = f32[2,2,2,2,32,256]{5,4,3,2,1,0:T(8,128)S(1)} collective-permute-done((f32[2,2,2,2,32,256]{5,4,3,2,1,0:T(8,128)S(1)}, f32[2,2,2,2,32,256]{5,4,3,2,1,0:T(8,128)S(1)}, u32[]{:S(2)}, u32[]{:S(2)}) %collective-permute-start.11) | collective-permute-done | bytes 524320 | tf_op jit(solution)/shard_map/ppermute | solution.py:382
  80.8 3.0 %first.3 = (f32[2,2,2,8,32,256]{5,4,3,2,1,0:T(8,128)S(1)}, f32[2,2,2,32,256]{4,3,2,1,0:T(8,128)S(1)}) custom-call(s32[3]{0:T(128)S(1)} %pad_add_fusion.1.scal, f32[2,2,2,2,32,256]{5,4,3,2,1,0:T(8,128)S(1)} %copy-done.5, f32[2,2,2,2,32,256]{5,4,3,2,1,0:T(8,128)} %collective-permute-done.9.refs_1_, f32[2,2,2,2,32,256]{5,4,3,2,1,0:T(8,128)} %collective-permute-done.10.refs_2_, ...), custom_call_target="tpu_custom_call" | custom-call | bytes 28311552 | tf_op jit(solution)/shard_map/first/pallas_call | solution.py:346
  88.4 2.3 %collective-permute-start.15 = (f32[2,2,2,2,32,256]{5,4,3,2,1,0:T(8,128)S(1)}, f32[2,2,2,2,32,256]{5,4,3,2,1,0:T(8,128)S(1)}, u32[]{:S(2)}, u32[]{:S(2)}) collective-permute-start(f32[2,2,2,2,32,256]{5,4,3,2,1,0:T(8,128)S(1)} %get-tuple-element.129), channel_id=1, source_target_pairs={{0,2},{1,3},{2,0},{3,1},{4,6},{5,7},{6,4},{7,5},{8,10},{9,11},{10,... | collective-permute-start | bytes 1572872 | tf_op jit(solution)/shard_map/ppermute | solution.py:382
  90.7 7.4 %collective-permute-done.13.other = f32[2,2,2,32,256]{4,3,2,1,0:T(8,128)S(1)} collective-permute-done((f32[2,2,2,32,256]{4,3,2,1,0:T(8,128)S(1)}, f32[2,2,2,32,256]{4,3,2,1,0:T(8,128)S(1)}, u32[]{:S(2)}, u32[]{:S(2)}) %collective-permute-start.13) | collective-permute-done | bytes 262176 | tf_op jit(solution)/shard_map/ppermute | solution.py:375
  99.1 2.9 %collective-permute-start.16 = (f32[2,2,3,8,256]{4,3,2,1,0:T(8,128)S(1)}, f32[2,2,3,8,256]{4,3,2,1,0:T(8,128)S(1)}, u32[]{:S(2)}, u32[]{:S(2)}) collective-permute-start(f32[2,2,3,8,256]{4,3,2,1,0:T(8,128)S(1)} %get-tuple-element.133), channel_id=1, source_target_pairs={{0,1},{1,2},{2,3},{3,0},{4,5},{5,6},{6,7},{7,4},{8,9},{9,10},{10,1... | collective-permute-start | bytes 294920 | tf_op jit(solution)/shard_map/ppermute | solution.py:605
  102.1 7.6 %collective-permute-done.16.before = f32[2,2,3,8,256]{4,3,2,1,0:T(8,128)S(1)} collective-permute-done((f32[2,2,3,8,256]{4,3,2,1,0:T(8,128)S(1)}, f32[2,2,3,8,256]{4,3,2,1,0:T(8,128)S(1)}, u32[]{:S(2)}, u32[]{:S(2)}) %collective-permute-start.16) | collective-permute-done | bytes 98336 | tf_op jit(solution)/shard_map/ppermute | solution.py:605
  109.8 5.0 %second_t.1 = (f32[2,2,2,8,32,256]{5,4,3,2,1,0:T(8,128)S(1)}, f32[2,2,2,32,256]{4,3,2,1,0:T(8,128)S(1)}) custom-call(s32[3]{0:T(128)S(1)} %pad_add_fusion.1.scal, f32[2,2,2,8,32,256]{5,4,3,2,1,0:T(8,128)S(1)} %get-tuple-element.130.x_ref, f32[2,2,2,8,32,256]{5,4,3,2,1,0:T(8,128)S(1)} %get-tuple-element.131.v_ref, ...), custom_call_target="tpu_custom_call" | custom-call | bytes 9412 | tf_op jit(solution)/shard_map/second_t/pallas_call | solution.py:346
  114.9 2.5 %collective-permute-start.19 = (f32[2,2,2,32,256]{4,3,2,1,0:T(8,128)S(1)}, f32[2,2,2,32,256]{4,3,2,1,0:T(8,128)S(1)}, u32[]{:S(2)}, u32[]{:S(2)}) collective-permute-start(f32[2,2,2,32,256]{4,3,2,1,0:T(8,128)S(1)} %get-tuple-element.140), channel_id=1, source_target_pairs={{0,4},{1,5},{2,6},{3,7},{4,0},{5,1},{6,2},{7,3},{8,12},{9,13},{10,... | collective-permute-start | bytes 786440 | tf_op jit(solution)/shard_map/ppermute | solution.py:375
  117.4 10.0 %collective-permute-done.18.refs_3_ = f32[2,2,2,2,32,256]{5,4,3,2,1,0:T(8,128)S(1)} collective-permute-done((f32[2,2,2,2,32,256]{5,4,3,2,1,0:T(8,128)S(1)}, f32[2,2,2,2,32,256]{5,4,3,2,1,0:T(8,128)S(1)}, u32[]{:S(2)}, u32[]{:S(2)}) %collective-permute-start.18) | collective-permute-done | bytes 524320 | tf_op jit(solution)/shard_map/ppermute | solution.py:382
  132.2 2.1 %place.3.refs_2_ = f32[2,4,2,2,4,32,256]{6,5,4,3,2,1,0:T(8,128)} custom-call(s32[3]{0:T(128)S(1)} %pad_add_fusion.1.scal, f32[2,2,2,2,32,256]{5,4,3,2,1,0:T(8,128)S(1)} %get-tuple-element.144.refs_0_, f32[2,2,2,2,32,256]{5,4,3,2,1,0:T(8,128)S(1)} %collective-permute-done.14.refs_1_, f32[2,2,2,2,32,256]{5,4,3,2,1,0:T(8,128)S(1)} %collective-permute-done.15.refs_2_, ...), custom_call_target="tpu_custom_call" | custom-call | bytes 6656 | tf_op jit(solution)/shard_map/place/pallas_call | solution.py:346
  134.3 5.2 %collective-permute-done.21.refs_0_ = f32[2,2,2,2,32,256]{5,4,3,2,1,0:T(8,128)S(1)} collective-permute-done((f32[2,2,2,2,32,256]{5,4,3,2,1,0:T(8,128)S(1)}, f32[2,2,2,2,32,256]{5,4,3,2,1,0:T(8,128)S(1)}, u32[]{:S(2)}, u32[]{:S(2)}) %collective-permute-start.21) | collective-permute-done | bytes 524320 | tf_op jit(solution)/shard_map/ppermute | solution.py:382
  139.4 5.4 %collective-permute-done.22.refs_1_ = f32[2,2,2,2,32,256]{5,4,3,2,1,0:T(8,128)S(1)} collective-permute-done((f32[2,2,2,2,32,256]{5,4,3,2,1,0:T(8,128)S(1)}, f32[2,2,2,2,32,256]{5,4,3,2,1,0:T(8,128)S(1)}, u32[]{:S(2)}, u32[]{:S(2)}) %collective-permute-start.22) | collective-permute-done | bytes 524320 | tf_op jit(solution)/shard_map/ppermute | solution.py:382
  146.4 6.6 %collective-permute-done.20.refs_0_ = f32[2,2,2,2,32,256]{5,4,3,2,1,0:T(8,128)S(1)} collective-permute-done((f32[2,2,2,2,32,256]{5,4,3,2,1,0:T(8,128)S(1)}, f32[2,2,2,2,32,256]{5,4,3,2,1,0:T(8,128)S(1)}, u32[]{:S(2)}, u32[]{:S(2)}) %collective-permute-start.20) | collective-permute-done | bytes 524320 | tf_op jit(solution)/shard_map/ppermute | solution.py:382
  (79 shorter events, 26.5 us)
Async XLA Ops:
  0.0 13.4 %collective-permute-start.1 = (f32[2,3,32,64]{3,2,1,0:T(8,128)}, f32[2,3,32,64]{3,2,1,0:T(8,128)S(1)}, u32[]{:S(2)}, u32[]{:S(2)}) collective-permute-start(f32[2,3,32,64]{3,2,1,0:T(8,128)} %param.9), channel_id=1, source_target_pairs={{0,4},{1,5},{2,6},{3,7},{4,0},{5,1},{6,2},{7,3},{8,12},{9,13},{10,... | collective-permute-start | bytes 147464 | tf_op jit(solution)/shard_map/ppermute | solution.py:375
  7.5 43.0 %collective-permute-start.5 = (f32[2,2,2,2,32,256]{5,4,3,2,1,0:T(8,128)}, f32[2,2,2,2,32,256]{5,4,3,2,1,0:T(8,128)}, u32[]{:S(2)}, u32[]{:S(2)}) collective-permute-start(f32[2,2,2,2,32,256]{5,4,3,2,1,0:T(8,128)} %get-tuple-element.96), channel_id=1, source_target_pairs={{0,3},{1,2},{2,1},{3,0},{4,7},{5,6},{6,5},{7,4},{8,11},{9,10},{10,... | collective-permute-start | bytes 1572872 | tf_op jit(solution)/shard_map/ppermute | solution.py:382
  12.7 34.1 %collective-permute-start = (f32[2,11,32,256]{3,2,1,0:T(8,128)}, f32[2,11,32,256]{3,2,1,0:T(8,128)}, u32[]{:S(2)}, u32[]{:S(2)}) collective-permute-start(f32[2,11,32,256]{3,2,1,0:T(8,128)} %get-tuple-element.93), channel_id=1, source_target_pairs={{0,4},{1,5},{2,6},{3,7},{4,0},{5,1},{6,2},{7,3},{8,12},{9,13},{10,... | collective-permute-start | bytes 2162696 | tf_op jit(solution)/shard_map/ppermute | solution.py:375
  13.6 11.3 %collective-permute-start.4 = (f32[2,3,2,32,64]{4,3,2,1,0:T(8,128)S(1)}, f32[2,3,2,32,64]{4,3,2,1,0:T(8,128)S(1)}, u32[]{:S(2)}, u32[]{:S(2)}) collective-permute-start(f32[2,3,2,32,64]{4,3,2,1,0:T(8,128)S(1)} %maximum_select_fusion), channel_id=1, source_target_pairs={{0,8},{8,16},{16,24},{24,0},{1,9},{9,17},{17,25},{25,1},{2,10},{10... | collective-permute-start | bytes 294920 | tf_op jit(solution)/shard_map/ppermute | solution.py:432
  13.7 11.8 %collective-permute-start.3 = (f32[2,3,2,32,64]{4,3,2,1,0:T(8,128)S(1)}, f32[2,3,2,32,64]{4,3,2,1,0:T(8,128)}, u32[]{:S(2)}, u32[]{:S(2)}) collective-permute-start(f32[2,3,2,32,64]{4,3,2,1,0:T(8,128)S(1)} %maximum_select_fusion), channel_id=1, source_target_pairs={{0,16},{8,24},{16,0},{24,8},{1,17},{9,25},{17,1},{25,9},{2,18},{10... | collective-permute-start | bytes 294920 | tf_op jit(solution)/shard_map/ppermute | solution.py:432
  15.3 10.7 %collective-permute-start.2 = (f32[2,3,2,32,64]{4,3,2,1,0:T(8,128)S(1)}, f32[2,3,2,32,64]{4,3,2,1,0:T(8,128)}, u32[]{:S(2)}, u32[]{:S(2)}) collective-permute-start(f32[2,3,2,32,64]{4,3,2,1,0:T(8,128)S(1)} %maximum_select_fusion), channel_id=1, source_target_pairs={{0,24},{8,0},{16,8},{24,16},{1,25},{9,1},{17,9},{25,17},{2,26},{10... | collective-permute-start | bytes 294920 | tf_op jit(solution)/shard_map/ppermute | solution.py:432
  24.9 25.6 %collective-permute-start.6 = (f32[2,2,2,2,32,256]{5,4,3,2,1,0:T(8,128)}, f32[2,2,2,2,32,256]{5,4,3,2,1,0:T(8,128)}, u32[]{:S(2)}, u32[]{:S(2)}) collective-permute-start(f32[2,2,2,2,32,256]{5,4,3,2,1,0:T(8,128)} %get-tuple-element.97), channel_id=1, source_target_pairs={{0,1},{1,0},{2,3},{3,2},{4,5},{5,4},{6,7},{7,6},{8,9},{9,8},{10,11... | collective-permute-start | bytes 1572872 | tf_op jit(solution)/shard_map/ppermute | solution.py:382
  25.5 25.0 %collective-permute-start.7 = (f32[2,2,2,2,32,256]{5,4,3,2,1,0:T(8,128)}, f32[2,2,2,2,32,256]{5,4,3,2,1,0:T(8,128)}, u32[]{:S(2)}, u32[]{:S(2)}) collective-permute-start(f32[2,2,2,2,32,256]{5,4,3,2,1,0:T(8,128)} %get-tuple-element.98), channel_id=1, source_target_pairs={{0,2},{1,3},{2,0},{3,1},{4,6},{5,7},{6,4},{7,5},{8,10},{9,11},{10,... | collective-permute-start | bytes 1572872 | tf_op jit(solution)/shard_map/ppermute | solution.py:382
  46.9 19.5 %collective-permute-start.9 = (f32[2,2,2,2,32,256]{5,4,3,2,1,0:T(8,128)}, f32[2,2,2,2,32,256]{5,4,3,2,1,0:T(8,128)}, u32[]{:S(2)}, u32[]{:S(2)}) collective-permute-start(f32[2,2,2,2,32,256]{5,4,3,2,1,0:T(8,128)} %get-tuple-element.105), channel_id=1, source_target_pairs={{0,1},{1,0},{2,3},{3,2},{4,5},{5,4},{6,7},{7,6},{8,9},{9,8},{10,11... | collective-permute-start | bytes 1572872 | tf_op jit(solution)/shard_map/ppermute | solution.py:382
  47.4 20.8 %collective-permute-start.10 = (f32[2,2,2,2,32,256]{5,4,3,2,1,0:T(8,128)}, f32[2,2,2,2,32,256]{5,4,3,2,1,0:T(8,128)}, u32[]{:S(2)}, u32[]{:S(2)}) collective-permute-start(f32[2,2,2,2,32,256]{5,4,3,2,1,0:T(8,128)} %get-tuple-element.106), channel_id=1, source_target_pairs={{0,2},{1,3},{2,0},{3,1},{4,6},{5,7},{6,4},{7,5},{8,10},{9,11},{10,... | collective-permute-start | bytes 1572872 | tf_op jit(solution)/shard_map/ppermute | solution.py:382
  53.7 12.6 %collective-permute-start.8 = (f32[2,2,2,32,256]{4,3,2,1,0:T(8,128)S(1)}, f32[2,2,2,32,256]{4,3,2,1,0:T(8,128)S(1)}, u32[]{:S(2)}, u32[]{:S(2)}) collective-permute-start(f32[2,2,2,32,256]{4,3,2,1,0:T(8,128)S(1)} %get-tuple-element.104), channel_id=1, source_target_pairs={{0,4},{1,5},{2,6},{3,7},{4,0},{5,1},{6,2},{7,3},{8,12},{9,13},{10,... | collective-permute-start | bytes 786440 | tf_op jit(solution)/shard_map/ppermute | solution.py:375
  54.5 26.3 %collective-permute-start.11 = (f32[2,2,2,2,32,256]{5,4,3,2,1,0:T(8,128)S(1)}, f32[2,2,2,2,32,256]{5,4,3,2,1,0:T(8,128)S(1)}, u32[]{:S(2)}, u32[]{:S(2)}) collective-permute-start(f32[2,2,2,2,32,256]{5,4,3,2,1,0:T(8,128)S(1)} %copy-done.9), channel_id=1, source_target_pairs={{0,3},{1,2},{2,1},{3,0},{4,7},{5,6},{6,5},{7,4},{8,11},{9,10},{10,... | collective-permute-start | bytes 1572872 | tf_op jit(solution)/shard_map/ppermute | solution.py:382
  68.2 12.7 %copy-start.5 = (f32[2,2,2,2,32,256]{5,4,3,2,1,0:T(8,128)S(1)}, f32[2,2,2,2,32,256]{5,4,3,2,1,0:T(8,128)}, u32[]{:S(2)}) copy-start(f32[2,2,2,2,32,256]{5,4,3,2,1,0:T(8,128)} %copy-done.4) | copy-start | bytes 1572868
  69.4 14.4 %collective-permute-start.12 = (f32[2,2,2,32,256]{4,3,2,1,0:T(8,128)S(1)}, f32[2,2,2,32,256]{4,3,2,1,0:T(8,128)S(1)}, u32[]{:S(2)}, u32[]{:S(2)}) collective-permute-start(f32[2,2,2,32,256]{4,3,2,1,0:T(8,128)S(1)} %get-tuple-element.118), channel_id=1, source_target_pairs={{0,4},{1,5},{2,6},{3,7},{4,0},{5,1},{6,2},{7,3},{8,12},{9,13},{10,... | collective-permute-start | bytes 786440 | tf_op jit(solution)/shard_map/ppermute | solution.py:375
  85.0 13.1 %collective-permute-start.13 = (f32[2,2,2,32,256]{4,3,2,1,0:T(8,128)S(1)}, f32[2,2,2,32,256]{4,3,2,1,0:T(8,128)S(1)}, u32[]{:S(2)}, u32[]{:S(2)}) collective-permute-start(f32[2,2,2,32,256]{4,3,2,1,0:T(8,128)S(1)} %get-tuple-element.124), channel_id=1, source_target_pairs={{0,4},{1,5},{2,6},{3,7},{4,0},{5,1},{6,2},{7,3},{8,12},{9,13},{10,... | collective-permute-start | bytes 786440 | tf_op jit(solution)/shard_map/ppermute | solution.py:375
  86.7 23.1 %collective-permute-start.14 = (f32[2,2,2,2,32,256]{5,4,3,2,1,0:T(8,128)S(1)}, f32[2,2,2,2,32,256]{5,4,3,2,1,0:T(8,128)S(1)}, u32[]{:S(2)}, u32[]{:S(2)}) collective-permute-start(f32[2,2,2,2,32,256]{5,4,3,2,1,0:T(8,128)S(1)} %get-tuple-element.128), channel_id=1, source_target_pairs={{0,1},{1,0},{2,3},{3,2},{4,5},{5,4},{6,7},{7,6},{8,9},{9,8},{10,11... | collective-permute-start | bytes 1572872 | tf_op jit(solution)/shard_map/ppermute | solution.py:382
  88.4 21.4 %collective-permute-start.15 = (f32[2,2,2,2,32,256]{5,4,3,2,1,0:T(8,128)S(1)}, f32[2,2,2,2,32,256]{5,4,3,2,1,0:T(8,128)S(1)}, u32[]{:S(2)}, u32[]{:S(2)}) collective-permute-start(f32[2,2,2,2,32,256]{5,4,3,2,1,0:T(8,128)S(1)} %get-tuple-element.129), channel_id=1, source_target_pairs={{0,2},{1,3},{2,0},{3,1},{4,6},{5,7},{6,4},{7,5},{8,10},{9,11},{10,... | collective-permute-start | bytes 1572872 | tf_op jit(solution)/shard_map/ppermute | solution.py:382
  99.1 10.6 %collective-permute-start.16 = (f32[2,2,3,8,256]{4,3,2,1,0:T(8,128)S(1)}, f32[2,2,3,8,256]{4,3,2,1,0:T(8,128)S(1)}, u32[]{:S(2)}, u32[]{:S(2)}) collective-permute-start(f32[2,2,3,8,256]{4,3,2,1,0:T(8,128)S(1)} %get-tuple-element.133), channel_id=1, source_target_pairs={{0,1},{1,2},{2,3},{3,0},{4,5},{5,6},{6,7},{7,4},{8,9},{9,10},{10,1... | collective-permute-start | bytes 294920 | tf_op jit(solution)/shard_map/ppermute | solution.py:605
  102.0 7.7 %collective-permute-start.17 = (f32[2,2,3,8,256]{4,3,2,1,0:T(8,128)S(1)}, f32[2,2,3,8,256]{4,3,2,1,0:T(8,128)S(1)}, u32[]{:S(2)}, u32[]{:S(2)}) collective-permute-start(f32[2,2,3,8,256]{4,3,2,1,0:T(8,128)S(1)} %get-tuple-element.134), channel_id=1, source_target_pairs={{1,0},{2,1},{3,2},{0,3},{5,4},{6,5},{7,6},{4,7},{9,8},{10,9},{11,1... | collective-permute-start | bytes 294920 | tf_op jit(solution)/shard_map/ppermute | solution.py:606
  109.7 17.7 %collective-permute-start.18 = (f32[2,2,2,2,32,256]{5,4,3,2,1,0:T(8,128)S(1)}, f32[2,2,2,2,32,256]{5,4,3,2,1,0:T(8,128)S(1)}, u32[]{:S(2)}, u32[]{:S(2)}) collective-permute-start(f32[2,2,2,2,32,256]{5,4,3,2,1,0:T(8,128)S(1)} %get-tuple-element.138), channel_id=1, source_target_pairs={{0,3},{1,2},{2,1},{3,0},{4,7},{5,6},{6,5},{7,4},{8,11},{9,10},{10,... | collective-permute-start | bytes 1572872 | tf_op jit(solution)/shard_map/ppermute | solution.py:382
  114.9 12.6 %collective-permute-start.19 = (f32[2,2,2,32,256]{4,3,2,1,0:T(8,128)S(1)}, f32[2,2,2,32,256]{4,3,2,1,0:T(8,128)S(1)}, u32[]{:S(2)}, u32[]{:S(2)}) collective-permute-start(f32[2,2,2,32,256]{4,3,2,1,0:T(8,128)S(1)} %get-tuple-element.140), channel_id=1, source_target_pairs={{0,4},{1,5},{2,6},{3,7},{4,0},{5,1},{6,2},{7,3},{8,12},{9,13},{10,... | collective-permute-start | bytes 786440 | tf_op jit(solution)/shard_map/ppermute | solution.py:375
  128.6 10.8 %collective-permute-start.21 = (f32[2,2,2,2,32,256]{5,4,3,2,1,0:T(8,128)S(1)}, f32[2,2,2,2,32,256]{5,4,3,2,1,0:T(8,128)S(1)}, u32[]{:S(2)}, u32[]{:S(2)}) collective-permute-start(f32[2,2,2,2,32,256]{5,4,3,2,1,0:T(8,128)S(1)} %get-tuple-element.142), channel_id=1, source_target_pairs={{0,1},{1,0},{2,3},{3,2},{4,5},{5,4},{6,7},{7,6},{8,9},{9,8},{10,11... | collective-permute-start | bytes 1572872 | tf_op jit(solution)/shard_map/ppermute | solution.py:382
  130.0 14.9 %collective-permute-start.22 = (f32[2,2,2,2,32,256]{5,4,3,2,1,0:T(8,128)S(1)}, f32[2,2,2,2,32,256]{5,4,3,2,1,0:T(8,128)S(1)}, u32[]{:S(2)}, u32[]{:S(2)}) collective-permute-start(f32[2,2,2,2,32,256]{5,4,3,2,1,0:T(8,128)S(1)} %get-tuple-element.143), channel_id=1, source_target_pairs={{0,2},{1,3},{2,0},{3,1},{4,6},{5,7},{6,4},{7,5},{8,10},{9,11},{10,... | collective-permute-start | bytes 1572872 | tf_op jit(solution)/shard_map/ppermute | solution.py:382
  130.3 22.7 %collective-permute-start.20 = (f32[2,2,2,2,32,256]{5,4,3,2,1,0:T(8,128)S(1)}, f32[2,2,2,2,32,256]{5,4,3,2,1,0:T(8,128)S(1)}, u32[]{:S(2)}, u32[]{:S(2)}) collective-permute-start(f32[2,2,2,2,32,256]{5,4,3,2,1,0:T(8,128)S(1)} %get-tuple-element.141), channel_id=1, source_target_pairs={{0,3},{1,2},{2,1},{3,0},{4,7},{5,6},{6,5},{7,4},{8,11},{9,10},{10,... | collective-permute-start | bytes 1572872 | tf_op jit(solution)/shard_map/ppermute | solution.py:382
  (13 other events, 52.0 us)

commit v5 on v4

--- a/solution.py
+++ b/solution.py
@@ -451,7 +451,7 @@
         scal,
         (members, own),
         [
-            (ocean_late, (1, 4, 1, nx, ny), lambda m, l, s: (m, 0, l, 0, 0)),
+            (pltpu.with_memory_space_constraint(ocean_late, pltpu.HBM), (1, 4, 1, nx, ny), lambda m, l, s: (m, 0, l, 0, 0)),
             (cell_n, (1, nx, ny), lambda m, l, s: (m, 0, 0)),
             (zonal_n, (1, nx, ny), lambda m, l, s: (m, 0, 0)),
             (merid_n, (1, nx, ny), lambda m, l, s: (m, 0, 0)),

time: 155 us -> 155 us (level)
  local copies, waits for them, and re-layouts: 3.36 us -> 1.19 us
    unnamed x28 -> x26, local copies, waits for them, and re-layouts: 3.06 us -> 0.89 us
  transfers between devices with their start and end apart: 23 -> 23, of which waited for: 10 -> 10; matrix products, arithmetic and copies ran while one was open for 1% -> 1% of each run, Pallas kernels for 20% -> 21%
where the time goes in v5:
time: 155 us; the launch traced here: 154 us
  waiting for transfers between devices  84 us (54%)
  Pallas kernels  36.2 us (23%)
  starting transfers between devices  31 us (20%)
  other arithmetic  1.68 us (1%)
    ppermute x12, waiting for transfers between devices, cross(): lax.ppermute(values[part], 'slab', moved(part))  38.9 us
    ppermute x6, waiting for transfers between devices, swap(): return lax.ppermute(values, 'slab', partner)  37.4 us
    pallas_call x14, Pallas kernels, call(): pl.pallas_call(kernel, grid_spec=pltpu.PrefetchScalarGridSpec(num_scalar_...  36.2 us
    ppermute x12, starting transfers between devices, cross(): lax.ppermute(values[part], 'slab', moved(part))  14 us
    ppermute x6, starting transfers between devices, swap(): return lax.ppermute(values, 'slab', partner)  11 us
    ppermute x1, waiting for transfers between devices, per_device(): t_before = lax.ppermute(t_end, 'slab', to_next)  7.68 us
  transfers between devices with their start and end apart: 23, of which 10 were waited for; matrix products, arithmetic and copies ran while one was open for 1% of the time, Pallas kernels for 21%

profile of v5, /device:TPU:0, one launch (start us, length us, event | category | flops | bytes accessed | tf_op | source)
XLA Modules:
  0.0 154.4 jit_solution(9655024605656172283)
XLA Ops:
  0.0 4.0 %collective-permute-start.1 = (f32[2,3,32,64]{3,2,1,0:T(8,128)}, f32[2,3,32,64]{3,2,1,0:T(8,128)S(1)}, u32[]{:S(2)}, u32[]{:S(2)}) collective-permute-start(f32[2,3,32,64]{3,2,1,0:T(8,128)} %param.9), channel_id=1, source_target_pairs={{0,4},{1,5},{2,6},{3,7},{4,0},{5,1},{6,2},{7,3},{8,12},{9,13},{10,... | collective-permute-start | bytes 147464 | tf_op jit(solution)/shard_map/ppermute | solution.py:375
  4.1 3.4 %split.1 = (f32[2,2,2,2,32,256]{5,4,3,2,1,0:T(8,128)S(1)}, f32[2,2,2,2,32,256]{5,4,3,2,1,0:T(8,128)}, f32[2,2,2,2,32,256]{5,4,3,2,1,0:T(8,128)}, f32[2,2,2,2,32,256]{5,4,3,2,1,0:T(8,128)}) custom-call(s32[3]{0:T(128)S(1)} %pad_add_fusion.1.scal, f32[2,4,2,2,4,32,256]{6,5,4,3,2,1,0:T(8,128)} %bitcast.32), custom_call_target="tpu_custom_call" | custom-call | bytes 2048 | tf_op jit(solution)/shard_map/split/pallas_call | solution.py:346
  7.5 2.6 %collective-permute-start.5 = (f32[2,2,2,2,32,256]{5,4,3,2,1,0:T(8,128)}, f32[2,2,2,2,32,256]{5,4,3,2,1,0:T(8,128)}, u32[]{:S(2)}, u32[]{:S(2)}) collective-permute-start(f32[2,2,2,2,32,256]{5,4,3,2,1,0:T(8,128)} %get-tuple-element.96), channel_id=1, source_target_pairs={{0,3},{1,2},{2,1},{3,0},{4,7},{5,6},{6,5},{7,4},{8,11},{9,10},{10,... | collective-permute-start | bytes 1572872 | tf_op jit(solution)/shard_map/ppermute | solution.py:382
  10.1 1.9 %give.1 = (f32[2,11,32,256]{3,2,1,0:T(8,128)}, f32[2,2,32,256]{3,2,1,0:T(8,128)S(1)}) custom-call(s32[3]{0:T(128)S(1)} %pad_add_fusion.1.scal, f32[2,16,32,256]{3,2,1,0:T(8,128)S(1)} %copy-done, f32[2,32,256]{2,1,0:T(8,128)S(1)} %copy-done.5, s32[2,256,256]{2,1,0:T(8,128)S(1)} %copy-done.2, s32[2,256,256]{2,1,0:T(8,128)S(1)} %copy-done.1), custom_call_target="tpu_custom_call" | custom-call | bytes 2944 | tf_op jit(solution)/shard_map/give/pallas_call | solution.py:346
  16.8 7.1 %advect.1 = (f32[2,2,2,2,32,256]{5,4,3,2,1,0:T(8,128)S(1)}, f32[2,2,2,2,32,256]{5,4,3,2,1,0:T(8,128)}, f32[2,2,2,2,32,256]{5,4,3,2,1,0:T(8,128)}, f32[2,2,2,2,32,256]{5,4,3,2,1,0:T(8,128)S(1)}) custom-call(s32[3]{0:T(128)S(1)} %pad_add_fusion.1.scal, f32[2,4,2,256,256]{4,3,2,1,0:T(8,128)} %state, s32[2,256,256]{2,1,0:T(8,128)S(1)} %compare_select_fusion.cell_n, ...), custom_call_target="tpu_custom_call" | custom-call | bytes 7680 | tf_op jit(solution)/shard_map/advect/pallas_call | solution.py:346
  26.3 20.5 %collective-permute-done.got = f32[2,11,32,256]{3,2,1,0:T(8,128)} collective-permute-done((f32[2,11,32,256]{3,2,1,0:T(8,128)}, f32[2,11,32,256]{3,2,1,0:T(8,128)}, u32[]{:S(2)}, u32[]{:S(2)}) %collective-permute-start) | collective-permute-done | bytes 720928 | tf_op jit(solution)/shard_map/ppermute | solution.py:375
  47.3 3.1 %factor.1 = (f32[2,2,8,32,256]{4,3,2,1,0:T(8,128)S(1)}, f32[2,2,8,32,256]{4,3,2,1,0:T(8,128)S(1)}, f32[2,2,8,32,256]{4,3,2,1,0:T(8,128)S(1)}, f32[2,2,2,32,256]{4,3,2,1,0:T(8,128)S(1)}, f32[2,2,2,32,256]{4,3,2,1,0:T(8,128)S(1)}) custom-call(s32[3]{0:T(128)S(1)} %pad_add_fusion.1.scal, f32[2,16,32,256]{3,2,1,0:T(8,128)S(1)} %copy-done, ...), custom_call_target="tpu_custom_call" | custom-call | bytes 5632 | tf_op jit(solution)/shard_map/factor/pallas_call | solution.py:346
  50.5 3.2 %first.2 = (f32[2,2,2,8,32,256]{5,4,3,2,1,0:T(8,128)S(1)}, f32[2,2,2,32,256]{4,3,2,1,0:T(8,128)S(1)}) custom-call(s32[3]{0:T(128)S(1)} %pad_add_fusion.1.scal, f32[2,2,2,2,32,256]{5,4,3,2,1,0:T(8,128)S(1)} %get-tuple-element.95.refs_0_, f32[2,2,2,2,32,256]{5,4,3,2,1,0:T(8,128)} %collective-permute-done.5.refs_1_, ...), custom_call_target="tpu_custom_call" | custom-call | bytes 28311552 | tf_op jit(solution)/shard_map/first/pallas_call | solution.py:346
  54.5 2.3 %collective-permute-start.11 = (f32[2,2,2,2,32,256]{5,4,3,2,1,0:T(8,128)S(1)}, f32[2,2,2,2,32,256]{5,4,3,2,1,0:T(8,128)S(1)}, u32[]{:S(2)}, u32[]{:S(2)}) collective-permute-start(f32[2,2,2,2,32,256]{5,4,3,2,1,0:T(8,128)S(1)} %copy-done.8), channel_id=1, source_target_pairs={{0,3},{1,2},{2,1},{3,0},{4,7},{5,6},{6,5},{7,4},{8,11},{9,10},{10,... | collective-permute-start | bytes 1572872 | tf_op jit(solution)/shard_map/ppermute | solution.py:382
  56.8 9.5 %collective-permute-done.8.other = f32[2,2,2,32,256]{4,3,2,1,0:T(8,128)S(1)} collective-permute-done((f32[2,2,2,32,256]{4,3,2,1,0:T(8,128)S(1)}, f32[2,2,2,32,256]{4,3,2,1,0:T(8,128)S(1)}, u32[]{:S(2)}, u32[]{:S(2)}) %collective-permute-start.8) | collective-permute-done | bytes 262176 | tf_op jit(solution)/shard_map/ppermute | solution.py:375
  71.0 9.8 %collective-permute-done.11.refs_3_ = f32[2,2,2,2,32,256]{5,4,3,2,1,0:T(8,128)S(1)} collective-permute-done((f32[2,2,2,2,32,256]{5,4,3,2,1,0:T(8,128)S(1)}, f32[2,2,2,2,32,256]{5,4,3,2,1,0:T(8,128)S(1)}, u32[]{:S(2)}, u32[]{:S(2)}) %collective-permute-start.11) | collective-permute-done | bytes 524320 | tf_op jit(solution)/shard_map/ppermute | solution.py:382
  80.8 3.0 %first.3 = (f32[2,2,2,8,32,256]{5,4,3,2,1,0:T(8,128)S(1)}, f32[2,2,2,32,256]{4,3,2,1,0:T(8,128)S(1)}) custom-call(s32[3]{0:T(128)S(1)} %pad_add_fusion.1.scal, f32[2,2,2,2,32,256]{5,4,3,2,1,0:T(8,128)S(1)} %copy-done.4, f32[2,2,2,2,32,256]{5,4,3,2,1,0:T(8,128)} %collective-permute-done.9.refs_1_, f32[2,2,2,2,32,256]{5,4,3,2,1,0:T(8,128)} %collective-permute-done.10.refs_2_, ...), custom_call_target="tpu_custom_call" | custom-call | bytes 28311552 | tf_op jit(solution)/shard_map/first/pallas_call | solution.py:346
  88.4 2.3 %collective-permute-start.15 = (f32[2,2,2,2,32,256]{5,4,3,2,1,0:T(8,128)S(1)}, f32[2,2,2,2,32,256]{5,4,3,2,1,0:T(8,128)S(1)}, u32[]{:S(2)}, u32[]{:S(2)}) collective-permute-start(f32[2,2,2,2,32,256]{5,4,3,2,1,0:T(8,128)S(1)} %get-tuple-element.129), channel_id=1, source_target_pairs={{0,2},{1,3},{2,0},{3,1},{4,6},{5,7},{6,4},{7,5},{8,10},{9,11},{10,... | collective-permute-start | bytes 1572872 | tf_op jit(solution)/shard_map/ppermute | solution.py:382
  90.7 7.4 %collective-permute-done.13.other = f32[2,2,2,32,256]{4,3,2,1,0:T(8,128)S(1)} collective-permute-done((f32[2,2,2,32,256]{4,3,2,1,0:T(8,128)S(1)}, f32[2,2,2,32,256]{4,3,2,1,0:T(8,128)S(1)}, u32[]{:S(2)}, u32[]{:S(2)}) %collective-permute-start.13) | collective-permute-done | bytes 262176 | tf_op jit(solution)/shard_map/ppermute | solution.py:375
  99.0 2.9 %collective-permute-start.16 = (f32[2,2,3,8,256]{4,3,2,1,0:T(8,128)S(1)}, f32[2,2,3,8,256]{4,3,2,1,0:T(8,128)S(1)}, u32[]{:S(2)}, u32[]{:S(2)}) collective-permute-start(f32[2,2,3,8,256]{4,3,2,1,0:T(8,128)S(1)} %get-tuple-element.133), channel_id=1, source_target_pairs={{0,1},{1,2},{2,3},{3,0},{4,5},{5,6},{6,7},{7,4},{8,9},{9,10},{10,1... | collective-permute-start | bytes 294920 | tf_op jit(solution)/shard_map/ppermute | solution.py:605
  102.0 7.7 %collective-permute-done.16.before = f32[2,2,3,8,256]{4,3,2,1,0:T(8,128)S(1)} collective-permute-done((f32[2,2,3,8,256]{4,3,2,1,0:T(8,128)S(1)}, f32[2,2,3,8,256]{4,3,2,1,0:T(8,128)S(1)}, u32[]{:S(2)}, u32[]{:S(2)}) %collective-permute-start.16) | collective-permute-done | bytes 98336 | tf_op jit(solution)/shard_map/ppermute | solution.py:605
  109.9 5.0 %second_t.1 = (f32[2,2,2,8,32,256]{5,4,3,2,1,0:T(8,128)S(1)}, f32[2,2,2,32,256]{4,3,2,1,0:T(8,128)S(1)}) custom-call(s32[3]{0:T(128)S(1)} %pad_add_fusion.1.scal, f32[2,2,2,8,32,256]{5,4,3,2,1,0:T(8,128)S(1)} %get-tuple-element.130.x_ref, f32[2,2,2,8,32,256]{5,4,3,2,1,0:T(8,128)S(1)} %get-tuple-element.131.v_ref, ...), custom_call_target="tpu_custom_call" | custom-call | bytes 9412 | tf_op jit(solution)/shard_map/second_t/pallas_call | solution.py:346
  114.9 2.5 %collective-permute-start.19 = (f32[2,2,2,32,256]{4,3,2,1,0:T(8,128)S(1)}, f32[2,2,2,32,256]{4,3,2,1,0:T(8,128)S(1)}, u32[]{:S(2)}, u32[]{:S(2)}) collective-permute-start(f32[2,2,2,32,256]{4,3,2,1,0:T(8,128)S(1)} %get-tuple-element.140), channel_id=1, source_target_pairs={{0,4},{1,5},{2,6},{3,7},{4,0},{5,1},{6,2},{7,3},{8,12},{9,13},{10,... | collective-permute-start | bytes 786440 | tf_op jit(solution)/shard_map/ppermute | solution.py:375
  117.4 10.0 %collective-permute-done.18.refs_3_ = f32[2,2,2,2,32,256]{5,4,3,2,1,0:T(8,128)S(1)} collective-permute-done((f32[2,2,2,2,32,256]{5,4,3,2,1,0:T(8,128)S(1)}, f32[2,2,2,2,32,256]{5,4,3,2,1,0:T(8,128)S(1)}, u32[]{:S(2)}, u32[]{:S(2)}) %collective-permute-start.18) | collective-permute-done | bytes 524320 | tf_op jit(solution)/shard_map/ppermute | solution.py:382
  130.3 1.9 %collective-permute-start.20 = (f32[2,2,2,2,32,256]{5,4,3,2,1,0:T(8,128)S(1)}, f32[2,2,2,2,32,256]{5,4,3,2,1,0:T(8,128)S(1)}, u32[]{:S(2)}, u32[]{:S(2)}) collective-permute-start(f32[2,2,2,2,32,256]{5,4,3,2,1,0:T(8,128)S(1)} %get-tuple-element.141), channel_id=1, source_target_pairs={{0,3},{1,2},{2,1},{3,0},{4,7},{5,6},{6,5},{7,4},{8,11},{9,10},{10,... | collective-permute-start | bytes 1572872 | tf_op jit(solution)/shard_map/ppermute | solution.py:382
  132.2 2.1 %place.3.refs_2_ = f32[2,4,2,2,4,32,256]{6,5,4,3,2,1,0:T(8,128)} custom-call(s32[3]{0:T(128)S(1)} %pad_add_fusion.1.scal, f32[2,2,2,2,32,256]{5,4,3,2,1,0:T(8,128)S(1)} %get-tuple-element.144.refs_0_, f32[2,2,2,2,32,256]{5,4,3,2,1,0:T(8,128)S(1)} %collective-permute-done.14.refs_1_, f32[2,2,2,2,32,256]{5,4,3,2,1,0:T(8,128)S(1)} %collective-permute-done.15.refs_2_, ...), custom_call_target="tpu_custom_call" | custom-call | bytes 6656 | tf_op jit(solution)/shard_map/place/pallas_call | solution.py:346
  134.3 5.2 %collective-permute-done.21.refs_0_ = f32[2,2,2,2,32,256]{5,4,3,2,1,0:T(8,128)S(1)} collective-permute-done((f32[2,2,2,2,32,256]{5,4,3,2,1,0:T(8,128)S(1)}, f32[2,2,2,2,32,256]{5,4,3,2,1,0:T(8,128)S(1)}, u32[]{:S(2)}, u32[]{:S(2)}) %collective-permute-start.21) | collective-permute-done | bytes 524320 | tf_op jit(solution)/shard_map/ppermute | solution.py:382
  139.5 5.4 %collective-permute-done.22.refs_1_ = f32[2,2,2,2,32,256]{5,4,3,2,1,0:T(8,128)S(1)} collective-permute-done((f32[2,2,2,2,32,256]{5,4,3,2,1,0:T(8,128)S(1)}, f32[2,2,2,2,32,256]{5,4,3,2,1,0:T(8,128)S(1)}, u32[]{:S(2)}, u32[]{:S(2)}) %collective-permute-start.22) | collective-permute-done | bytes 524320 | tf_op jit(solution)/shard_map/ppermute | solution.py:382
  146.4 6.6 %collective-permute-done.20.refs_0_ = f32[2,2,2,2,32,256]{5,4,3,2,1,0:T(8,128)S(1)} collective-permute-done((f32[2,2,2,2,32,256]{5,4,3,2,1,0:T(8,128)S(1)}, f32[2,2,2,2,32,256]{5,4,3,2,1,0:T(8,128)S(1)}, u32[]{:S(2)}, u32[]{:S(2)}) %collective-permute-start.20) | collective-permute-done | bytes 524320 | tf_op jit(solution)/shard_map/ppermute | solution.py:382
  (77 shorter events, 24.6 us)
Async XLA Ops:
  0.0 13.4 %collective-permute-start.1 = (f32[2,3,32,64]{3,2,1,0:T(8,128)}, f32[2,3,32,64]{3,2,1,0:T(8,128)S(1)}, u32[]{:S(2)}, u32[]{:S(2)}) collective-permute-start(f32[2,3,32,64]{3,2,1,0:T(8,128)} %param.9), channel_id=1, source_target_pairs={{0,4},{1,5},{2,6},{3,7},{4,0},{5,1},{6,2},{7,3},{8,12},{9,13},{10,... | collective-permute-start | bytes 147464 | tf_op jit(solution)/shard_map/ppermute | solution.py:375
  7.5 43.0 %collective-permute-start.5 = (f32[2,2,2,2,32,256]{5,4,3,2,1,0:T(8,128)}, f32[2,2,2,2,32,256]{5,4,3,2,1,0:T(8,128)}, u32[]{:S(2)}, u32[]{:S(2)}) collective-permute-start(f32[2,2,2,2,32,256]{5,4,3,2,1,0:T(8,128)} %get-tuple-element.96), channel_id=1, source_target_pairs={{0,3},{1,2},{2,1},{3,0},{4,7},{5,6},{6,5},{7,4},{8,11},{9,10},{10,... | collective-permute-start | bytes 1572872 | tf_op jit(solution)/shard_map/ppermute | solution.py:382
  12.7 34.1 %collective-permute-start = (f32[2,11,32,256]{3,2,1,0:T(8,128)}, f32[2,11,32,256]{3,2,1,0:T(8,128)}, u32[]{:S(2)}, u32[]{:S(2)}) collective-permute-start(f32[2,11,32,256]{3,2,1,0:T(8,128)} %get-tuple-element.93), channel_id=1, source_target_pairs={{0,4},{1,5},{2,6},{3,7},{4,0},{5,1},{6,2},{7,3},{8,12},{9,13},{10,... | collective-permute-start | bytes 2162696 | tf_op jit(solution)/shard_map/ppermute | solution.py:375
  13.6 10.3 %collective-permute-start.4 = (f32[2,3,2,32,64]{4,3,2,1,0:T(8,128)S(1)}, f32[2,3,2,32,64]{4,3,2,1,0:T(8,128)S(1)}, u32[]{:S(2)}, u32[]{:S(2)}) collective-permute-start(f32[2,3,2,32,64]{4,3,2,1,0:T(8,128)S(1)} %maximum_select_fusion), channel_id=1, source_target_pairs={{0,8},{8,16},{16,24},{24,0},{1,9},{9,17},{17,25},{25,1},{2,10},{10... | collective-permute-start | bytes 294920 | tf_op jit(solution)/shard_map/ppermute | solution.py:432
  13.7 10.8 %collective-permute-start.3 = (f32[2,3,2,32,64]{4,3,2,1,0:T(8,128)S(1)}, f32[2,3,2,32,64]{4,3,2,1,0:T(8,128)}, u32[]{:S(2)}, u32[]{:S(2)}) collective-permute-start(f32[2,3,2,32,64]{4,3,2,1,0:T(8,128)S(1)} %maximum_select_fusion), channel_id=1, source_target_pairs={{0,16},{8,24},{16,0},{24,8},{1,17},{9,25},{17,1},{25,9},{2,18},{10... | collective-permute-start | bytes 294920 | tf_op jit(solution)/shard_map/ppermute | solution.py:432
  15.2 9.7 %collective-permute-start.2 = (f32[2,3,2,32,64]{4,3,2,1,0:T(8,128)S(1)}, f32[2,3,2,32,64]{4,3,2,1,0:T(8,128)}, u32[]{:S(2)}, u32[]{:S(2)}) collective-permute-start(f32[2,3,2,32,64]{4,3,2,1,0:T(8,128)S(1)} %maximum_select_fusion), channel_id=1, source_target_pairs={{0,24},{8,0},{16,8},{24,16},{1,25},{9,1},{17,9},{25,17},{2,26},{10... | collective-permute-start | bytes 294920 | tf_op jit(solution)/shard_map/ppermute | solution.py:432
  23.9 26.6 %collective-permute-start.6 = (f32[2,2,2,2,32,256]{5,4,3,2,1,0:T(8,128)}, f32[2,2,2,2,32,256]{5,4,3,2,1,0:T(8,128)}, u32[]{:S(2)}, u32[]{:S(2)}) collective-permute-start(f32[2,2,2,2,32,256]{5,4,3,2,1,0:T(8,128)} %get-tuple-element.97), channel_id=1, source_target_pairs={{0,1},{1,0},{2,3},{3,2},{4,5},{5,4},{6,7},{7,6},{8,9},{9,8},{10,11... | collective-permute-start | bytes 1572872 | tf_op jit(solution)/shard_map/ppermute | solution.py:382
  24.5 26.0 %collective-permute-start.7 = (f32[2,2,2,2,32,256]{5,4,3,2,1,0:T(8,128)}, f32[2,2,2,2,32,256]{5,4,3,2,1,0:T(8,128)}, u32[]{:S(2)}, u32[]{:S(2)}) collective-permute-start(f32[2,2,2,2,32,256]{5,4,3,2,1,0:T(8,128)} %get-tuple-element.98), channel_id=1, source_target_pairs={{0,2},{1,3},{2,0},{3,1},{4,6},{5,7},{6,4},{7,5},{8,10},{9,11},{10,... | collective-permute-start | bytes 1572872 | tf_op jit(solution)/shard_map/ppermute | solution.py:382
  46.8 19.4 %collective-permute-start.9 = (f32[2,2,2,2,32,256]{5,4,3,2,1,0:T(8,128)}, f32[2,2,2,2,32,256]{5,4,3,2,1,0:T(8,128)}, u32[]{:S(2)}, u32[]{:S(2)}) collective-permute-start(f32[2,2,2,2,32,256]{5,4,3,2,1,0:T(8,128)} %get-tuple-element.105), channel_id=1, source_target_pairs={{0,1},{1,0},{2,3},{3,2},{4,5},{5,4},{6,7},{7,6},{8,9},{9,8},{10,11... | collective-permute-start | bytes 1572872 | tf_op jit(solution)/shard_map/ppermute | solution.py:382
  47.3 20.8 %collective-permute-start.10 = (f32[2,2,2,2,32,256]{5,4,3,2,1,0:T(8,128)}, f32[2,2,2,2,32,256]{5,4,3,2,1,0:T(8,128)}, u32[]{:S(2)}, u32[]{:S(2)}) collective-permute-start(f32[2,2,2,2,32,256]{5,4,3,2,1,0:T(8,128)} %get-tuple-element.106), channel_id=1, source_target_pairs={{0,2},{1,3},{2,0},{3,1},{4,6},{5,7},{6,4},{7,5},{8,10},{9,11},{10,... | collective-permute-start | bytes 1572872 | tf_op jit(solution)/shard_map/ppermute | solution.py:382
  53.7 12.6 %collective-permute-start.8 = (f32[2,2,2,32,256]{4,3,2,1,0:T(8,128)S(1)}, f32[2,2,2,32,256]{4,3,2,1,0:T(8,128)S(1)}, u32[]{:S(2)}, u32[]{:S(2)}) collective-permute-start(f32[2,2,2,32,256]{4,3,2,1,0:T(8,128)S(1)} %get-tuple-element.104), channel_id=1, source_target_pairs={{0,4},{1,5},{2,6},{3,7},{4,0},{5,1},{6,2},{7,3},{8,12},{9,13},{10,... | collective-permute-start | bytes 786440 | tf_op jit(solution)/shard_map/ppermute | solution.py:375
  54.5 26.3 %collective-permute-start.11 = (f32[2,2,2,2,32,256]{5,4,3,2,1,0:T(8,128)S(1)}, f32[2,2,2,2,32,256]{5,4,3,2,1,0:T(8,128)S(1)}, u32[]{:S(2)}, u32[]{:S(2)}) collective-permute-start(f32[2,2,2,2,32,256]{5,4,3,2,1,0:T(8,128)S(1)} %copy-done.8), channel_id=1, source_target_pairs={{0,3},{1,2},{2,1},{3,0},{4,7},{5,6},{6,5},{7,4},{8,11},{9,10},{10,... | collective-permute-start | bytes 1572872 | tf_op jit(solution)/shard_map/ppermute | solution.py:382
  68.1 12.6 %copy-start.4 = (f32[2,2,2,2,32,256]{5,4,3,2,1,0:T(8,128)S(1)}, f32[2,2,2,2,32,256]{5,4,3,2,1,0:T(8,128)}, u32[]{:S(2)}) copy-start(f32[2,2,2,2,32,256]{5,4,3,2,1,0:T(8,128)} %copy-done.3) | copy-start | bytes 1572868
  69.4 14.4 %collective-permute-start.12 = (f32[2,2,2,32,256]{4,3,2,1,0:T(8,128)S(1)}, f32[2,2,2,32,256]{4,3,2,1,0:T(8,128)S(1)}, u32[]{:S(2)}, u32[]{:S(2)}) collective-permute-start(f32[2,2,2,32,256]{4,3,2,1,0:T(8,128)S(1)} %get-tuple-element.118), channel_id=1, source_target_pairs={{0,4},{1,5},{2,6},{3,7},{4,0},{5,1},{6,2},{7,3},{8,12},{9,13},{10,... | collective-permute-start | bytes 786440 | tf_op jit(solution)/shard_map/ppermute | solution.py:375
  85.0 13.1 %collective-permute-start.13 = (f32[2,2,2,32,256]{4,3,2,1,0:T(8,128)S(1)}, f32[2,2,2,32,256]{4,3,2,1,0:T(8,128)S(1)}, u32[]{:S(2)}, u32[]{:S(2)}) collective-permute-start(f32[2,2,2,32,256]{4,3,2,1,0:T(8,128)S(1)} %get-tuple-element.124), channel_id=1, source_target_pairs={{0,4},{1,5},{2,6},{3,7},{4,0},{5,1},{6,2},{7,3},{8,12},{9,13},{10,... | collective-permute-start | bytes 786440 | tf_op jit(solution)/shard_map/ppermute | solution.py:375
  86.7 23.1 %collective-permute-start.14 = (f32[2,2,2,2,32,256]{5,4,3,2,1,0:T(8,128)S(1)}, f32[2,2,2,2,32,256]{5,4,3,2,1,0:T(8,128)S(1)}, u32[]{:S(2)}, u32[]{:S(2)}) collective-permute-start(f32[2,2,2,2,32,256]{5,4,3,2,1,0:T(8,128)S(1)} %get-tuple-element.128), channel_id=1, source_target_pairs={{0,1},{1,0},{2,3},{3,2},{4,5},{5,4},{6,7},{7,6},{8,9},{9,8},{10,11... | collective-permute-start | bytes 1572872 | tf_op jit(solution)/shard_map/ppermute | solution.py:382
  88.4 21.4 %collective-permute-start.15 = (f32[2,2,2,2,32,256]{5,4,3,2,1,0:T(8,128)S(1)}, f32[2,2,2,2,32,256]{5,4,3,2,1,0:T(8,128)S(1)}, u32[]{:S(2)}, u32[]{:S(2)}) collective-permute-start(f32[2,2,2,2,32,256]{5,4,3,2,1,0:T(8,128)S(1)} %get-tuple-element.129), channel_id=1, source_target_pairs={{0,2},{1,3},{2,0},{3,1},{4,6},{5,7},{6,4},{7,5},{8,10},{9,11},{10,... | collective-permute-start | bytes 1572872 | tf_op jit(solution)/shard_map/ppermute | solution.py:382
  99.0 10.7 %collective-permute-start.16 = (f32[2,2,3,8,256]{4,3,2,1,0:T(8,128)S(1)}, f32[2,2,3,8,256]{4,3,2,1,0:T(8,128)S(1)}, u32[]{:S(2)}, u32[]{:S(2)}) collective-permute-start(f32[2,2,3,8,256]{4,3,2,1,0:T(8,128)S(1)} %get-tuple-element.133), channel_id=1, source_target_pairs={{0,1},{1,2},{2,3},{3,0},{4,5},{5,6},{6,7},{7,4},{8,9},{9,10},{10,1... | collective-permute-start | bytes 294920 | tf_op jit(solution)/shard_map/ppermute | solution.py:605
  102.0 7.7 %collective-permute-start.17 = (f32[2,2,3,8,256]{4,3,2,1,0:T(8,128)S(1)}, f32[2,2,3,8,256]{4,3,2,1,0:T(8,128)S(1)}, u32[]{:S(2)}, u32[]{:S(2)}) collective-permute-start(f32[2,2,3,8,256]{4,3,2,1,0:T(8,128)S(1)} %get-tuple-element.134), channel_id=1, source_target_pairs={{1,0},{2,1},{3,2},{0,3},{5,4},{6,5},{7,6},{4,7},{9,8},{10,9},{11,1... | collective-permute-start | bytes 294920 | tf_op jit(solution)/shard_map/ppermute | solution.py:606
  109.7 17.7 %collective-permute-start.18 = (f32[2,2,2,2,32,256]{5,4,3,2,1,0:T(8,128)S(1)}, f32[2,2,2,2,32,256]{5,4,3,2,1,0:T(8,128)S(1)}, u32[]{:S(2)}, u32[]{:S(2)}) collective-permute-start(f32[2,2,2,2,32,256]{5,4,3,2,1,0:T(8,128)S(1)} %get-tuple-element.138), channel_id=1, source_target_pairs={{0,3},{1,2},{2,1},{3,0},{4,7},{5,6},{6,5},{7,4},{8,11},{9,10},{10,... | collective-permute-start | bytes 1572872 | tf_op jit(solution)/shard_map/ppermute | solution.py:382
  114.9 12.6 %collective-permute-start.19 = (f32[2,2,2,32,256]{4,3,2,1,0:T(8,128)S(1)}, f32[2,2,2,32,256]{4,3,2,1,0:T(8,128)S(1)}, u32[]{:S(2)}, u32[]{:S(2)}) collective-permute-start(f32[2,2,2,32,256]{4,3,2,1,0:T(8,128)S(1)} %get-tuple-element.140), channel_id=1, source_target_pairs={{0,4},{1,5},{2,6},{3,7},{4,0},{5,1},{6,2},{7,3},{8,12},{9,13},{10,... | collective-permute-start | bytes 786440 | tf_op jit(solution)/shard_map/ppermute | solution.py:375
  128.7 10.8 %collective-permute-start.21 = (f32[2,2,2,2,32,256]{5,4,3,2,1,0:T(8,128)S(1)}, f32[2,2,2,2,32,256]{5,4,3,2,1,0:T(8,128)S(1)}, u32[]{:S(2)}, u32[]{:S(2)}) collective-permute-start(f32[2,2,2,2,32,256]{5,4,3,2,1,0:T(8,128)S(1)} %get-tuple-element.142), channel_id=1, source_target_pairs={{0,1},{1,0},{2,3},{3,2},{4,5},{5,4},{6,7},{7,6},{8,9},{9,8},{10,11... | collective-permute-start | bytes 1572872 | tf_op jit(solution)/shard_map/ppermute | solution.py:382
  130.0 14.9 %collective-permute-start.22 = (f32[2,2,2,2,32,256]{5,4,3,2,1,0:T(8,128)S(1)}, f32[2,2,2,2,32,256]{5,4,3,2,1,0:T(8,128)S(1)}, u32[]{:S(2)}, u32[]{:S(2)}) collective-permute-start(f32[2,2,2,2,32,256]{5,4,3,2,1,0:T(8,128)S(1)} %get-tuple-element.143), channel_id=1, source_target_pairs={{0,2},{1,3},{2,0},{3,1},{4,6},{5,7},{6,4},{7,5},{8,10},{9,11},{10,... | collective-permute-start | bytes 1572872 | tf_op jit(solution)/shard_map/ppermute | solution.py:382
  130.3 22.7 %collective-permute-start.20 = (f32[2,2,2,2,32,256]{5,4,3,2,1,0:T(8,128)S(1)}, f32[2,2,2,2,32,256]{5,4,3,2,1,0:T(8,128)S(1)}, u32[]{:S(2)}, u32[]{:S(2)}) collective-permute-start(f32[2,2,2,2,32,256]{5,4,3,2,1,0:T(8,128)S(1)} %get-tuple-element.141), channel_id=1, source_target_pairs={{0,3},{1,2},{2,1},{3,0},{4,7},{5,6},{6,5},{7,4},{8,11},{9,10},{10,... | collective-permute-start | bytes 1572872 | tf_op jit(solution)/shard_map/ppermute | solution.py:382
  (12 other events, 52.1 us)

commit v6 on v4

--- a/solution.py
+++ b/solution.py
@@ -329,7 +329,7 @@
 SPLIT_LIMIT = 40
 
 
-def call(kernel, name, scal, grid, inputs, outputs, scratch=(), aliases=None, limit=40, weight=1 / 1024):
+def call(kernel, name, scal, grid, inputs, outputs, scratch=(), aliases=None, limit=24, weight=1 / 1024):
     def spec(block, index):
         if block is None:
             return pl.BlockSpec(memory_space=pl.ANY)

time: 155 us -> 156 us (level)
  waiting for transfers between devices: 82.9 us -> 86.2 us
    ppermute x12, waiting for transfers between devices: 38.9 us -> 40.6 us  [cross(): lax.ppermute(values[part], 'slab', moved(part))]
  transfers between devices with their start and end apart: 23 -> 23, of which waited for: 10 -> 11; matrix products, arithmetic and copies ran while one was open for 1% -> 1% of each run, Pallas kernels for 20% -> 20%
where the time goes in v6:
time: 156 us
  waiting for transfers between devices  86.2 us (55%)
  Pallas kernels  35.1 us (22%)
  starting transfers between devices  29.4 us (19%)
  local copies, waits for them, and re-layouts  2.78 us (2%)
  other arithmetic  1.78 us (1%)
    ppermute x12, waiting for transfers between devices, cross(): lax.ppermute(values[part], 'slab', moved(part))  40.6 us
    ppermute x6, waiting for transfers between devices, swap(): return lax.ppermute(values, 'slab', partner)  37.8 us
    pallas_call x14, Pallas kernels, call(): pl.pallas_call(kernel, grid_spec=pltpu.PrefetchScalarGridSpec(num_scalar_...  35.1 us
    ppermute x12, starting transfers between devices, cross(): lax.ppermute(values[part], 'slab', moved(part))  13.8 us
    ppermute x6, starting transfers between devices, swap(): return lax.ppermute(values, 'slab', partner)  9.6 us
    ppermute x1, waiting for transfers between devices, per_device(): t_before = lax.ppermute(t_end, 'slab', to_next)  7.83 us
  transfers between devices with their start and end apart: 23, of which 11 were waited for; matrix products, arithmetic and copies ran while one was open for 1% of the time, Pallas kernels for 20%

profile of v6, /device:TPU:0, one launch (start us, length us, event | category | flops | bytes accessed | tf_op | source)
XLA Modules:
  0.0 155.6 jit_solution(10858939054065889556)
XLA Ops:
  0.0 4.0 %collective-permute-start.1 = (f32[2,3,32,64]{3,2,1,0:T(8,128)}, f32[2,3,32,64]{3,2,1,0:T(8,128)S(1)}, u32[]{:S(2)}, u32[]{:S(2)}) collective-permute-start(f32[2,3,32,64]{3,2,1,0:T(8,128)} %param.9), channel_id=1, source_target_pairs={{0,4},{1,5},{2,6},{3,7},{4,0},{5,1},{6,2},{7,3},{8,12},{9,13},{10,... | collective-permute-start | bytes 147464 | tf_op jit(solution)/shard_map/ppermute | solution.py:375
  4.1 3.4 %split.1 = (f32[2,2,2,2,32,256]{5,4,3,2,1,0:T(8,128)S(1)}, f32[2,2,2,2,32,256]{5,4,3,2,1,0:T(8,128)}, f32[2,2,2,2,32,256]{5,4,3,2,1,0:T(8,128)}, f32[2,2,2,2,32,256]{5,4,3,2,1,0:T(8,128)}) custom-call(s32[3]{0:T(128)S(1)} %pad_add_fusion.1.scal, f32[2,4,2,2,4,32,256]{6,5,4,3,2,1,0:T(8,128)} %bitcast.28), custom_call_target="tpu_custom_call" | custom-call | bytes 2048 | tf_op jit(solution)/shard_map/split/pallas_call | solution.py:346
  7.5 2.6 %collective-permute-start.5 = (f32[2,2,2,2,32,256]{5,4,3,2,1,0:T(8,128)}, f32[2,2,2,2,32,256]{5,4,3,2,1,0:T(8,128)}, u32[]{:S(2)}, u32[]{:S(2)}) collective-permute-start(f32[2,2,2,2,32,256]{5,4,3,2,1,0:T(8,128)} %get-tuple-element.96), channel_id=1, source_target_pairs={{0,3},{1,2},{2,1},{3,0},{4,7},{5,6},{6,5},{7,4},{8,11},{9,10},{10,... | collective-permute-start | bytes 1572872 | tf_op jit(solution)/shard_map/ppermute | solution.py:382
  16.2 2.2 %copy-done = f32[2,4,2,256,256]{4,3,2,1,0:T(8,128)S(1)} copy-done((f32[2,4,2,256,256]{4,3,2,1,0:T(8,128)S(1)}, f32[2,4,2,256,256]{4,3,2,1,0:T(8,128)}, u32[]{:S(2)}) %copy-start) | copy-done | bytes 4194328
  18.4 5.9 %advect.1 = (f32[2,2,2,2,32,256]{5,4,3,2,1,0:T(8,128)S(1)}, f32[2,2,2,2,32,256]{5,4,3,2,1,0:T(8,128)}, f32[2,2,2,2,32,256]{5,4,3,2,1,0:T(8,128)}, f32[2,2,2,2,32,256]{5,4,3,2,1,0:T(8,128)S(1)}) custom-call(s32[3]{0:T(128)S(1)} %pad_add_fusion.1.scal, f32[2,4,2,256,256]{4,3,2,1,0:T(8,128)S(1)} %copy-done, s32[2,256,256]{2,1,0:T(8,128)S(1)} %compare_select_fusion.cell_n, ...), custom_call_target="tpu_custom_call" | custom-call | bytes 7680 | tf_op jit(solution)/shard_map/advect/pallas_call | solution.py:346
  26.9 19.3 %collective-permute-done.got = f32[2,11,32,256]{3,2,1,0:T(8,128)} collective-permute-done((f32[2,11,32,256]{3,2,1,0:T(8,128)}, f32[2,11,32,256]{3,2,1,0:T(8,128)}, u32[]{:S(2)}, u32[]{:S(2)}) %collective-permute-start) | collective-permute-done | bytes 720928 | tf_op jit(solution)/shard_map/ppermute | solution.py:375
  46.7 3.1 %factor.1 = (f32[2,2,8,32,256]{4,3,2,1,0:T(8,128)S(1)}, f32[2,2,8,32,256]{4,3,2,1,0:T(8,128)S(1)}, f32[2,2,8,32,256]{4,3,2,1,0:T(8,128)S(1)}, f32[2,2,2,32,256]{4,3,2,1,0:T(8,128)S(1)}, f32[2,2,2,32,256]{4,3,2,1,0:T(8,128)S(1)}) custom-call(s32[3]{0:T(128)S(1)} %pad_add_fusion.1.scal, f32[2,16,32,256]{3,2,1,0:T(8,128)S(1)} %copy-done.1, ...), custom_call_target="tpu_custom_call" | custom-call | bytes 5632 | tf_op jit(solution)/shard_map/factor/pallas_call | solution.py:346
  50.2 3.2 %first.2 = (f32[2,2,2,8,32,256]{5,4,3,2,1,0:T(8,128)S(1)}, f32[2,2,2,32,256]{4,3,2,1,0:T(8,128)S(1)}) custom-call(s32[3]{0:T(128)S(1)} %pad_add_fusion.1.scal, f32[2,2,2,2,32,256]{5,4,3,2,1,0:T(8,128)S(1)} %get-tuple-element.95.refs_0_, f32[2,2,2,2,32,256]{5,4,3,2,1,0:T(8,128)} %collective-permute-done.5.refs_1_, ...), custom_call_target="tpu_custom_call" | custom-call | bytes 28311552 | tf_op jit(solution)/shard_map/first/pallas_call | solution.py:346
  54.0 2.2 %collective-permute-start.11 = (f32[2,2,2,2,32,256]{5,4,3,2,1,0:T(8,128)S(1)}, f32[2,2,2,2,32,256]{5,4,3,2,1,0:T(8,128)S(1)}, u32[]{:S(2)}, u32[]{:S(2)}) collective-permute-start(f32[2,2,2,2,32,256]{5,4,3,2,1,0:T(8,128)S(1)} %copy-done.9), channel_id=1, source_target_pairs={{0,3},{1,2},{2,1},{3,0},{4,7},{5,6},{6,5},{7,4},{8,11},{9,10},{10,... | collective-permute-start | bytes 1572872 | tf_op jit(solution)/shard_map/ppermute | solution.py:382
  56.2 10.1 %collective-permute-done.8.other = f32[2,2,2,32,256]{4,3,2,1,0:T(8,128)S(1)} collective-permute-done((f32[2,2,2,32,256]{4,3,2,1,0:T(8,128)S(1)}, f32[2,2,2,32,256]{4,3,2,1,0:T(8,128)S(1)}, u32[]{:S(2)}, u32[]{:S(2)}) %collective-permute-start.8) | collective-permute-done | bytes 262176 | tf_op jit(solution)/shard_map/ppermute | solution.py:375
  68.8 2.2 %collective-permute-start.12 = (f32[2,2,2,32,256]{4,3,2,1,0:T(8,128)S(1)}, f32[2,2,2,32,256]{4,3,2,1,0:T(8,128)S(1)}, u32[]{:S(2)}, u32[]{:S(2)}) collective-permute-start(f32[2,2,2,32,256]{4,3,2,1,0:T(8,128)S(1)} %get-tuple-element.118), channel_id=1, source_target_pairs={{0,4},{1,5},{2,6},{3,7},{4,0},{5,1},{6,2},{7,3},{8,12},{9,13},{10,... | collective-permute-start | bytes 786440 | tf_op jit(solution)/shard_map/ppermute | solution.py:375
  71.0 11.2 %collective-permute-done.11.refs_3_ = f32[2,2,2,2,32,256]{5,4,3,2,1,0:T(8,128)S(1)} collective-permute-done((f32[2,2,2,2,32,256]{5,4,3,2,1,0:T(8,128)S(1)}, f32[2,2,2,2,32,256]{5,4,3,2,1,0:T(8,128)S(1)}, u32[]{:S(2)}, u32[]{:S(2)}) %collective-permute-start.11) | collective-permute-done | bytes 524320 | tf_op jit(solution)/shard_map/ppermute | solution.py:382
  82.2 3.0 %first.3 = (f32[2,2,2,8,32,256]{5,4,3,2,1,0:T(8,128)S(1)}, f32[2,2,2,32,256]{4,3,2,1,0:T(8,128)S(1)}) custom-call(s32[3]{0:T(128)S(1)} %pad_add_fusion.1.scal, f32[2,2,2,2,32,256]{5,4,3,2,1,0:T(8,128)S(1)} %copy-done.5, f32[2,2,2,2,32,256]{5,4,3,2,1,0:T(8,128)} %collective-permute-done.9.refs_1_, f32[2,2,2,2,32,256]{5,4,3,2,1,0:T(8,128)} %collective-permute-done.10.refs_2_, ...), custom_call_target="tpu_custom_call" | custom-call | bytes 28311552 | tf_op jit(solution)/shard_map/first/pallas_call | solution.py:346
  88.4 2.3 %collective-permute-start.15 = (f32[2,2,2,2,32,256]{5,4,3,2,1,0:T(8,128)S(1)}, f32[2,2,2,2,32,256]{5,4,3,2,1,0:T(8,128)S(1)}, u32[]{:S(2)}, u32[]{:S(2)}) collective-permute-start(f32[2,2,2,2,32,256]{5,4,3,2,1,0:T(8,128)S(1)} %get-tuple-element.129), channel_id=1, source_target_pairs={{0,2},{1,3},{2,0},{3,1},{4,6},{5,7},{6,4},{7,5},{8,10},{9,11},{10,... | collective-permute-start | bytes 1572872 | tf_op jit(solution)/shard_map/ppermute | solution.py:382
  90.7 8.3 %collective-permute-done.13.other = f32[2,2,2,32,256]{4,3,2,1,0:T(8,128)S(1)} collective-permute-done((f32[2,2,2,32,256]{4,3,2,1,0:T(8,128)S(1)}, f32[2,2,2,32,256]{4,3,2,1,0:T(8,128)S(1)}, u32[]{:S(2)}, u32[]{:S(2)}) %collective-permute-start.13) | collective-permute-done | bytes 262176 | tf_op jit(solution)/shard_map/ppermute | solution.py:375
  100.0 2.4 %collective-permute-start.16 = (f32[2,2,3,8,256]{4,3,2,1,0:T(8,128)S(1)}, f32[2,2,3,8,256]{4,3,2,1,0:T(8,128)S(1)}, u32[]{:S(2)}, u32[]{:S(2)}) collective-permute-start(f32[2,2,3,8,256]{4,3,2,1,0:T(8,128)S(1)} %get-tuple-element.133), channel_id=1, source_target_pairs={{0,1},{1,2},{2,3},{3,0},{4,5},{5,6},{6,7},{7,4},{8,9},{9,10},{10,1... | collective-permute-start | bytes 294920 | tf_op jit(solution)/shard_map/ppermute | solution.py:605
  103.0 7.8 %collective-permute-done.16.before = f32[2,2,3,8,256]{4,3,2,1,0:T(8,128)S(1)} collective-permute-done((f32[2,2,3,8,256]{4,3,2,1,0:T(8,128)S(1)}, f32[2,2,3,8,256]{4,3,2,1,0:T(8,128)S(1)}, u32[]{:S(2)}, u32[]{:S(2)}) %collective-permute-start.16) | collective-permute-done | bytes 98336 | tf_op jit(solution)/shard_map/ppermute | solution.py:605
  111.0 5.0 %second_t.1 = (f32[2,2,2,8,32,256]{5,4,3,2,1,0:T(8,128)S(1)}, f32[2,2,2,32,256]{4,3,2,1,0:T(8,128)S(1)}) custom-call(s32[3]{0:T(128)S(1)} %pad_add_fusion.1.scal, f32[2,2,2,8,32,256]{5,4,3,2,1,0:T(8,128)S(1)} %get-tuple-element.130.x_ref, f32[2,2,2,8,32,256]{5,4,3,2,1,0:T(8,128)S(1)} %get-tuple-element.131.v_ref, ...), custom_call_target="tpu_custom_call" | custom-call | bytes 9412 | tf_op jit(solution)/shard_map/second_t/pallas_call | solution.py:346
  118.0 11.7 %collective-permute-done.18.refs_3_ = f32[2,2,2,2,32,256]{5,4,3,2,1,0:T(8,128)S(1)} collective-permute-done((f32[2,2,2,2,32,256]{5,4,3,2,1,0:T(8,128)S(1)}, f32[2,2,2,2,32,256]{5,4,3,2,1,0:T(8,128)S(1)}, u32[]{:S(2)}, u32[]{:S(2)}) %collective-permute-start.18) | collective-permute-done | bytes 524320 | tf_op jit(solution)/shard_map/ppermute | solution.py:382
  131.4 3.1 %collective-permute-start.20 = (f32[2,2,2,2,32,256]{5,4,3,2,1,0:T(8,128)S(1)}, f32[2,2,2,2,32,256]{5,4,3,2,1,0:T(8,128)S(1)}, u32[]{:S(2)}, u32[]{:S(2)}) collective-permute-start(f32[2,2,2,2,32,256]{5,4,3,2,1,0:T(8,128)S(1)} %get-tuple-element.141), channel_id=1, source_target_pairs={{0,3},{1,2},{2,1},{3,0},{4,7},{5,6},{6,5},{7,4},{8,11},{9,10},{10,... | collective-permute-start | bytes 1572872 | tf_op jit(solution)/shard_map/ppermute | solution.py:382
  134.5 2.1 %place.3.refs_2_ = f32[2,4,2,2,4,32,256]{6,5,4,3,2,1,0:T(8,128)} custom-call(s32[3]{0:T(128)S(1)} %pad_add_fusion.1.scal, f32[2,2,2,2,32,256]{5,4,3,2,1,0:T(8,128)S(1)} %get-tuple-element.144.refs_0_, f32[2,2,2,2,32,256]{5,4,3,2,1,0:T(8,128)S(1)} %collective-permute-done.14.refs_1_, f32[2,2,2,2,32,256]{5,4,3,2,1,0:T(8,128)S(1)} %collective-permute-done.15.refs_2_, ...), custom_call_target="tpu_custom_call" | custom-call | bytes 6656 | tf_op jit(solution)/shard_map/place/pallas_call | solution.py:346
  136.6 6.8 %collective-permute-done.21.refs_0_ = f32[2,2,2,2,32,256]{5,4,3,2,1,0:T(8,128)S(1)} collective-permute-done((f32[2,2,2,2,32,256]{5,4,3,2,1,0:T(8,128)S(1)}, f32[2,2,2,2,32,256]{5,4,3,2,1,0:T(8,128)S(1)}, u32[]{:S(2)}, u32[]{:S(2)}) %collective-permute-start.21) | collective-permute-done | bytes 524320 | tf_op jit(solution)/shard_map/ppermute | solution.py:382
  143.4 2.9 %collective-permute-done.22.refs_1_ = f32[2,2,2,2,32,256]{5,4,3,2,1,0:T(8,128)S(1)} collective-permute-done((f32[2,2,2,2,32,256]{5,4,3,2,1,0:T(8,128)S(1)}, f32[2,2,2,2,32,256]{5,4,3,2,1,0:T(8,128)S(1)}, u32[]{:S(2)}, u32[]{:S(2)}) %collective-permute-start.22) | collective-permute-done | bytes 524320 | tf_op jit(solution)/shard_map/ppermute | solution.py:382
  147.8 6.4 %collective-permute-done.20.refs_0_ = f32[2,2,2,2,32,256]{5,4,3,2,1,0:T(8,128)S(1)} collective-permute-done((f32[2,2,2,2,32,256]{5,4,3,2,1,0:T(8,128)S(1)}, f32[2,2,2,2,32,256]{5,4,3,2,1,0:T(8,128)S(1)}, u32[]{:S(2)}, u32[]{:S(2)}) %collective-permute-start.20) | collective-permute-done | bytes 524320 | tf_op jit(solution)/shard_map/ppermute | solution.py:382
  (79 shorter events, 24.0 us)
Async XLA Ops:
  0.0 12.8 %collective-permute-start.1 = (f32[2,3,32,64]{3,2,1,0:T(8,128)}, f32[2,3,32,64]{3,2,1,0:T(8,128)S(1)}, u32[]{:S(2)}, u32[]{:S(2)}) collective-permute-start(f32[2,3,32,64]{3,2,1,0:T(8,128)} %param.9), channel_id=1, source_target_pairs={{0,4},{1,5},{2,6},{3,7},{4,0},{5,1},{6,2},{7,3},{8,12},{9,13},{10,... | collective-permute-start | bytes 147464 | tf_op jit(solution)/shard_map/ppermute | solution.py:375
  7.5 42.3 %collective-permute-start.5 = (f32[2,2,2,2,32,256]{5,4,3,2,1,0:T(8,128)}, f32[2,2,2,2,32,256]{5,4,3,2,1,0:T(8,128)}, u32[]{:S(2)}, u32[]{:S(2)}) collective-permute-start(f32[2,2,2,2,32,256]{5,4,3,2,1,0:T(8,128)} %get-tuple-element.96), channel_id=1, source_target_pairs={{0,3},{1,2},{2,1},{3,0},{4,7},{5,6},{6,5},{7,4},{8,11},{9,10},{10,... | collective-permute-start | bytes 1572872 | tf_op jit(solution)/shard_map/ppermute | solution.py:382
  12.1 34.1 %collective-permute-start = (f32[2,11,32,256]{3,2,1,0:T(8,128)}, f32[2,11,32,256]{3,2,1,0:T(8,128)}, u32[]{:S(2)}, u32[]{:S(2)}) collective-permute-start(f32[2,11,32,256]{3,2,1,0:T(8,128)} %get-tuple-element.93), channel_id=1, source_target_pairs={{0,4},{1,5},{2,6},{3,7},{4,0},{5,1},{6,2},{7,3},{8,12},{9,13},{10,... | collective-permute-start | bytes 2162696 | tf_op jit(solution)/shard_map/ppermute | solution.py:375
  13.0 11.3 %collective-permute-start.4 = (f32[2,3,2,32,64]{4,3,2,1,0:T(8,128)S(1)}, f32[2,3,2,32,64]{4,3,2,1,0:T(8,128)}, u32[]{:S(2)}, u32[]{:S(2)}) collective-permute-start(f32[2,3,2,32,64]{4,3,2,1,0:T(8,128)S(1)} %maximum_select_fusion), channel_id=1, source_target_pairs={{0,8},{8,16},{16,24},{24,0},{1,9},{9,17},{17,25},{25,1},{2,10},{10... | collective-permute-start | bytes 294920 | tf_op jit(solution)/shard_map/ppermute | solution.py:432
  13.1 11.8 %collective-permute-start.3 = (f32[2,3,2,32,64]{4,3,2,1,0:T(8,128)S(1)}, f32[2,3,2,32,64]{4,3,2,1,0:T(8,128)}, u32[]{:S(2)}, u32[]{:S(2)}) collective-permute-start(f32[2,3,2,32,64]{4,3,2,1,0:T(8,128)S(1)} %maximum_select_fusion), channel_id=1, source_target_pairs={{0,16},{8,24},{16,0},{24,8},{1,17},{9,25},{17,1},{25,9},{2,18},{10... | collective-permute-start | bytes 294920 | tf_op jit(solution)/shard_map/ppermute | solution.py:432
  14.7 10.7 %collective-permute-start.2 = (f32[2,3,2,32,64]{4,3,2,1,0:T(8,128)S(1)}, f32[2,3,2,32,64]{4,3,2,1,0:T(8,128)}, u32[]{:S(2)}, u32[]{:S(2)}) collective-permute-start(f32[2,3,2,32,64]{4,3,2,1,0:T(8,128)S(1)} %maximum_select_fusion), channel_id=1, source_target_pairs={{0,24},{8,0},{16,8},{24,16},{1,25},{9,1},{17,9},{25,17},{2,26},{10... | collective-permute-start | bytes 294920 | tf_op jit(solution)/shard_map/ppermute | solution.py:432
  24.3 25.5 %collective-permute-start.6 = (f32[2,2,2,2,32,256]{5,4,3,2,1,0:T(8,128)}, f32[2,2,2,2,32,256]{5,4,3,2,1,0:T(8,128)}, u32[]{:S(2)}, u32[]{:S(2)}) collective-permute-start(f32[2,2,2,2,32,256]{5,4,3,2,1,0:T(8,128)} %get-tuple-element.97), channel_id=1, source_target_pairs={{0,1},{1,0},{2,3},{3,2},{4,5},{5,4},{6,7},{7,6},{8,9},{9,8},{10,11... | collective-permute-start | bytes 1572872 | tf_op jit(solution)/shard_map/ppermute | solution.py:382
  24.9 25.3 %collective-permute-start.7 = (f32[2,2,2,2,32,256]{5,4,3,2,1,0:T(8,128)}, f32[2,2,2,2,32,256]{5,4,3,2,1,0:T(8,128)}, u32[]{:S(2)}, u32[]{:S(2)}) collective-permute-start(f32[2,2,2,2,32,256]{5,4,3,2,1,0:T(8,128)} %get-tuple-element.98), channel_id=1, source_target_pairs={{0,2},{1,3},{2,0},{3,1},{4,6},{5,7},{6,4},{7,5},{8,10},{9,11},{10,... | collective-permute-start | bytes 1572872 | tf_op jit(solution)/shard_map/ppermute | solution.py:382
  46.2 20.1 %collective-permute-start.9 = (f32[2,2,2,2,32,256]{5,4,3,2,1,0:T(8,128)}, f32[2,2,2,2,32,256]{5,4,3,2,1,0:T(8,128)}, u32[]{:S(2)}, u32[]{:S(2)}) collective-permute-start(f32[2,2,2,2,32,256]{5,4,3,2,1,0:T(8,128)} %get-tuple-element.105), channel_id=1, source_target_pairs={{0,1},{1,0},{2,3},{3,2},{4,5},{5,4},{6,7},{7,6},{8,9},{9,8},{10,11... | collective-permute-start | bytes 1572872 | tf_op jit(solution)/shard_map/ppermute | solution.py:382
  46.7 20.8 %collective-permute-start.10 = (f32[2,2,2,2,32,256]{5,4,3,2,1,0:T(8,128)}, f32[2,2,2,2,32,256]{5,4,3,2,1,0:T(8,128)}, u32[]{:S(2)}, u32[]{:S(2)}) collective-permute-start(f32[2,2,2,2,32,256]{5,4,3,2,1,0:T(8,128)} %get-tuple-element.106), channel_id=1, source_target_pairs={{0,2},{1,3},{2,0},{3,1},{4,6},{5,7},{6,4},{7,5},{8,10},{9,11},{10,... | collective-permute-start | bytes 1572872 | tf_op jit(solution)/shard_map/ppermute | solution.py:382
  53.4 12.9 %collective-permute-start.8 = (f32[2,2,2,32,256]{4,3,2,1,0:T(8,128)S(1)}, f32[2,2,2,32,256]{4,3,2,1,0:T(8,128)S(1)}, u32[]{:S(2)}, u32[]{:S(2)}) collective-permute-start(f32[2,2,2,32,256]{4,3,2,1,0:T(8,128)S(1)} %get-tuple-element.104), channel_id=1, source_target_pairs={{0,4},{1,5},{2,6},{3,7},{4,0},{5,1},{6,2},{7,3},{8,12},{9,13},{10,... | collective-permute-start | bytes 786440 | tf_op jit(solution)/shard_map/ppermute | solution.py:375
  54.0 28.2 %collective-permute-start.11 = (f32[2,2,2,2,32,256]{5,4,3,2,1,0:T(8,128)S(1)}, f32[2,2,2,2,32,256]{5,4,3,2,1,0:T(8,128)S(1)}, u32[]{:S(2)}, u32[]{:S(2)}) collective-permute-start(f32[2,2,2,2,32,256]{5,4,3,2,1,0:T(8,128)S(1)} %copy-done.9), channel_id=1, source_target_pairs={{0,3},{1,2},{2,1},{3,0},{4,7},{5,6},{6,5},{7,4},{8,11},{9,10},{10,... | collective-permute-start | bytes 1572872 | tf_op jit(solution)/shard_map/ppermute | solution.py:382
  67.5 14.7 %copy-start.5 = (f32[2,2,2,2,32,256]{5,4,3,2,1,0:T(8,128)S(1)}, f32[2,2,2,2,32,256]{5,4,3,2,1,0:T(8,128)}, u32[]{:S(2)}) copy-start(f32[2,2,2,2,32,256]{5,4,3,2,1,0:T(8,128)} %copy-done.4) | copy-start | bytes 1572868
  68.8 16.5 %collective-permute-start.12 = (f32[2,2,2,32,256]{4,3,2,1,0:T(8,128)S(1)}, f32[2,2,2,32,256]{4,3,2,1,0:T(8,128)S(1)}, u32[]{:S(2)}, u32[]{:S(2)}) collective-permute-start(f32[2,2,2,32,256]{4,3,2,1,0:T(8,128)S(1)} %get-tuple-element.118), channel_id=1, source_target_pairs={{0,4},{1,5},{2,6},{3,7},{4,0},{5,1},{6,2},{7,3},{8,12},{9,13},{10,... | collective-permute-start | bytes 786440 | tf_op jit(solution)/shard_map/ppermute | solution.py:375
  86.4 12.6 %collective-permute-start.13 = (f32[2,2,2,32,256]{4,3,2,1,0:T(8,128)S(1)}, f32[2,2,2,32,256]{4,3,2,1,0:T(8,128)S(1)}, u32[]{:S(2)}, u32[]{:S(2)}) collective-permute-start(f32[2,2,2,32,256]{4,3,2,1,0:T(8,128)S(1)} %get-tuple-element.124), channel_id=1, source_target_pairs={{0,4},{1,5},{2,6},{3,7},{4,0},{5,1},{6,2},{7,3},{8,12},{9,13},{10,... | collective-permute-start | bytes 786440 | tf_op jit(solution)/shard_map/ppermute | solution.py:375
  86.7 24.2 %collective-permute-start.14 = (f32[2,2,2,2,32,256]{5,4,3,2,1,0:T(8,128)S(1)}, f32[2,2,2,2,32,256]{5,4,3,2,1,0:T(8,128)S(1)}, u32[]{:S(2)}, u32[]{:S(2)}) collective-permute-start(f32[2,2,2,2,32,256]{5,4,3,2,1,0:T(8,128)S(1)} %get-tuple-element.128), channel_id=1, source_target_pairs={{0,1},{1,0},{2,3},{3,2},{4,5},{5,4},{6,7},{7,6},{8,9},{9,8},{10,11... | collective-permute-start | bytes 1572872 | tf_op jit(solution)/shard_map/ppermute | solution.py:382
  88.4 22.5 %collective-permute-start.15 = (f32[2,2,2,2,32,256]{5,4,3,2,1,0:T(8,128)S(1)}, f32[2,2,2,2,32,256]{5,4,3,2,1,0:T(8,128)S(1)}, u32[]{:S(2)}, u32[]{:S(2)}) collective-permute-start(f32[2,2,2,2,32,256]{5,4,3,2,1,0:T(8,128)S(1)} %get-tuple-element.129), channel_id=1, source_target_pairs={{0,2},{1,3},{2,0},{3,1},{4,6},{5,7},{6,4},{7,5},{8,10},{9,11},{10,... | collective-permute-start | bytes 1572872 | tf_op jit(solution)/shard_map/ppermute | solution.py:382
  100.0 10.8 %collective-permute-start.16 = (f32[2,2,3,8,256]{4,3,2,1,0:T(8,128)S(1)}, f32[2,2,3,8,256]{4,3,2,1,0:T(8,128)S(1)}, u32[]{:S(2)}, u32[]{:S(2)}) collective-permute-start(f32[2,2,3,8,256]{4,3,2,1,0:T(8,128)S(1)} %get-tuple-element.133), channel_id=1, source_target_pairs={{0,1},{1,2},{2,3},{3,0},{4,5},{5,6},{6,7},{7,4},{8,9},{9,10},{10,1... | collective-permute-start | bytes 294920 | tf_op jit(solution)/shard_map/ppermute | solution.py:605
  102.4 8.4 %collective-permute-start.17 = (f32[2,2,3,8,256]{4,3,2,1,0:T(8,128)S(1)}, f32[2,2,3,8,256]{4,3,2,1,0:T(8,128)S(1)}, u32[]{:S(2)}, u32[]{:S(2)}) collective-permute-start(f32[2,2,3,8,256]{4,3,2,1,0:T(8,128)S(1)} %get-tuple-element.134), channel_id=1, source_target_pairs={{1,0},{2,1},{3,2},{0,3},{5,4},{6,5},{7,6},{4,7},{9,8},{10,9},{11,1... | collective-permute-start | bytes 294920 | tf_op jit(solution)/shard_map/ppermute | solution.py:606
  110.8 18.9 %collective-permute-start.18 = (f32[2,2,2,2,32,256]{5,4,3,2,1,0:T(8,128)S(1)}, f32[2,2,2,2,32,256]{5,4,3,2,1,0:T(8,128)S(1)}, u32[]{:S(2)}, u32[]{:S(2)}) collective-permute-start(f32[2,2,2,2,32,256]{5,4,3,2,1,0:T(8,128)S(1)} %get-tuple-element.138), channel_id=1, source_target_pairs={{0,3},{1,2},{2,1},{3,0},{4,7},{5,6},{6,5},{7,4},{8,11},{9,10},{10,... | collective-permute-start | bytes 1572872 | tf_op jit(solution)/shard_map/ppermute | solution.py:382
  116.0 13.7 %collective-permute-start.19 = (f32[2,2,2,32,256]{4,3,2,1,0:T(8,128)S(1)}, f32[2,2,2,32,256]{4,3,2,1,0:T(8,128)S(1)}, u32[]{:S(2)}, u32[]{:S(2)}) collective-permute-start(f32[2,2,2,32,256]{4,3,2,1,0:T(8,128)S(1)} %get-tuple-element.140), channel_id=1, source_target_pairs={{0,4},{1,5},{2,6},{3,7},{4,0},{5,1},{6,2},{7,3},{8,12},{9,13},{10,... | collective-permute-start | bytes 786440 | tf_op jit(solution)/shard_map/ppermute | solution.py:375
  130.9 12.4 %collective-permute-start.21 = (f32[2,2,2,2,32,256]{5,4,3,2,1,0:T(8,128)S(1)}, f32[2,2,2,2,32,256]{5,4,3,2,1,0:T(8,128)S(1)}, u32[]{:S(2)}, u32[]{:S(2)}) collective-permute-start(f32[2,2,2,2,32,256]{5,4,3,2,1,0:T(8,128)S(1)} %get-tuple-element.142), channel_id=1, source_target_pairs={{0,1},{1,0},{2,3},{3,2},{4,5},{5,4},{6,7},{7,6},{8,9},{9,8},{10,11... | collective-permute-start | bytes 1572872 | tf_op jit(solution)/shard_map/ppermute | solution.py:382
  131.4 14.9 %collective-permute-start.22 = (f32[2,2,2,2,32,256]{5,4,3,2,1,0:T(8,128)S(1)}, f32[2,2,2,2,32,256]{5,4,3,2,1,0:T(8,128)S(1)}, u32[]{:S(2)}, u32[]{:S(2)}) collective-permute-start(f32[2,2,2,2,32,256]{5,4,3,2,1,0:T(8,128)S(1)} %get-tuple-element.143), channel_id=1, source_target_pairs={{0,2},{1,3},{2,0},{3,1},{4,6},{5,7},{6,4},{7,5},{8,10},{9,11},{10,... | collective-permute-start | bytes 1572872 | tf_op jit(solution)/shard_map/ppermute | solution.py:382
  131.4 22.8 %collective-permute-start.20 = (f32[2,2,2,2,32,256]{5,4,3,2,1,0:T(8,128)S(1)}, f32[2,2,2,2,32,256]{5,4,3,2,1,0:T(8,128)S(1)}, u32[]{:S(2)}, u32[]{:S(2)}) collective-permute-start(f32[2,2,2,2,32,256]{5,4,3,2,1,0:T(8,128)S(1)} %get-tuple-element.141), channel_id=1, source_target_pairs={{0,3},{1,2},{2,1},{3,0},{4,7},{5,6},{6,5},{7,4},{8,11},{9,10},{10,... | collective-permute-start | bytes 1572872 | tf_op jit(solution)/shard_map/ppermute | solution.py:382
  (13 other events, 54.1 us)
